TPU v7x, 128 devices: a whole 4x4x4 slice. The times are simulated.
128 devices in a mesh: gx: 8 (over x_hi, z), gy: 16 (over y, x_lo, core).
Axes of the slice: x: 4 (x_hi: 2, x_lo: 2; x = x_hi * 2 + x_lo), y: 4, z: 4, core: 2. Of those that a mesh axis runs over, the one named last changes fastest.
Arguments:
- neutral_wind: float32 [2, 128, 512, 128], P(None, 'gx', 'gy'), may hold values from -6 to 6
- forcing: float32 [2, 128, 512, 128], P(None, 'gx', 'gy'), may hold values from -3 to 3
- ion_density: float32 [2, 16384, 512], P(None, ('gx', 'gy')), may hold values from 0.5 to 2
- inverse: bfloat16 [8, 2, 512, 512], P('gx'), may hold values from -0.25 to 0.25
- drift_fraction: float32 [16384], P(('gx', 'gy')), may hold values from 0.1 to 0.4
- viscosity: float32 [128], replicated, may hold values from 0.02 to 0.15
- coupling: float32 [2, 2], replicated, may hold values from 0.2 to 0.8
- drag_rate: float32 [2], replicated, may hold values from 0.5 to 1.5
- outgoing_column: int32 [128, 128, 256], P(('gx', 'gy')), may hold values from 0 to 511
- send_level: int32 [128, 128, 256], P(('gx', 'gy')), may hold values from 0 to 127
- recv_tube: int32 [128, 128, 256], P(('gx', 'gy')), may hold values from 0 to 127
- recv_point: int32 [128, 128, 256], P(('gx', 'gy')), may hold values from 0 to 511
- recv_weight: float32 [128, 128, 256], P(('gx', 'gy')), may hold values from 0.2 to 1
- pair_count: int32 [128, 128], replicated, may hold values from 64 to 256, as said below
Outputs:
- wind_out: float32 [2, 128, 512, 128], P(None, 'gx', 'gy')
- ion_out: float32 [2, 16384, 512], P(None, ('gx', 'gy'))
Inputs may be any that keep to these rules, and one draw needn't show every extreme that they name: `pair_count`: every entry is at most 256; in every draw some destination device receives exactly 256 live crossings from every source device, and a few destinations receive far more than the mean.
All inputs are finite; a program needn't handle non-finite values.
Results may differ from a plain program's by a relative error of at most 0.0003.
The roundings to bfloat16 on the way count: a program that leaves them out, or rounds other values in their place, can miss the bound.
Values sent between devices are 32-bit elements; how exact they have to be, the bound alone decides.
No kernel may reach another device: no remote copies, remote signals or barrier semaphores. Data moves between devices by JAX's collectives and lax.ppermute only.
A program may use at most 128 MiB of HBM per device.

v0:
```python
import jax
import jax.numpy as jnp
from jax import lax
from jax.sharding import PartitionSpec as P

neutral_step = 0.4
ion_factor = 0.5


def extended(array, sides, width):
    edges = {}
    for axis, dim in sides:
        peers, length = (lax.axis_size(axis), array.shape[dim])
        up = [(i, (i + 1) % peers) for i in range(peers - 1)]
        last = lax.slice_in_dim(array, length - width, length, axis=dim)
        initial = lax.slice_in_dim(array, 0, width, axis=dim)
        edges[dim] = (
            lax.ppermute(last, axis, up),
            lax.ppermute(initial, axis, [(b, a) for a, b in up]),
        )
    done = []
    for _, dim in sides:
        low, high = edges[dim]
        around = [(width, width) if d in done else (0, 0) for d in range(array.ndim)]
        array = jnp.concatenate([jnp.pad(low, around), array, jnp.pad(high, around)], axis=dim)
        done.append(dim)
    return array


def shifted(block, axis, distance):
    devices = range(lax.axis_size(axis))
    route = [(i - distance, i) for i in devices if i - distance in devices]
    return lax.ppermute(block, axis, route)


def send_winds(values):
    return lax.all_to_all(values, ("gx", "gy"), split_axis=1, concat_axis=1, tiled=True)


def send_drag(values):
    return lax.all_to_all(values, ("gx", "gy"), split_axis=1, concat_axis=1, tiled=True)


def tendency(wind_field, viscous, drag_cells, forcing):
    padded = extended(wind_field, (("gx", 1), ("gy", 2)), 1)
    beside = padded[:, 2:, 1:-1, :] + padded[:, :-2, 1:-1, :]
    beside = beside + padded[:, 1:-1, 2:, :] + padded[:, 1:-1, :-2, :]
    stacked = jnp.pad(wind_field, ((0, 0), (0, 0), (0, 0), (1, 1)))
    beside = beside + stacked[..., 2:] + stacked[..., :-2]
    return viscous * (beside - 6.0 * wind_field) + drag_cells + forcing


def ion_update(ion_state, tube_winds, bundle_reverse_order, coupling, drift_fraction):
    growth = coupling[:, 0, None, None] * tube_winds[0] + coupling[:, 1, None, None] * tube_winds[1]
    right_side = ion_state + ion_factor * ion_state * growth
    half_step_forcing = right_side.astype(jnp.bfloat16)
    mixing = jnp.einsum(
        "jwe,jex->jwx", half_step_forcing, bundle_reverse_order, preferred_element_type=jnp.float32
    )
    smoothed_field = right_side + mixing
    outflow = drift_fraction[None, :, None] * smoothed_field
    upstream = shifted(outflow[:, -1:, :], "gy", 1)
    inflow = jnp.concatenate([upstream, outflow[:, :-1, :]], axis=1)
    return smoothed_field - outflow + inflow


def per_device(
    neutral_wind,
    forcing,
    ion_density,
    inverse,
    drift_fraction,
    viscosity,
    coupling,
    drag_rate,
    outgoing_column,
    send_level,
    recv_tube,
    recv_point,
    recv_weight,
    pair_count,
):
    device_count = lax.axis_size("gx") * lax.axis_size("gy")
    own_index = lax.axis_index(("gx", "gy"))
    vertical_level_count = neutral_wind.shape[3]
    point_count = ion_density.shape[2]
    cell_list = outgoing_column[0] * vertical_level_count + send_level[0]
    slot_list = (recv_tube[0] * point_count + recv_point[0]).reshape(-1)
    capacity = cell_list.shape[1]
    position = lax.broadcasted_iota(jnp.int32, (device_count, capacity), 1)
    incoming = lax.dynamic_slice_in_dim(pair_count, own_index, 1, 1)
    pair_gain = recv_weight[0] * (position < incoming).astype(jnp.float32)
    viscous = viscosity[None, None, None, :]
    bundle_reverse_order = inverse[0]
    tube_shape = ion_density.shape
    field_shape = neutral_wind.shape

    def section(wind_field, ion_state):
        flattened = wind_field.reshape(2, -1)
        values = flattened[:, cell_list]
        arrived = send_winds(values)
        contribution = (arrived * pair_gain[None]).reshape(2, -1)
        tube_winds = (
            jnp.zeros((2, tube_shape[1] * tube_shape[2]), jnp.float32)
            .at[:, slot_list]
            .add(contribution)
        )
        tube_winds = tube_winds.reshape(tube_shape)
        updated = ion_update(ion_state, tube_winds, bundle_reverse_order, coupling, drift_fraction)
        drag_force = -(drag_rate[0] * updated[0] + drag_rate[1] * updated[1])[None] * tube_winds
        selected_entries = (
            drag_force.reshape(2, -1)[:, slot_list].reshape(2, device_count, capacity)
            * pair_gain[None]
        )
        returned = send_drag(selected_entries)
        gathered_sum = (
            jnp.zeros((2, flattened.shape[1]), jnp.float32)
            .at[:, cell_list.reshape(-1)]
            .add(returned.reshape(2, -1))
        )
        drag_cells = gathered_sum.reshape(field_shape)
        return (updated, tendency(wind_field, viscous, drag_cells, forcing))

    first_ions, first_tend = section(neutral_wind, ion_density)
    midpoint = neutral_wind + neutral_step * first_tend
    second_ions, second_tend = section(midpoint, first_ions)
    wind_out = neutral_wind + 0.5 * neutral_step * (first_tend + second_tend)
    ion_out = 0.5 * (ion_density + second_ions)
    return (wind_out, ion_out)


def solution(mesh):
    placed = (
        P(None, "gx", "gy", None),
        P(None, "gx", "gy", None),
        P(None, ("gx", "gy"), None),
        P("gx", None, None, None),
        P(("gx", "gy")),
        P(),
        P(),
        P(),
        P(("gx", "gy"), None, None),
        P(("gx", "gy"), None, None),
        P(("gx", "gy"), None, None),
        P(("gx", "gy"), None, None),
        P(("gx", "gy"), None, None),
        P(),
    )
    return jax.shard_map(
        per_device,
        mesh=mesh,
        in_specs=placed,
        out_specs=(P(None, "gx", "gy", None), P(None, ("gx", "gy"), None)),
        check_vma=False,
    )
```

profile of v0, /device:TPU:1, one launch (start us, length us, event | category | flops | bytes accessed | tf_op | source)
XLA Modules:
  0.0 1594.8 jit_solution(12413124481931325185)
XLA Ops:
  0.7 17.4 %copy.32 = f32[2,16,32,128]{0,3,2,1:T(8,128)} copy(f32[2,16,32,128]{3,2,1,0:T(8,128)} %param.14) | data formatting | bytes 1048576 | tf_op args[0]
  18.3 119.5 %gather_fusion = f32[32768,2]{1,0:T(8,128)} fusion(f32[2,65536]{0,1:T(8,128)} %bitcast.65, s32[32768]{0:T(1024)S(1)} %broadcast_clamp_fusion.1), kind=kCustom, calls=%fused_computation | custom fusion | bytes 655360 | tf_op jit(solution)/shard_map/gather | solution.py:100
  137.7 9.8 copy.33
  147.6 11.5 all-to-all-start
  159.7 4.0 collective-permute-start.1
  163.7 1.3 collective-permute-start
  165.6 3.6 collective-permute-start.3
  169.3 1.9 collective-permute-start.2
  173.7 8.2 copy.34
  181.9 187.6 %scatter_custom_fusion = f32[2,65536]{0,1:T(8,128)} fusion(s32[32768]{0:T(1024)S(1)} %bitcast.81, f32[32768,2]{1,0:T(8,128)} %copy.34, f32[]{:T(128)} %constant.13.clone.1), kind=kCustom, calls=%fused_computation.20 | custom fusion | flops 65536 | bytes 524800 | tf_op jit(solution)/shard_map/scatter-add | solution.py:106
  369.4 32.8 %slice_reduce_fusion.3 = (f32[65536]{0:T(1024)S(1)}, f32[65536]{0:T(1024)S(1)}) fusion(f32[2,65536]{0,1:T(8,128)} %scatter_custom_fusion), kind=kLoop, calls=%fused_computation.11 | loop fusion | bytes 1048576 | tf_op jit(solution)/shard_map/slice | solution.py:54
  403.4 3.6 collective-permute-start.4
  407.1 1.3 fusion.62
  409.2 1.2 fusion.42
  410.5 23.0 %broadcast_multiply_fusion.1 = f32[2,65536]{0,1:T(8,128)} fusion(f32[2,65536]{0,1:T(8,128)} %scatter_custom_fusion, f32[65536]{0:T(1024)S(1)} %bitcast.75), kind=kLoop, calls=%fused_computation.13 | loop fusion | flops 131072 | bytes 1310720 | tf_op jit(solution)/shard_map/mul | solution.py:110
  433.5 119.5 %gather_fusion.1 = f32[32768,2]{1,0:T(8,128)} fusion(f32[2,65536]{0,1:T(8,128)} %broadcast_multiply_fusion.1, s32[32768]{0:T(1024)S(1)} %broadcast_clamp_fusion), kind=kCustom, calls=%fused_computation.1 | custom fusion | bytes 655360 | tf_op jit(solution)/shard_map/gather | solution.py:112
  552.9 9.5 copy.35
  563.3 12.8 all-to-all-start.1
  576.1 1.4 constant_dynamic-update-slice_fusion.2
  578.3 1.4 constant_dynamic-update-slice_fusion
  579.6 7.5 all-to-all-done.1
  587.1 8.1 copy.36
  595.2 187.5 %scatter_custom_fusion.1 = f32[2,65536]{0,1:T(8,128)} fusion(s32[32768]{0:T(1024)} %bitcast.86, f32[32768,2]{1,0:T(8,128)} %copy.36, f32[]{:T(128)} %constant.13.clone.1), kind=kCustom, calls=%fused_computation.18 | custom fusion | flops 65536 | bytes 524800 | tf_op jit(solution)/shard_map/scatter-add | solution.py:119
  782.8 19.5 %copy.37 = f32[2,16,32,128]{3,2,1,0:T(8,128)S(1)} copy(f32[2,16,32,128]{0,3,2,1:T(8,128)} %bitcast.64) | data formatting | bytes 1048576 | tf_op jit(solution)/shard_map/reshape | solution.py:121
  802.2 2.6 multiply_add_fusion.1
  804.8 16.4 %copy.38 = f32[2,16,32,128]{0,3,2,1:T(8,128)} copy(f32[2,16,32,128]{3,2,1,0:T(8,128)S(1)} %get-tuple-element.10) | data formatting | bytes 1048576 | tf_op jit(solution)/shard_map/add | solution.py:125
  821.2 119.5 %gather_fusion.2 = f32[32768,2]{1,0:T(8,128)} fusion(f32[2,65536]{0,1:T(8,128)} %bitcast.66, s32[32768]{0:T(1024)S(1)} %broadcast_clamp_fusion.1), kind=kCustom, calls=%fused_computation.2 | custom fusion | bytes 655360 | tf_op jit(solution)/shard_map/gather | solution.py:100
  940.7 9.5 copy.39
  950.2 15.3 all_to_all.20
  965.6 8.2 copy.40
  973.8 187.6 %scatter_custom_fusion.2 = f32[2,65536]{0,1:T(8,128)} fusion(s32[32768]{0:T(1024)} %bitcast.82, f32[32768,2]{1,0:T(8,128)} %copy.40, f32[]{:T(128)} %constant.13.clone.1), kind=kCustom, calls=%fused_computation.16 | custom fusion | flops 65536 | bytes 524800 | tf_op jit(solution)/shard_map/scatter-add | solution.py:106
  1161.4 33.5 %slice_reduce_fusion.1 = (f32[65536]{0:T(1024)}, f32[65536]{0:T(1024)}) fusion(f32[2,65536]{0,1:T(8,128)} %scatter_custom_fusion.2), kind=kLoop, calls=%fused_computation.9 | loop fusion | bytes 1048576 | tf_op jit(solution)/shard_map/slice | solution.py:54
  1194.9 1.7 mul.282
  1196.6 1.7 mul.279
  1198.3 1.6 broadcast_multiply_fusion.2
  1199.9 2.8 collective-permute-start.9
  1205.8 23.0 %broadcast_multiply_fusion = f32[2,65536]{0,1:T(8,128)} fusion(f32[2,65536]{0,1:T(8,128)} %scatter_custom_fusion.2, f32[65536]{0:T(1024)S(1)} %bitcast.76), kind=kLoop, calls=%fused_computation.12 | loop fusion | flops 131072 | bytes 1310720 | tf_op jit(solution)/shard_map/mul | solution.py:110
  1228.8 119.5 %gather_fusion.3 = f32[32768,2]{1,0:T(8,128)} fusion(f32[2,65536]{0,1:T(8,128)} %broadcast_multiply_fusion, s32[32768]{0:T(1024)S(1)} %broadcast_clamp_fusion), kind=kCustom, calls=%fused_computation.3 | custom fusion | bytes 655360 | tf_op jit(solution)/shard_map/gather | solution.py:112
  1348.3 9.5 copy.41
  1358.6 6.7 all-to-all-start.3
  1365.3 1.3 collective-permute-start.5
  1366.6 4.0 collective-permute-start.6
  1370.6 4.1 collective-permute-start.8
  1374.7 1.9 collective-permute-start.7
  1376.7 8.2 copy.42
  1384.9 187.6 %scatter_custom_fusion.3 = f32[2,65536]{0,1:T(8,128)} fusion(s32[32768]{0:T(1024)} %bitcast.87, f32[32768,2]{1,0:T(8,128)} %copy.42, f32[]{:T(128)} %constant.13.clone.1), kind=kCustom, calls=%fused_computation.14 | custom fusion | flops 65536 | bytes 524800 | tf_op jit(solution)/shard_map/scatter-add | solution.py:119
  1572.5 19.5 %copy.43 = f32[2,16,32,128]{3,2,1,0:T(8,128)S(1)} copy(f32[2,16,32,128]{0,3,2,1:T(8,128)} %bitcast.63) | data formatting | bytes 1048576 | tf_op jit(solution)/shard_map/reshape | solution.py:121
  1592.0 2.3 fusion.24
  (78 shorter events, 11.6 us)
Async XLA Ops:
  0.6 401.7 %copy-start = (bf16[1,2,512,512]{3,2,1,0:T(8,128)(2,1)S(1)}, bf16[1,2,512,512]{3,2,1,0:T(8,128)(2,1)}, u32[]{:S(2)}) copy-start(bf16[1,2,512,512]{3,2,1,0:T(8,128)(2,1)} %param.17) | copy-start | bytes 3145732
  0.6 158.4 %copy-start.1 = (f32[2,16,32,128]{3,2,1,0:T(8,128)S(1)}, f32[2,16,32,128]{3,2,1,0:T(8,128)}, u32[]{:S(2)}) copy-start(f32[2,16,32,128]{3,2,1,0:T(8,128)} %param.14) | copy-start | bytes 1572868
  0.7 17.5 %copy-start.5 = (s32[1,128,256]{2,1,0:T(8,128)S(1)}, s32[1,128,256]{2,1,0:T(8,128)}, u32[]{:S(2)}) copy-start(s32[1,128,256]{2,1,0:T(8,128)} %param.23) | copy-start | bytes 393220
  0.7 17.5 %copy-start.6 = (s32[1,128,256]{2,1,0:T(8,128)S(1)}, s32[1,128,256]{2,1,0:T(8,128)}, u32[]{:S(2)}) copy-start(s32[1,128,256]{2,1,0:T(8,128)} %param.22) | copy-start | bytes 393220
  0.7 171.5 %copy-start.8 = (s32[1,128,256]{2,1,0:T(8,128)S(1)}, s32[1,128,256]{2,1,0:T(8,128)}, u32[]{:S(2)}) copy-start(s32[1,128,256]{2,1,0:T(8,128)} %param.25) | copy-start | bytes 393220
  0.7 171.5 %copy-start.9 = (s32[1,128,256]{2,1,0:T(8,128)S(1)}, s32[1,128,256]{2,1,0:T(8,128)}, u32[]{:S(2)}) copy-start(s32[1,128,256]{2,1,0:T(8,128)} %param.24) | copy-start | bytes 393220
  0.7 171.8 %copy-start.15 = (f32[2,2]{1,0:T(2,128)S(1)}, f32[2,2]{1,0:T(2,128)}, u32[]{:S(2)}) copy-start(f32[2,2]{1,0:T(2,128)} %param.20) | copy-start | bytes 52
  0.7 172.5 %copy-start.11 = (s32[128,128]{1,0:T(8,128)S(1)}, s32[128,128]{1,0:T(8,128)}, u32[]{:S(2)}) copy-start(s32[128,128]{1,0:T(8,128)} %param.27) | copy-start | bytes 196612
  0.7 172.7 %copy-start.10 = (f32[1,128,256]{2,1,0:T(8,128)S(1)}, f32[1,128,256]{2,1,0:T(8,128)}, u32[]{:S(2)}) copy-start(f32[1,128,256]{2,1,0:T(8,128)} %param.26) | copy-start | bytes 393220
  147.6 26.0 %all-to-all-start = ((f32[2,128,256]{2,0,1:T(2,128)}), f32[2,128,256]{2,0,1:T(2,128)S(1)}, u32[]{:S(2)}, u32[]{:S(2)}) async-start(f32[2,128,256]{2,0,1:T(2,128)} %bitcast.6), calls=%async_computation | async-start | bytes 524288 | tf_op jit(solution)/shard_map/all_to_all | solution.py:37
  159.7 416.4 %collective-permute-start.1 = (f32[2,1,32,128]{3,2,1,0:T(8,128)}, f32[2,1,32,128]{3,2,1,0:T(8,128)}, u32[]{:S(2)}, u32[]{:S(2)}) collective-permute-start(f32[2,1,32,128]{3,2,1,0:T(8,128)} %get-tuple-element.19), channel_id=1, source_target_pairs={{0,16},{16,32},{32,48},{48,64},{64,80},{80,96},{96,112},{1,17},{17... | collective-permute-start | bytes 98312 | tf_op jit(solution)/shard_map/ppermute | solution.py:18
  163.7 414.6 %collective-permute-start = (f32[2,1,32,128]{3,2,1,0:T(8,128)}, f32[2,1,32,128]{3,2,1,0:T(8,128)}, u32[]{:S(2)}, u32[]{:S(2)}) collective-permute-start(f32[2,1,32,128]{3,2,1,0:T(8,128)} %get-tuple-element.18), channel_id=1, source_target_pairs={{16,0},{32,16},{48,32},{64,48},{80,64},{96,80},{112,96},{17,1},{33... | collective-permute-start | bytes 98312 | tf_op jit(solution)/shard_map/ppermute | solution.py:19
  165.6 636.6 %collective-permute-start.3 = (f32[2,16,1,128]{3,2,1,0:T(1,128)}, f32[2,16,1,128]{3,2,1,0:T(1,128)S(1)}, u32[]{:S(2)}, u32[]{:S(2)}) collective-permute-start(f32[2,16,1,128]{3,2,1,0:T(1,128)} %get-tuple-element.17), channel_id=1, source_target_pairs={{0,1},{1,2},{2,3},{3,4},{4,5},{5,6},{6,7},{7,8},{8,9},{9,10},{10,1... | collective-permute-start | bytes 49160 | tf_op jit(solution)/shard_map/ppermute | solution.py:18
  169.3 633.0 %collective-permute-start.2 = (f32[2,16,1,128]{3,2,1,0:T(1,128)}, f32[2,16,1,128]{3,2,1,0:T(1,128)}, u32[]{:S(2)}, u32[]{:S(2)}) collective-permute-start(f32[2,16,1,128]{3,2,1,0:T(1,128)} %get-tuple-element.16), channel_id=1, source_target_pairs={{1,0},{2,1},{3,2},{4,3},{5,4},{6,5},{7,6},{8,7},{9,8},{10,9},{11,1... | collective-permute-start | bytes 49160 | tf_op jit(solution)/shard_map/ppermute | solution.py:19
  172.5 9.4 copy-start.7
  369.4 32.9 %copy-start.2 = (f32[2,128,512]{2,1,0:T(8,128)S(1)}, f32[2,128,512]{2,1,0:T(8,128)}, u32[]{:S(2)}) copy-start(f32[2,128,512]{2,1,0:T(8,128)} %param.16) | copy-start | bytes 1572868
  403.4 4.9 collective-permute-start.4
  563.3 23.8 %all-to-all-start.1 = ((f32[2,128,256]{2,0,1:T(2,128)}), f32[2,128,256]{2,0,1:T(2,128)S(1)}, u32[]{:S(2)}, u32[]{:S(2)}) async-start(f32[2,128,256]{2,0,1:T(2,128)} %broadcast_multiply_fusion.6), calls=%async_computation.1 | async-start | bytes 524288 | tf_op jit(solution)/shard_map/all_to_all | solution.py:41
  1161.4 37.0 %copy-start.12 = (f32[128]{0:T(128)S(1)}, f32[128]{0:T(128)}, u32[]{:S(2)}) copy-start(f32[128]{0:T(128)} %param.18) | copy-start | bytes 1540
  1161.4 36.9 %copy-start.13 = (f32[2]{0:T(128)S(1)}, f32[2]{0:T(128)}, u32[]{:S(2)}) copy-start(f32[2]{0:T(128)} %get-tuple-element.6) | copy-start | bytes 28
  1161.4 36.9 %copy-start.14 = (f32[2]{0:T(128)S(1)}, f32[2]{0:T(128)}, u32[]{:S(2)}) copy-start(f32[2]{0:T(128)} %get-tuple-element.7) | copy-start | bytes 28
  1161.4 42.1 %copy-start.3 = (f32[2,128,512]{2,1,0:T(8,128)S(1)}, f32[2,128,512]{2,1,0:T(8,128)}, u32[]{:S(2)}) copy-start(f32[2,128,512]{2,1,0:T(8,128)} %param.16) | copy-start | bytes 1572868
  1199.9 3.6 collective-permute-start.9
  1358.6 18.1 %all-to-all-start.3 = ((f32[2,128,256]{2,0,1:T(2,128)}), f32[2,128,256]{2,0,1:T(2,128)S(1)}, u32[]{:S(2)}, u32[]{:S(2)}) async-start(f32[2,128,256]{2,0,1:T(2,128)} %broadcast_multiply_fusion.4), calls=%async_computation.3 | async-start | bytes 524288 | tf_op jit(solution)/shard_map/all_to_all | solution.py:41
  1365.3 226.7 %collective-permute-start.5 = (f32[2,1,32,128]{3,2,1,0:T(8,128)S(1)}, f32[2,1,32,128]{3,2,1,0:T(8,128)S(1)}, u32[]{:S(2)}, u32[]{:S(2)}) collective-permute-start(f32[2,1,32,128]{3,2,1,0:T(8,128)S(1)} %get-tuple-element.15), channel_id=1, source_target_pairs={{16,0},{32,16},{48,32},{64,48},{80,64},{96,80},{112,96},{17,1},{33... | collective-permute-start | bytes 98312 | tf_op jit(solution)/shard_map/ppermute | solution.py:19
  1366.6 225.4 %collective-permute-start.6 = (f32[2,1,32,128]{3,2,1,0:T(8,128)S(1)}, f32[2,1,32,128]{3,2,1,0:T(8,128)S(1)}, u32[]{:S(2)}, u32[]{:S(2)}) collective-permute-start(f32[2,1,32,128]{3,2,1,0:T(8,128)S(1)} %get-tuple-element.14), channel_id=1, source_target_pairs={{0,16},{16,32},{32,48},{48,64},{64,80},{80,96},{96,112},{1,17},{17... | collective-permute-start | bytes 98312 | tf_op jit(solution)/shard_map/ppermute | solution.py:18
  1370.6 221.3 %collective-permute-start.8 = (f32[2,16,1,128]{3,2,1,0:T(1,128)S(1)}, f32[2,16,1,128]{3,2,1,0:T(1,128)S(1)}, u32[]{:S(2)}, u32[]{:S(2)}) collective-permute-start(f32[2,16,1,128]{3,2,1,0:T(1,128)S(1)} %get-tuple-element.13), channel_id=1, source_target_pairs={{0,1},{1,2},{2,3},{3,4},{4,5},{5,6},{6,7},{7,8},{8,9},{9,10},{10,1... | collective-permute-start | bytes 49160 | tf_op jit(solution)/shard_map/ppermute | solution.py:18
  1374.7 217.2 %collective-permute-start.7 = (f32[2,16,1,128]{3,2,1,0:T(1,128)S(1)}, f32[2,16,1,128]{3,2,1,0:T(1,128)S(1)}, u32[]{:S(2)}, u32[]{:S(2)}) collective-permute-start(f32[2,16,1,128]{3,2,1,0:T(1,128)S(1)} %get-tuple-element.12), channel_id=1, source_target_pairs={{1,0},{2,1},{3,2},{4,3},{5,4},{6,5},{7,6},{8,7},{9,8},{10,9},{11,1... | collective-permute-start | bytes 49160 | tf_op jit(solution)/shard_map/ppermute | solution.py:19
  1384.9 207.1 %copy-start.4 = (f32[2,16,32,128]{3,2,1,0:T(8,128)S(1)}, f32[2,16,32,128]{3,2,1,0:T(8,128)}, u32[]{:S(2)}) copy-start(f32[2,16,32,128]{3,2,1,0:T(8,128)} %param.15) | copy-start | bytes 1572868
  1384.9 207.1 %copy-start.16 = (f32[128]{0:T(128)S(1)}, f32[128]{0:T(128)}, u32[]{:S(2)}) copy-start(f32[128]{0:T(128)} %param.19) | copy-start | bytes 1540
where the time goes:
time: 1610 us; the launch traced here: 1590 us
  other arithmetic  808 us (50%)
  local copies, waits for them, and re-layouts  699 us (43%)
  starting transfers between devices  59.6 us (4%)
    scatter-add x2, other arithmetic, section(): gathered_sum = jnp.zeros((2, flattened.shape[1]), jnp.float32).at[:, cell...  375 us
    scatter-add x2, other arithmetic, section(): tube_winds = jnp.zeros((2, tube_shape[1] * tube_shape[2]), jnp.float32).a...  375 us
    gather x4, local copies, waits for them, and re-layouts, section(): values = flattened[:, cell_list]  258 us
    gather x2, local copies, waits for them, and re-layouts, section(): drag_force.reshape(2, -1)[:, slot_list].reshape(2, device_count, capacity)  239 us
    slice x2, local copies, waits for them, and re-layouts, ion_update(): tube_winds[0]  66.3 us
    mul x2, other arithmetic, section(): -(drag_rate[0] * updated[0] + drag_rate[1] * updated[1])[None] * tube_winds  46.1 us
    reshape x2, local copies, waits for them, and re-layouts, section(): drag_cells = gathered_sum.reshape(field_shape)  38.9 us
  transfers between devices with their start and end apart: 13, of which 2 were waited for; matrix products, arithmetic and copies ran while one was open for 52% of the time, Pallas kernels for 0%

commit v1 on v0

v1 whole, which is shorter than its diff:
```python
import jax
import jax.numpy as jnp
from jax import lax
from jax.experimental import pallas as pl
from jax.experimental.pallas import tpu as pltpu
from jax.sharding import PartitionSpec as P

i32, f32, bf16 = jnp.int32, jnp.float32, jnp.bfloat16
VM = pl.BlockSpec(memory_space=pltpu.VMEM)
SM = pl.BlockSpec(memory_space=pltpu.SMEM)
W = 128
neutral_step = 0.4
ion_factor = 0.5


def bitonic(x):
    n, L = x.shape
    x = x.reshape(n//8, 8, L)
    sub = lax.broadcasted_iota(i32, (1, 8, L), 1)
    k = 2
    while k <= n:
        d = k//2
        while d >= 1:
            if d >= 8:
                dv = d//8
                y = x.reshape(n//(16*dv), 2, dv, 8, L)
                a, b = y[:, 0], y[:, 1]
                lo, hi = jnp.minimum(a, b), jnp.maximum(a, b)
                parts = []
                for g in range(n//(16*dv)):
                    up = ((g*2*d) & k) == 0
                    parts += [lo[g], hi[g]] if up else [hi[g], lo[g]]
                x = jnp.concatenate(parts, axis=0)
            else:
                up_r = pltpu.roll(x, 8-d, 1)
                dn_r = pltpu.roll(x, d, 1)
                first = (sub & d) == 0
                p = jnp.where(first, up_r, dn_r)
                mn, mx = jnp.minimum(x, p), jnp.maximum(x, p)
                if k >= 8:
                    if k == 8:
                        vi = lax.broadcasted_iota(i32, (n//8, 1, 1), 0)
                    parts = []
                    xs = []
                    take_min_up = first
                    kv = k//8
                    for g in range(0, n//8, kv):
                        up = (g*8 & k) == 0
                        sel = first if up else jnp.logical_not(first)
                        xs.append(jnp.where(sel, mn[g:g+kv], mx[g:g+kv]))
                    x = jnp.concatenate(xs, axis=0) if len(xs) > 1 else xs[0]
                else:
                    up = (sub & k) == 0
                    sel = first == up
                    x = jnp.where(sel, mn, mx)
            d //= 2
        k *= 2
    return x.reshape(n, L)

def sort_side(key16, cell_ref, pos_ref, inv_ref, bnd_ref):
    P, C = key16.shape
    c = lax.broadcasted_iota(i32, (P, C), 1)
    k = (key16 * 256 + c).T
    s = bitonic(k)
    cell = s >> 8
    pos = s & 255
    cell_ref[...] = cell
    pos_ref[...] = pos.T
    r = lax.broadcasted_iota(i32, (C, P), 0)
    inv = bitonic(pos*256 + r) & 255
    inv_ref[...] = inv.T
    row = (cell >> 7).reshape(C//8, 8, P)
    lo = jnp.min(jnp.min(row, axis=1), axis=1, keepdims=True)
    hi = jnp.max(jnp.max(row, axis=1), axis=1, keepdims=True)
    lane = lax.broadcasted_iota(i32, (C//8, 128), 1)
    bnd_ref[...] = jnp.where(lane == 0, lo, hi)

def sort_kernel(col, lev, tub, pnt, cellA, posA, invA, bndA, cellB, posB, invB, bndB):
    sort_side(col[0]*128 + lev[0], cellA, posA, invA, bndA)
    p = pnt[0]
    sort_side(((p >> 7) << 14) + (tub[0] << 7) + (p & 127), cellB, posB, invB, bndB)

def sort_call(col, lev, tub, pnt):
    P, C = col.shape[1:]
    side = [jax.ShapeDtypeStruct((C, P), i32), jax.ShapeDtypeStruct((P, C), i32), jax.ShapeDtypeStruct((P, C), i32), jax.ShapeDtypeStruct((C//8, 128), i32)]
    return pl.pallas_call(sort_kernel, out_shape=side*2, in_specs=[VM]*4, out_specs=[VM]*8, name="sort")(col, lev, tub, pnt)

def permute_lanes(x, idx):
    outs = []
    for h in range(2):
        ix = idx[:, h*128:(h+1)*128]
        low = ix & 127
        a = jnp.take_along_axis(x[:, :128], low, axis=1)
        b = jnp.take_along_axis(x[:, 128:], low, axis=1)
        outs.append(jnp.where(ix < 128, a, b))
    return outs

def lookup(bnd, cell_ref, t_ref, s_ref):
    def block(v, _):
        cell = cell_ref[pl.ds(pl.multiple_of(v*8, 8), 8), :]
        row, lev = cell >> 7, cell & 127
        lo, hi = bnd[v, 0], bnd[v, 1]
        g0 = lo // 8
        def rows(g, acc):
            a0, a1 = acc
            base = pl.multiple_of(g*8, 8)
            rel = row - base
            b0 = t_ref[0, pl.ds(base, 8), :]
            b1 = t_ref[1, pl.ds(base, 8), :]
            for j in range(8):
                m = rel == j
                x0 = jnp.take_along_axis(jnp.broadcast_to(b0[j:j+1], (8, 128)), lev, axis=1)
                x1 = jnp.take_along_axis(jnp.broadcast_to(b1[j:j+1], (8, 128)), lev, axis=1)
                a0 = jnp.where(m, x0, a0)
                a1 = jnp.where(m, x1, a1)
            return a0, a1
        z = jnp.zeros((8, 128), f32)
        a0, a1 = lax.fori_loop(g0, hi//8 + 1, rows, (z, z))
        s_ref[0, pl.ds(pl.multiple_of(v*8, 8), 8), :] = a0
        s_ref[1, pl.ds(pl.multiple_of(v*8, 8), 8), :] = a1
        return 0
    lax.fori_loop(0, 32, block, 0)

def scatter_add(bnd, cell_ref, val_ref, acc_ref):
    acc_ref[...] = jnp.zeros_like(acc_ref)
    iota = lax.broadcasted_iota(i32, (128, 128), 0).astype(f32).astype(bf16)
    one = jnp.ones((128, 128), bf16); zero = jnp.zeros((128, 128), bf16)
    def block(v, _):
        sl = pl.ds(pl.multiple_of(v*8, 8), 8)
        cell = cell_ref[sl, :]
        row, lev = cell >> 7, (cell & 127).astype(f32)
        lo, hi = bnd[v, 0], bnd[v, 1]
        base = (lo // 8) * 8
        vals = []
        for k in range(2):
            x = val_ref[k, sl, :]
            h = x.astype(bf16).astype(f32)
            vals.append((h, x - h))
        def spread(x):
            return jnp.broadcast_to(x, (128, 128)).astype(bf16)
        V = [[], []]
        for r in range(8):
            m = iota == spread(lev[r:r+1])
            for p in range(2):
                V[p].append(jnp.concatenate([jnp.where(m, spread(vals[k][p][r:r+1]), zero) for k in range(2)], axis=0))
        V = [jnp.concatenate(v_, axis=1) for v_ in V]
        def win(it, _):
            rb = pl.multiple_of(base + it*W, 8)
            rel = (row - rb).astype(f32)
            oh = jnp.concatenate([jnp.where(iota == spread(rel[r:r+1]), one, zero) for r in range(8)], axis=1)
            dn = (((1,), (1,)), ((), ()))
            o = lax.dot_general(oh, V[0], dn, preferred_element_type=f32) + lax.dot_general(oh, V[1], dn, preferred_element_type=f32)
            acc_ref[pl.ds(rb, W), :] += o
            return 0
        lax.fori_loop(0, (hi - base)//W + 1, win, 0)
        return 0
    lax.fori_loop(0, 32, block, 0)


def to_wire(inv, s, out, gain=None):
    for k in range(2):
        o = permute_lanes(s[k].T, inv[...])
        for h in range(2):
            x = o[h]
            if gain is not None:
                x = x * gain[:, h*128:(h+1)*128]
            out[:, 2*k+h, :] = x


def from_wire(pos, wire, val, gain=None):
    for k in range(2):
        x = [wire[:, 2*k+h, :] for h in range(2)]
        if gain is not None:
            x = [x[h] * gain[:, h*128:(h+1)*128] for h in range(2)]
        o = permute_lanes(jnp.concatenate(x, axis=1), pos[...])
        val[k, :128, :] = o[0].T
        val[k, 128:, :] = o[1].T


def gather_kernel(bnd, cell, inv, t, out, s):
    lookup(bnd, cell, t, s)
    to_wire(inv, s, out)


def tube_kernel(bnd, coupling, cell, pos, gain, drift, wire, ions, inverse, w_out, smooth_out, last_out, val, acc):
    from_wire(pos, wire, val, gain)
    scatter_add(bnd, cell, val, acc)
    w = []
    for k in range(2):
        for j in range(4):
            w_out[k, :, j*128:(j+1)*128] = acc[j*128:(j+1)*128, k*128:(k+1)*128]
    for k in range(2):
        n = ions[k]
        growth = coupling[k, 0] * w_out[0] + coupling[k, 1] * w_out[1]
        rhs = n + ion_factor * n * growth
        mix = lax.dot_general(rhs.astype(bf16), inverse[0, k], (((1,), (0,)), ((), ())), preferred_element_type=f32)
        sm = rhs + mix
        smooth_out[k] = sm
        last_out[k] = drift[127:128, :1] * sm[127:128, :]


def drag_kernel(last, bnd, drag, cell, inv, gain, drift, w, smooth, up, ions, n_out, wire, t, s):
    first = lax.broadcasted_iota(i32, (128, 128), 0) == 0
    d = drift[...]
    n = [[], []]
    for k in range(2):
        for j in range(4):
            sl = slice(j*128, (j+1)*128)
            sm = smooth[k, :, sl]
            out = d * sm
            inflow = jnp.where(first, jnp.broadcast_to(up[k, :, sl], (128, 128)), pltpu.roll(out, 1, 0))
            x = sm - out + inflow
            n[k].append(x)
            n_out[k, :, sl] = 0.5 * (ions[k, :, sl] + x) if last else x
    for j in range(4):
        f = -(drag[0] * n[0][j] + drag[1] * n[1][j])
        for k in range(2):
            t[k, j*128:(j+1)*128, :] = f * w[k, :, j*128:(j+1)*128]
    lookup(bnd, cell, t, s)
    to_wire(inv, s, wire, gain)


def tend_all(wind, forcing, visc, xlo, xhi, ylo, yhi, acc, emit):
    CX, CY = wind.shape[1], wind.shape[2]
    sub = lax.broadcasted_iota(i32, (CY, 128), 0)
    lane = lax.broadcasted_iota(i32, (CY, 128), 1)
    v = jnp.broadcast_to(visc[...], (CY, 128))
    for k in range(2):
        for i in range(CX):
            u = wind[k, i]
            b = (wind[k, i+1] if i < CX-1 else xhi[k, 0]) + (wind[k, i-1] if i > 0 else xlo[k, 0])
            nxt = jnp.where(sub == CY-1, jnp.broadcast_to(yhi[k, i], (CY, 128)), pltpu.roll(u, CY-1, 0))
            prv = jnp.where(sub == 0, jnp.broadcast_to(ylo[k, i], (CY, 128)), pltpu.roll(u, 1, 0))
            b = b + nxt + prv
            b = b + jnp.where(lane == 127, 0.0, pltpu.roll(u, 127, 1)) + jnp.where(lane == 0, 0.0, pltpu.roll(u, 1, 1))
            emit(k, i, u, v * (b - 6.0 * u) + acc[i*CY:(i+1)*CY, k*128:(k+1)*128] + forcing[k, i])


def mid_kernel(bnd, cell, pos, inv, wire, wind, forcing, visc, xlo, xhi, ylo, yhi, mid, wire_out, val, acc, s):
    from_wire(pos, wire, val)
    scatter_add(bnd, cell, val, acc)
    CY = wind.shape[2]

    def emit(k, i, u, f):
        mid[k, i*CY:(i+1)*CY, :] = u + neutral_step * f

    tend_all(wind, forcing, visc, xlo, xhi, ylo, yhi, acc, emit)
    lookup(bnd, cell, mid, s)
    to_wire(inv, s, wire_out)


def end_kernel(bnd, cell, pos, wire, start, wind, forcing, visc, xlo, xhi, ylo, yhi, out, val, acc):
    from_wire(pos, wire, val)
    scatter_add(bnd, cell, val, acc)

    def emit(k, i, u, f):
        out[k, i] = 0.5 * (start[k, i] + u) + (0.5 * neutral_step) * f

    tend_all(wind, forcing, visc, xlo, xhi, ylo, yhi, acc, emit)


def call(kernel, outs, scratch, *args, smem=1, name=None):
    return pl.pallas_call(
        kernel,
        out_shape=outs,
        in_specs=[SM] * smem + [VM] * (len(args) - smem),
        out_specs=jax.tree.map(lambda _: VM, outs),
        scratch_shapes=scratch,
        name=name,
    )(*args)


def edges(wind):
    out = []
    for axis, dim in (("gx", 1), ("gy", 2)):
        peers, length = lax.axis_size(axis), wind.shape[dim]
        up = [(i, i + 1) for i in range(peers - 1)]
        out.append(lax.ppermute(lax.slice_in_dim(wind, length - 1, length, axis=dim), axis, up))
        out.append(lax.ppermute(lax.slice_in_dim(wind, 0, 1, axis=dim), axis, [(b, a) for a, b in up]))
    return out


def exchange(x):
    return lax.all_to_all(x, ("gx", "gy"), split_axis=0, concat_axis=0, tiled=True)


def per_device(
    neutral_wind,
    forcing,
    ion_density,
    inverse,
    drift_fraction,
    viscosity,
    coupling,
    drag_rate,
    outgoing_column,
    send_level,
    recv_tube,
    recv_point,
    recv_weight,
    pair_count,
):
    own = lax.axis_index(("gx", "gy"))
    cap = recv_weight.shape[2]
    incoming = lax.dynamic_slice_in_dim(pair_count, own, 1, 1)
    position = lax.broadcasted_iota(i32, (128, cap), 1)
    gain = recv_weight[0] * (position < incoming).astype(f32)
    drift = jnp.broadcast_to(drift_fraction[:, None], (128, 128))
    visc = viscosity[None, :]
    sd = jax.ShapeDtypeStruct
    wire_t = sd((128, 4, 128), f32)
    tube_t = sd(ion_density.shape, f32)
    vals = pltpu.VMEM((2, 256, 128), f32)
    accs = pltpu.VMEM((512 + W, 256), f32)
    tabs = pltpu.VMEM((2, 512, 128), f32)
    cA, pA, iA, bA, cB, pB, iB, bB = sort_call(outgoing_column, send_level, recv_tube, recv_point)
    flat = (2, 512, 128)
    up_route = [(i, i + 1) for i in range(lax.axis_size("gy") - 1)]

    def tubes(wire, ions, last):
        w, smooth, out_last = call(
            tube_kernel, (tube_t, tube_t, sd((2, 1, 512), f32)), [vals, accs],
            bB, coupling, cB, pB, gain, drift, wire, ions, inverse, smem=2, name="tube")
        up = lax.ppermute(out_last, "gy", up_route)
        return call(
            lambda *a: drag_kernel(last, *a), (tube_t, wire_t), [tabs, vals],
            bB, drag_rate, cB, iB, gain, drift, w, smooth, up, ion_density, smem=2, name="drag")

    halo = edges(neutral_wind)
    wire = call(gather_kernel, wire_t, [vals], bA, cA, iA, neutral_wind.reshape(flat), name="first")
    n1, wire = tubes(exchange(wire), ion_density, False)
    mid, wire = call(
        mid_kernel, (sd(flat, f32), wire_t), [vals, accs, vals],
        bA, cA, pA, iA, exchange(wire), neutral_wind, forcing, visc, *halo, name="mid")
    mid = mid.reshape(neutral_wind.shape)
    halo = edges(mid)
    ion_out, wire = tubes(exchange(wire), n1, True)
    wind_out = call(
        end_kernel, sd(neutral_wind.shape, f32), [vals, accs],
        bA, cA, pA, exchange(wire), neutral_wind, mid, forcing, visc, *halo, name="end")
    return (wind_out, ion_out)


def solution(mesh):
    placed = (
        P(None, "gx", "gy", None),
        P(None, "gx", "gy", None),
        P(None, ("gx", "gy"), None),
        P("gx", None, None, None),
        P(("gx", "gy")),
        P(),
        P(),
        P(),
        P(("gx", "gy"), None, None),
        P(("gx", "gy"), None, None),
        P(("gx", "gy"), None, None),
        P(("gx", "gy"), None, None),
        P(("gx", "gy"), None, None),
        P(),
    )
    return jax.shard_map(
        per_device,
        mesh=mesh,
        in_specs=placed,
        out_specs=(P(None, "gx", "gy", None), P(None, ("gx", "gy"), None)),
        check_vma=False,
    )
```

time: 1610 us -> 331 us (0.21)
  other arithmetic: 808 us -> 0.74 us
  local copies, waits for them, and re-layouts: 699 us -> 8.28 us
  Pallas kernels: 0 us -> 213 us
    scatter-add x4 -> x0, other arithmetic: 750 us -> none  [the longest x2 375 us: section(): gathered_sum = jnp.zeros((2, flattened.shape[1]), jnp.float32).at[:, cell...]
    gather x6 -> x0, local copies, waits for them, and re-layouts: 497 us -> none  [the longest x4 258 us: section(): values = flattened[:, cell_list]]
    pallas_call x0 -> x8, Pallas kernels: none -> 213 us  [the longest x7 208 us: call(): pl.pallas_call(kernel, out_shape=outs, in_specs=[SM] * smem + [VM] * (len...]
    reshape x8 -> x0, local copies, waits for them, and re-layouts: 90.6 us -> none  [the longest x2 38.9 us: section(): drag_cells = gathered_sum.reshape(field_shape)]
    slice x10 -> x4, local copies, waits for them, and re-layouts: 69.6 us -> 3.57 us  [edges(): lax.slice_in_dim(wind, 0, 1, axis=dim)]
    mul x8 -> x1, other arithmetic: 49.1 us -> 0.74 us  [per_device(): gain = recv_weight[0] * (position < incoming).astype(f32)]
    add x1 -> x0, local copies, waits for them, and re-layouts: 16.4 us -> none  [per_device(): midpoint = neutral_wind + neutral_step * first_tend]
    unnamed x42 -> x32, local copies, waits for them, and re-layouts: 20.2 us -> 3.84 us
  transfers between devices with their start and end apart: 13 -> 13, of which waited for: 2 -> 5; matrix products, arithmetic and copies ran while one was open for 52% -> 1% of each run, Pallas kernels for 0% -> 0%
where the time goes in v1:
time: 331 us; the launch traced here: 326 us
  Pallas kernels  213 us (64%)
  starting transfers between devices  60.3 us (18%)
  blocking collectives  24.5 us (7%)
  waiting for transfers between devices  18.2 us (5%)
  local copies, waits for them, and re-layouts  8.28 us (3%)
    pallas_call x7, Pallas kernels, call(): pl.pallas_call(kernel, out_shape=outs, in_specs=[SM] * smem + [VM] * (len...  208 us
    all_to_all x3, starting transfers between devices, exchange(): lax.all_to_all(x, ('gx', 'gy'), split_axis=0, concat_axis=0, tiled=True)  34.2 us
    all_to_all x1, blocking collectives, exchange(): lax.all_to_all(x, ('gx', 'gy'), split_axis=0, concat_axis=0, tiled=True)  24.5 us
    ppermute x4, starting transfers between devices, edges(): lax.ppermute(lax.slice_in_dim(wind, length - 1, length, axis=dim), axis, up)  14.1 us
    all_to_all x3, waiting for transfers between devices, exchange(): lax.all_to_all(x, ('gx', 'gy'), split_axis=0, concat_axis=0, tiled=True)  10.1 us
  transfers between devices with their start and end apart: 13, of which 5 were waited for; matrix products, arithmetic and copies ran while one was open for 1% of the time, Pallas kernels for 0%

profile of v1, /device:TPU:1, one launch (start us, length us, event | category | flops | bytes accessed | tf_op | source)
XLA Modules:
  0.0 326.3 jit_solution(2630440216404477228)
XLA Ops:
  0.6 0.0 copy-start
  0.6 5.5 %sort.1 = (s32[256,128]{1,0:T(8,128)}, s32[128,256]{1,0:T(8,128)}, s32[128,256]{1,0:T(8,128)}, s32[32,128]{1,0:T(8,128)}, s32[256,128]{1,0:T(8,128)}, /*index=5*...) custom-call(s32[1,128,256]{2,1,0:T(8,128)} %col.1, s32[1,128,256]{2,1,0:T(8,128)} %lev.1, s32[1,128,256]{2,1,0:T(8,128)} %tub.1, ...), custom_call_target="tpu_custom_call" | custom-call | tf_op jit(solution)/shard_map/sort/pallas_call | solution.py:86
  6.1 32.0 %first.1 = f32[128,4,128]{2,1,0:T(4,128)} custom-call(s32[32,128]{1,0:T(8,128)} %get-tuple-element.22.bnd, s32[256,128]{1,0:T(8,128)} %get-tuple-element.23.cell, s32[128,256]{1,0:T(8,128)} %get-tuple-element.29.inv, f32[2,512,128]{2,1,0:T(8,128)} %bitcast.5), custom_call_target="tpu_custom_call" | custom-call | tf_op jit(solution)/shard_map/first/pallas_call | solution.py:263
  38.1 14.8 %all-to-all-start = ((f32[128,4,128]{2,1,0:T(4,128)}), f32[128,4,128]{2,1,0:T(4,128)S(1)}, u32[]{:S(2)}, u32[]{:S(2)}) async-start(f32[128,4,128]{2,1,0:T(4,128)} %first.1), calls=%async_computation | async-start | bytes 524288 | tf_op jit(solution)/shard_map/all_to_all | solution.py:284
  52.9 0.2 dynamic-slice_reduce_fusion
  53.1 0.7 bitcast_select_fusion.gain.a_4_
  53.9 10.1 %all-to-all-done.wire = f32[128,4,128]{2,1,0:T(4,128)S(1)} async-done(((f32[128,4,128]{2,1,0:T(4,128)}), f32[128,4,128]{2,1,0:T(4,128)S(1)}, u32[]{:S(2)}, u32[]{:S(2)}) %all-to-all-start) | async-done | bytes 262176 | tf_op jit(solution)/shard_map/all_to_all | solution.py:284
  64.0 0.7 copy-done.15
  64.6 0.7 broadcast_in_dim.4.drift.a_5_
  65.3 20.5 %tube.2 = (f32[2,128,512]{2,1,0:T(8,128)}, f32[2,128,512]{2,1,0:T(8,128)}, f32[2,1,512]{2,1,0:T(1,128)}) custom-call(s32[32,128]{1,0:T(8,128)} %get-tuple-element.25.bnd.a_0_, f32[2,2]{1,0:T(2,128)} %coupling.3, s32[256,128]{1,0:T(8,128)} %get-tuple-element.26.cell.a_2_, s32[128,256]{1,0:T(8,128)} %get-tuple-element.28.pos, ...), custom_call_target="tpu_custom_call" | custom-call | tf_op jit(solution)/shard_map/tube/pallas_call | solution.py:263
  85.9 2.8 collective-permute-start
  88.7 0.9 collective-permute-done.a_8_
  89.6 0.6 copy-done.14
  90.2 31.9 %drag.2 = (f32[2,128,512]{2,1,0:T(8,128)}, f32[128,4,128]{2,1,0:T(4,128)}) custom-call(s32[32,128]{1,0:T(8,128)} %get-tuple-element.25.bnd.a_0_, f32[2]{0:T(128)} %a_1_.3, s32[256,128]{1,0:T(8,128)} %get-tuple-element.26.cell.a_2_, s32[128,256]{1,0:T(8,128)} %get-tuple-element.27.a_3_, f32[128,256]{1,0:T(8,128)} %bitcast_select_fusion.gain.a_4_, ...), custom_call_target="tpu_custom_call" | custom-call | tf_op jit(solution)/shard_map/drag/pallas_call | solution.py:263
  122.1 9.7 %all-to-all-start.1 = ((f32[128,4,128]{2,1,0:T(4,128)}), f32[128,4,128]{2,1,0:T(4,128)S(1)}, u32[]{:S(2)}, u32[]{:S(2)}) async-start(f32[128,4,128]{2,1,0:T(4,128)} %get-tuple-element.33), calls=%async_computation.1 | async-start | bytes 524288 | tf_op jit(solution)/shard_map/all_to_all | solution.py:284
  131.8 0.8 fusion.3
  132.6 3.4 %collective-permute-start.1 = (f32[2,1,32,128]{3,2,1,0:T(8,128)S(1)}, f32[2,1,32,128]{3,2,1,0:T(8,128)S(1)}, u32[]{:S(2)}, u32[]{:S(2)}) collective-permute-start(f32[2,1,32,128]{3,2,1,0:T(8,128)S(1)} %get-tuple-element.49), channel_id=1, source_target_pairs={{0,16},{16,32},{32,48},{48,64},{64,80},{80,96},{96,112},{1,17},{17... | collective-permute-start | bytes 98312 | tf_op jit(solution)/shard_map/ppermute | solution.py:278
  136.0 1.3 collective-permute-start.2
  137.3 1.0 fusion.2
  138.3 3.7 %collective-permute-start.3 = (f32[2,16,1,128]{3,2,1,0:T(1,128)S(1)}, f32[2,16,1,128]{3,2,1,0:T(1,128)S(1)}, u32[]{:S(2)}, u32[]{:S(2)}) collective-permute-start(f32[2,16,1,128]{3,2,1,0:T(1,128)S(1)} %get-tuple-element.47), channel_id=1, source_target_pairs={{0,1},{1,2},{2,3},{3,4},{4,5},{5,6},{6,7},{7,8},{8,9},{9,10},{10,1... | collective-permute-start | bytes 49160 | tf_op jit(solution)/shard_map/ppermute | solution.py:278
  142.0 1.9 collective-permute-start.4
  143.9 0.0 collective-permute-done.3.ylo
  143.9 3.1 collective-permute-done.4.yhi
  147.1 0.0 copy-start.2
  147.1 0.5 copy-done.11
  147.6 0.0 copy-done.5
  147.6 0.0 copy-done.7
  147.6 0.1 copy-done.2
  147.8 50.5 %mid.1 = (f32[2,512,128]{2,1,0:T(8,128)}, f32[128,4,128]{2,1,0:T(4,128)}) custom-call(s32[32,128]{1,0:T(8,128)} %get-tuple-element.22.bnd, s32[256,128]{1,0:T(8,128)} %get-tuple-element.23.cell, s32[128,256]{1,0:T(8,128)} %get-tuple-element.24.pos, s32[128,256]{1,0:T(8,128)} %get-tuple-element.29.inv, f32[128,4,128]{2,1,0:T(4,128)} %copy-done.2, ...), custom_call_target="tpu_custom_call" | custom-call | tf_op jit(solution)/shard_map/mid/pallas_call | solution.py:263
  198.2 24.5 %all_to_all.20.wire = f32[128,4,128]{2,1,0:T(4,128)} all-to-all(f32[128,4,128]{2,1,0:T(4,128)} %get-tuple-element.34), channel_id=1, replica_groups=mesh['gx'=8,'gy'=16] {'gx','gy'}, dimensions={0} | all-to-all | bytes 524288 | tf_op jit(solution)/shard_map/all_to_all | solution.py:284
  222.7 20.6 %tube.3 = (f32[2,128,512]{2,1,0:T(8,128)}, f32[2,128,512]{2,1,0:T(8,128)}, f32[2,1,512]{2,1,0:T(1,128)}) custom-call(s32[32,128]{1,0:T(8,128)} %get-tuple-element.25.bnd.a_0_, f32[2,2]{1,0:T(2,128)} %coupling.3, s32[256,128]{1,0:T(8,128)} %get-tuple-element.26.cell.a_2_, s32[128,256]{1,0:T(8,128)} %get-tuple-element.28.pos, ...), custom_call_target="tpu_custom_call" | custom-call | tf_op jit(solution)/shard_map/tube/pallas_call | solution.py:263
  243.2 2.8 collective-permute-start.5
  246.0 0.9 collective-permute-done.5.a_8_
  247.0 0.6 copy-done.13
  247.6 31.9 %drag.3 = (f32[2,128,512]{2,1,0:T(8,128)}, f32[128,4,128]{2,1,0:T(4,128)}) custom-call(s32[32,128]{1,0:T(8,128)} %get-tuple-element.25.bnd.a_0_, f32[2]{0:T(128)} %a_1_.3, s32[256,128]{1,0:T(8,128)} %get-tuple-element.26.cell.a_2_, s32[128,256]{1,0:T(8,128)} %get-tuple-element.27.a_3_, f32[128,256]{1,0:T(8,128)} %bitcast_select_fusion.gain.a_4_, ...), custom_call_target="tpu_custom_call" | custom-call | tf_op jit(solution)/shard_map/drag/pallas_call | solution.py:263
  279.5 9.7 %all-to-all-start.3 = ((f32[128,4,128]{2,1,0:T(4,128)}), f32[128,4,128]{2,1,0:T(4,128)S(1)}, u32[]{:S(2)}, u32[]{:S(2)}) async-start(f32[128,4,128]{2,1,0:T(4,128)} %get-tuple-element.39), calls=%async_computation.3 | async-start | bytes 524288 | tf_op jit(solution)/shard_map/all_to_all | solution.py:284
  289.2 0.8 fusion.1
  290.0 3.4 %collective-permute-start.6 = (f32[2,1,32,128]{3,2,1,0:T(8,128)S(1)}, f32[2,1,32,128]{3,2,1,0:T(8,128)S(1)}, u32[]{:S(2)}, u32[]{:S(2)}) collective-permute-start(f32[2,1,32,128]{3,2,1,0:T(8,128)S(1)} %get-tuple-element.45), channel_id=1, source_target_pairs={{0,16},{16,32},{32,48},{48,64},{64,80},{80,96},{96,112},{1,17},{17... | collective-permute-start | bytes 98312 | tf_op jit(solution)/shard_map/ppermute | solution.py:278
  293.4 1.3 collective-permute-start.7
  294.7 1.0 fusion
  295.7 3.7 %collective-permute-start.8 = (f32[2,16,1,128]{3,2,1,0:T(1,128)S(1)}, f32[2,16,1,128]{3,2,1,0:T(1,128)S(1)}, u32[]{:S(2)}, u32[]{:S(2)}) collective-permute-start(f32[2,16,1,128]{3,2,1,0:T(1,128)S(1)} %get-tuple-element.43), channel_id=1, source_target_pairs={{0,1},{1,2},{2,3},{3,4},{4,5},{5,6},{6,7},{7,8},{8,9},{9,10},{10,1... | collective-permute-start | bytes 49160 | tf_op jit(solution)/shard_map/ppermute | solution.py:278
  299.3 1.9 collective-permute-start.9
  301.3 3.1 collective-permute-done.9.yhi
  304.4 0.6 copy-done.12
  305.0 0.0 copy-done.6
  305.0 0.0 copy-done.8
  305.0 0.7 copy-done.1
  305.7 20.5 %end.1 = f32[2,16,32,128]{3,2,1,0:T(8,128)} custom-call(s32[32,128]{1,0:T(8,128)} %get-tuple-element.22.bnd, s32[256,128]{1,0:T(8,128)} %get-tuple-element.23.cell, s32[128,256]{1,0:T(8,128)} %get-tuple-element.24.pos, f32[128,4,128]{2,1,0:T(4,128)} %copy-done.1, f32[2,16,32,128]{3,2,1,0:T(8,128)} %start.1, f32[2,16,32,128]{3,2,1,0:T(8,128)} %bitcast.8, ...), custom_call_target="tpu_custom_call" | custom-call | tf_op jit(solution)/shard_map/end/pallas_call | solution.py:263
  (26 shorter events, 0.1 us)
Async XLA Ops:
  0.6 52.3 %copy-start = (s32[128,128]{1,0:T(8,128)S(1)}, s32[128,128]{1,0:T(8,128)}, u32[]{:S(2)}) copy-start(s32[128,128]{1,0:T(8,128)} %param.27) | copy-start | bytes 196612
  38.1 15.0 %copy-start.4 = (f32[1,128,256]{2,1,0:T(8,128)S(1)}, f32[1,128,256]{2,1,0:T(8,128)}, u32[]{:S(2)}) copy-start(f32[1,128,256]{2,1,0:T(8,128)} %param.26) | copy-start | bytes 393220
  38.1 25.8 %all-to-all-start = ((f32[128,4,128]{2,1,0:T(4,128)}), f32[128,4,128]{2,1,0:T(4,128)S(1)}, u32[]{:S(2)}, u32[]{:S(2)}) async-start(f32[128,4,128]{2,1,0:T(4,128)} %first.1), calls=%async_computation | async-start | bytes 524288 | tf_op jit(solution)/shard_map/all_to_all | solution.py:284
  64.0 1.4 copy-start.3
  64.0 0.7 copy-start.15
  85.9 3.8 %collective-permute-start = (f32[2,1,512]{2,1,0:T(1,128)}, f32[2,1,512]{2,1,0:T(1,128)S(1)}, u32[]{:S(2)}, u32[]{:S(2)}) collective-permute-start(f32[2,1,512]{2,1,0:T(1,128)} %get-tuple-element.32), channel_id=1, source_target_pairs={{0,1},{1,2},{2,3},{3,4},{4,5},{5,6},{6,7},{7,8},{8,9},{9,10},{10,1... | collective-permute-start | bytes 12296 | tf_op jit(solution)/shard_map/ppermute | solution.py:324
  89.6 0.6 copy-start.14
  122.1 24.9 %all-to-all-start.1 = ((f32[128,4,128]{2,1,0:T(4,128)}), f32[128,4,128]{2,1,0:T(4,128)S(1)}, u32[]{:S(2)}, u32[]{:S(2)}) async-start(f32[128,4,128]{2,1,0:T(4,128)} %get-tuple-element.33), calls=%async_computation.1 | async-start | bytes 524288 | tf_op jit(solution)/shard_map/all_to_all | solution.py:284
  132.6 14.4 %collective-permute-start.1 = (f32[2,1,32,128]{3,2,1,0:T(8,128)S(1)}, f32[2,1,32,128]{3,2,1,0:T(8,128)S(1)}, u32[]{:S(2)}, u32[]{:S(2)}) collective-permute-start(f32[2,1,32,128]{3,2,1,0:T(8,128)S(1)} %get-tuple-element.49), channel_id=1, source_target_pairs={{0,16},{16,32},{32,48},{48,64},{64,80},{80,96},{96,112},{1,17},{17... | collective-permute-start | bytes 98312 | tf_op jit(solution)/shard_map/ppermute | solution.py:278
  136.0 11.0 %collective-permute-start.2 = (f32[2,1,32,128]{3,2,1,0:T(8,128)S(1)}, f32[2,1,32,128]{3,2,1,0:T(8,128)S(1)}, u32[]{:S(2)}, u32[]{:S(2)}) collective-permute-start(f32[2,1,32,128]{3,2,1,0:T(8,128)S(1)} %get-tuple-element.48), channel_id=1, source_target_pairs={{16,0},{32,16},{48,32},{64,48},{80,64},{96,80},{112,96},{17,1},{33... | collective-permute-start | bytes 98312 | tf_op jit(solution)/shard_map/ppermute | solution.py:279
  138.3 5.6 %collective-permute-start.3 = (f32[2,16,1,128]{3,2,1,0:T(1,128)S(1)}, f32[2,16,1,128]{3,2,1,0:T(1,128)S(1)}, u32[]{:S(2)}, u32[]{:S(2)}) collective-permute-start(f32[2,16,1,128]{3,2,1,0:T(1,128)S(1)} %get-tuple-element.47), channel_id=1, source_target_pairs={{0,1},{1,2},{2,3},{3,4},{4,5},{5,6},{6,7},{7,8},{8,9},{9,10},{10,1... | collective-permute-start | bytes 49160 | tf_op jit(solution)/shard_map/ppermute | solution.py:278
  142.0 5.1 %collective-permute-start.4 = (f32[2,16,1,128]{3,2,1,0:T(1,128)S(1)}, f32[2,16,1,128]{3,2,1,0:T(1,128)S(1)}, u32[]{:S(2)}, u32[]{:S(2)}) collective-permute-start(f32[2,16,1,128]{3,2,1,0:T(1,128)S(1)} %get-tuple-element.46), channel_id=1, source_target_pairs={{1,0},{2,1},{3,2},{4,3},{5,4},{6,5},{7,6},{8,7},{9,8},{10,9},{11,1... | collective-permute-start | bytes 49160 | tf_op jit(solution)/shard_map/ppermute | solution.py:279
  143.9 3.2 copy-start.9
  147.0 0.6 copy-start.11
  147.0 0.6 copy-start.5
  147.0 0.6 copy-start.7
  147.1 0.7 copy-start.2
  243.2 3.8 %collective-permute-start.5 = (f32[2,1,512]{2,1,0:T(1,128)}, f32[2,1,512]{2,1,0:T(1,128)S(1)}, u32[]{:S(2)}, u32[]{:S(2)}) collective-permute-start(f32[2,1,512]{2,1,0:T(1,128)} %get-tuple-element.38), channel_id=1, source_target_pairs={{0,1},{1,2},{2,3},{3,4},{4,5},{5,6},{6,7},{7,8},{8,9},{9,10},{10,1... | collective-permute-start | bytes 12296 | tf_op jit(solution)/shard_map/ppermute | solution.py:324
  247.0 0.6 copy-start.13
  279.5 24.9 %all-to-all-start.3 = ((f32[128,4,128]{2,1,0:T(4,128)}), f32[128,4,128]{2,1,0:T(4,128)S(1)}, u32[]{:S(2)}, u32[]{:S(2)}) async-start(f32[128,4,128]{2,1,0:T(4,128)} %get-tuple-element.39), calls=%async_computation.3 | async-start | bytes 524288 | tf_op jit(solution)/shard_map/all_to_all | solution.py:284
  290.0 14.4 %collective-permute-start.6 = (f32[2,1,32,128]{3,2,1,0:T(8,128)S(1)}, f32[2,1,32,128]{3,2,1,0:T(8,128)S(1)}, u32[]{:S(2)}, u32[]{:S(2)}) collective-permute-start(f32[2,1,32,128]{3,2,1,0:T(8,128)S(1)} %get-tuple-element.45), channel_id=1, source_target_pairs={{0,16},{16,32},{32,48},{48,64},{64,80},{80,96},{96,112},{1,17},{17... | collective-permute-start | bytes 98312 | tf_op jit(solution)/shard_map/ppermute | solution.py:278
  293.4 11.0 %collective-permute-start.7 = (f32[2,1,32,128]{3,2,1,0:T(8,128)S(1)}, f32[2,1,32,128]{3,2,1,0:T(8,128)S(1)}, u32[]{:S(2)}, u32[]{:S(2)}) collective-permute-start(f32[2,1,32,128]{3,2,1,0:T(8,128)S(1)} %get-tuple-element.44), channel_id=1, source_target_pairs={{16,0},{32,16},{48,32},{64,48},{80,64},{96,80},{112,96},{17,1},{33... | collective-permute-start | bytes 98312 | tf_op jit(solution)/shard_map/ppermute | solution.py:279
  295.7 5.6 %collective-permute-start.8 = (f32[2,16,1,128]{3,2,1,0:T(1,128)S(1)}, f32[2,16,1,128]{3,2,1,0:T(1,128)S(1)}, u32[]{:S(2)}, u32[]{:S(2)}) collective-permute-start(f32[2,16,1,128]{3,2,1,0:T(1,128)S(1)} %get-tuple-element.43), channel_id=1, source_target_pairs={{0,1},{1,2},{2,3},{3,4},{4,5},{5,6},{6,7},{7,8},{8,9},{9,10},{10,1... | collective-permute-start | bytes 49160 | tf_op jit(solution)/shard_map/ppermute | solution.py:278
  299.3 5.1 %collective-permute-start.9 = (f32[2,16,1,128]{3,2,1,0:T(1,128)S(1)}, f32[2,16,1,128]{3,2,1,0:T(1,128)S(1)}, u32[]{:S(2)}, u32[]{:S(2)}) collective-permute-start(f32[2,16,1,128]{3,2,1,0:T(1,128)S(1)} %get-tuple-element.42), channel_id=1, source_target_pairs={{1,0},{2,1},{3,2},{4,3},{5,4},{6,5},{7,6},{8,7},{9,8},{10,9},{11,1... | collective-permute-start | bytes 49160 | tf_op jit(solution)/shard_map/ppermute | solution.py:279
  301.3 3.2 copy-start.10
  304.4 0.6 copy-start.12
  304.4 0.6 copy-start.6
  304.4 0.6 copy-start.8
  305.0 0.7 copy-start.1

commit v2 on v1

--- a/solution.py
+++ b/solution.py
@@ -8,7 +8,7 @@
 i32, f32, bf16 = jnp.int32, jnp.float32, jnp.bfloat16
 VM = pl.BlockSpec(memory_space=pltpu.VMEM)
 SM = pl.BlockSpec(memory_space=pltpu.SMEM)
-W = 128
+W, NB, LB, LR = 64, 16, 8, 16
 neutral_step = 0.4
 ion_factor = 0.5
 
@@ -76,9 +76,12 @@
     bnd_ref[...] = jnp.where(lane == 0, lo, hi)
 
 def sort_kernel(col, lev, tub, pnt, cellA, posA, invA, bndA, cellB, posB, invB, bndB):
-    sort_side(col[0]*128 + lev[0], cellA, posA, invA, bndA)
+    def key(row, lane):
+        return ((row & 255) << 8) + ((row >> 8) << 7) + lane
+
+    sort_side(key(col[0], lev[0]), cellA, posA, invA, bndA)
     p = pnt[0]
-    sort_side(((p >> 7) << 14) + (tub[0] << 7) + (p & 127), cellB, posB, invB, bndB)
+    sort_side(key((p >> 7)*128 + tub[0], p & 127), cellB, posB, invB, bndB)
 
 def sort_call(col, lev, tub, pnt):
     P, C = col.shape[1:]
@@ -96,65 +99,79 @@
     return outs
 
 def lookup(bnd, cell_ref, t_ref, s_ref):
-    def block(v, _):
-        cell = cell_ref[pl.ds(pl.multiple_of(v*8, 8), 8), :]
-        row, lev = cell >> 7, cell & 127
-        lo, hi = bnd[v, 0], bnd[v, 1]
-        g0 = lo // 8
+    half = t_ref.shape[1] // 2
+
+    def blocks(u, _):
+        row, lev, start, count = [], [], [], None
+        for i in range(LB):
+            v = u*LB + i
+            key = cell_ref[pl.ds(pl.multiple_of(v*8, 8), 8), :]
+            row.append(key >> 7)
+            lev.append(key & 127)
+            lo = bnd[v, 0] >> 1
+            start.append(lo)
+            need = (bnd[v, 1] - 2*lo) // LR + 1
+            count = need if count is None else jnp.maximum(count, need)
+
         def rows(g, acc):
-            a0, a1 = acc
-            base = pl.multiple_of(g*8, 8)
-            rel = row - base
-            b0 = t_ref[0, pl.ds(base, 8), :]
-            b1 = t_ref[1, pl.ds(base, 8), :]
-            for j in range(8):
-                m = rel == j
-                x0 = jnp.take_along_axis(jnp.broadcast_to(b0[j:j+1], (8, 128)), lev, axis=1)
-                x1 = jnp.take_along_axis(jnp.broadcast_to(b1[j:j+1], (8, 128)), lev, axis=1)
-                a0 = jnp.where(m, x0, a0)
-                a1 = jnp.where(m, x1, a1)
-            return a0, a1
-        z = jnp.zeros((8, 128), f32)
-        a0, a1 = lax.fori_loop(g0, hi//8 + 1, rows, (z, z))
-        s_ref[0, pl.ds(pl.multiple_of(v*8, 8), 8), :] = a0
-        s_ref[1, pl.ds(pl.multiple_of(v*8, 8), 8), :] = a1
+            acc = list(acc)
+            for i in range(LB):
+                base = jnp.minimum(start[i] + g*(LR//2), half - LR//2)
+                rel = row[i] - 2*base
+                for j in range(LR):
+                    m = rel == j
+                    for k in range(2):
+                        x = t_ref[k, pl.ds(base + (j//2) + (j % 2)*half, 1), :]
+                        x = jnp.take_along_axis(jnp.broadcast_to(x, (8, 128)), lev[i], axis=1, mode="promise_in_bounds")
+                        acc[2*i+k] = jnp.where(m, x, acc[2*i+k])
+            return tuple(acc)
+
+        acc = lax.fori_loop(0, count, rows, (jnp.zeros((8, 128), f32),)*(2*LB))
+        for i in range(LB):
+            for k in range(2):
+                s_ref[k, pl.ds(pl.multiple_of((u*LB + i)*8, 8), 8), :] = acc[2*i+k]
         return 0
-    lax.fori_loop(0, 32, block, 0)
+
+    lax.fori_loop(0, 32//LB, blocks, 0)
+
 
 def scatter_add(bnd, cell_ref, val_ref, acc_ref):
     acc_ref[...] = jnp.zeros_like(acc_ref)
-    iota = lax.broadcasted_iota(i32, (128, 128), 0).astype(f32).astype(bf16)
-    one = jnp.ones((128, 128), bf16); zero = jnp.zeros((128, 128), bf16)
+    iota = lax.broadcasted_iota(i32, (256, 128), 0).astype(f32).astype(bf16)
+    one, zero = jnp.ones((256, 128), bf16), jnp.zeros((256, 128), bf16)
+
+    def spread(x, n):
+        return jnp.broadcast_to(x, (n, 128)).astype(bf16)
+
     def block(v, _):
-        sl = pl.ds(pl.multiple_of(v*8, 8), 8)
-        cell = cell_ref[sl, :]
-        row, lev = cell >> 7, (cell & 127).astype(f32)
-        lo, hi = bnd[v, 0], bnd[v, 1]
+        sl = pl.ds(pl.multiple_of(v*NB, 8), NB)
+        key = cell_ref[sl, :]
+        q, lane = key >> 8, (key & 255).astype(f32)
+        lo, hi = bnd[v*(NB//8), 0] >> 1, bnd[(v+1)*(NB//8) - 1, 1] >> 1
         base = (lo // 8) * 8
         vals = []
         for k in range(2):
             x = val_ref[k, sl, :]
             h = x.astype(bf16).astype(f32)
-            vals.append((h, x - h))
-        def spread(x):
-            return jnp.broadcast_to(x, (128, 128)).astype(bf16)
-        V = [[], []]
-        for r in range(8):
-            m = iota == spread(lev[r:r+1])
-            for p in range(2):
-                V[p].append(jnp.concatenate([jnp.where(m, spread(vals[k][p][r:r+1]), zero) for k in range(2)], axis=0))
-        V = [jnp.concatenate(v_, axis=1) for v_ in V]
-        def win(it, _):
+            vals += [h, x - h]
+        lanes = jnp.concatenate([jnp.where(iota == spread(lane[r:r+1], 256), one, zero) for r in range(NB)], axis=1)
+
+        def window(it, _):
             rb = pl.multiple_of(base + it*W, 8)
-            rel = (row - rb).astype(f32)
-            oh = jnp.concatenate([jnp.where(iota == spread(rel[r:r+1]), one, zero) for r in range(8)], axis=1)
-            dn = (((1,), (1,)), ((), ()))
-            o = lax.dot_general(oh, V[0], dn, preferred_element_type=f32) + lax.dot_general(oh, V[1], dn, preferred_element_type=f32)
-            acc_ref[pl.ds(rb, W), :] += o
+            rel = (q - rb).astype(f32)
+            rows = []
+            for r in range(NB):
+                m = iota[:W] == spread(rel[r:r+1], W)
+                rows.append(jnp.concatenate([jnp.where(m, spread(x[r:r+1], W), zero[:W]) for x in vals], axis=0))
+            z = lax.dot_general(jnp.concatenate(rows, axis=1), lanes, (((1,), (1,)), ((), ())), preferred_element_type=f32)
+            for k in range(2):
+                acc_ref[k, pl.ds(rb, W), :] += z[2*k*W:(2*k+1)*W] + z[(2*k+1)*W:(2*k+2)*W]
             return 0
-        lax.fori_loop(0, (hi - base)//W + 1, win, 0)
+
+        lax.fori_loop(0, (hi - base)//W + 1, window, 0)
         return 0
-    lax.fori_loop(0, 32, block, 0)
+
+    lax.fori_loop(0, 256//NB, block, 0)
 
 
 def to_wire(inv, s, out, gain=None):
@@ -188,7 +205,7 @@
     w = []
     for k in range(2):
         for j in range(4):
-            w_out[k, :, j*128:(j+1)*128] = acc[j*128:(j+1)*128, k*128:(k+1)*128]
+            w_out[k, :, j*128:(j+1)*128] = acc[k, (j%2)*128:(j%2+1)*128, (j//2)*128:(j//2+1)*128]
     for k in range(2):
         n = ions[k]
         growth = coupling[k, 0] * w_out[0] + coupling[k, 1] * w_out[1]
@@ -233,7 +250,7 @@
             prv = jnp.where(sub == 0, jnp.broadcast_to(ylo[k, i], (CY, 128)), pltpu.roll(u, 1, 0))
             b = b + nxt + prv
             b = b + jnp.where(lane == 127, 0.0, pltpu.roll(u, 127, 1)) + jnp.where(lane == 0, 0.0, pltpu.roll(u, 1, 1))
-            emit(k, i, u, v * (b - 6.0 * u) + acc[i*CY:(i+1)*CY, k*128:(k+1)*128] + forcing[k, i])
+            emit(k, i, u, v * (b - 6.0 * u) + acc[k, (i*CY) % 256:(i*CY) % 256 + CY, (i*CY)//256*128:(i*CY)//256*128 + 128] + forcing[k, i])
 
 
 def mid_kernel(bnd, cell, pos, inv, wire, wind, forcing, visc, xlo, xhi, ylo, yhi, mid, wire_out, val, acc, s):
@@ -311,7 +328,7 @@
     wire_t = sd((128, 4, 128), f32)
     tube_t = sd(ion_density.shape, f32)
     vals = pltpu.VMEM((2, 256, 128), f32)
-    accs = pltpu.VMEM((512 + W, 256), f32)
+    accs = pltpu.VMEM((2, 256 + W, 256), f32)
     tabs = pltpu.VMEM((2, 512, 128), f32)
     cA, pA, iA, bA, cB, pB, iB, bB = sort_call(outgoing_column, send_level, recv_tube, recv_point)
     flat = (2, 512, 128)

time: 331 us -> 216 us (0.65)
  the two profiles are of different devices: /device:TPU:1 before, /device:TPU:23 now
where the time goes in v2:
time: 216 us; the launch traced here: 217 us
  Pallas kernels  108 us (50%)
  starting transfers between devices  67.4 us (31%)
  waiting for transfers between devices  17 us (8%)
  blocking collectives  14.4 us (7%)
  local copies, waits for them, and re-layouts  8.28 us (4%)
    pallas_call x7, Pallas kernels, call(): pl.pallas_call(kernel, out_shape=outs, in_specs=[SM] * smem + [VM] * (len...  103 us
    all_to_all x3, starting transfers between devices, exchange(): lax.all_to_all(x, ('gx', 'gy'), split_axis=0, concat_axis=0, tiled=True)  31.9 us
    ppermute x4, starting transfers between devices, edges(): lax.ppermute(lax.slice_in_dim(wind, 0, 1, axis=dim), axis, [(b, a) for a,...  14.9 us
    ppermute x4, starting transfers between devices, edges(): lax.ppermute(lax.slice_in_dim(wind, length - 1, length, axis=dim), axis, up)  14.6 us
    all_to_all x1, blocking collectives, exchange(): lax.all_to_all(x, ('gx', 'gy'), split_axis=0, concat_axis=0, tiled=True)  14.4 us
    ppermute x4, waiting for transfers between devices, edges(): lax.ppermute(lax.slice_in_dim(wind, 0, 1, axis=dim), axis, [(b, a) for a,...  8.02 us
    all_to_all x3, waiting for transfers between devices, exchange(): lax.all_to_all(x, ('gx', 'gy'), split_axis=0, concat_axis=0, tiled=True)  7.11 us
    ppermute x2, starting transfers between devices, tubes(): up = lax.ppermute(out_last, 'gy', up_route)  5.88 us
  transfers between devices with their start and end apart: 13, of which 5 were waited for; matrix products, arithmetic and copies ran while one was open for 2% of the time, Pallas kernels for 0%

profile of v2, /device:TPU:23, one launch (start us, length us, event | category | flops | bytes accessed | tf_op | source)
XLA Modules:
  0.0 216.7 jit_solution(10992223394096114609)
XLA Ops:
  0.6 0.0 copy-start
  0.6 5.5 %sort.1 = (s32[256,128]{1,0:T(8,128)}, s32[128,256]{1,0:T(8,128)}, s32[128,256]{1,0:T(8,128)}, s32[32,128]{1,0:T(8,128)}, s32[256,128]{1,0:T(8,128)}, /*index=5*...) custom-call(s32[1,128,256]{2,1,0:T(8,128)} %col.1, s32[1,128,256]{2,1,0:T(8,128)} %lev.1, s32[1,128,256]{2,1,0:T(8,128)} %tub.1, ...), custom_call_target="tpu_custom_call" | custom-call | tf_op jit(solution)/shard_map/sort/pallas_call | solution.py:89
  6.1 12.8 %first.1 = f32[128,4,128]{2,1,0:T(4,128)} custom-call(s32[32,128]{1,0:T(8,128)} %get-tuple-element.22.bnd, s32[256,128]{1,0:T(8,128)} %get-tuple-element.23.cell, s32[128,256]{1,0:T(8,128)} %get-tuple-element.29.inv, f32[2,512,128]{2,1,0:T(8,128)} %bitcast.5), custom_call_target="tpu_custom_call" | custom-call | tf_op jit(solution)/shard_map/first/pallas_call | solution.py:280
  18.9 10.0 %all-to-all-start = ((f32[128,4,128]{2,1,0:T(4,128)}), f32[128,4,128]{2,1,0:T(4,128)S(1)}, u32[]{:S(2)}, u32[]{:S(2)}) async-start(f32[128,4,128]{2,1,0:T(4,128)} %first.1), calls=%async_computation | async-start | bytes 524288 | tf_op jit(solution)/shard_map/all_to_all | solution.py:301
  28.9 0.2 dynamic-slice_reduce_fusion
  29.1 0.7 bitcast_select_fusion.gain.a_4_
  29.9 7.1 %all-to-all-done.wire = f32[128,4,128]{2,1,0:T(4,128)S(1)} async-done(((f32[128,4,128]{2,1,0:T(4,128)}), f32[128,4,128]{2,1,0:T(4,128)S(1)}, u32[]{:S(2)}, u32[]{:S(2)}) %all-to-all-start) | async-done | bytes 262176 | tf_op jit(solution)/shard_map/all_to_all | solution.py:301
  37.0 0.7 copy-done.15
  37.6 0.7 broadcast_in_dim.4.drift.a_5_
  38.3 12.3 %tube.2 = (f32[2,128,512]{2,1,0:T(8,128)}, f32[2,128,512]{2,1,0:T(8,128)}, f32[2,1,512]{2,1,0:T(1,128)}) custom-call(s32[32,128]{1,0:T(8,128)} %get-tuple-element.25.bnd.a_0_, f32[2,2]{1,0:T(2,128)} %coupling.3, s32[256,128]{1,0:T(8,128)} %get-tuple-element.26.cell.a_2_, s32[128,256]{1,0:T(8,128)} %get-tuple-element.28.pos, ...), custom_call_target="tpu_custom_call" | custom-call | tf_op jit(solution)/shard_map/tube/pallas_call | solution.py:280
  50.6 2.9 %collective-permute-start = (f32[2,1,512]{2,1,0:T(1,128)}, f32[2,1,512]{2,1,0:T(1,128)S(1)}, u32[]{:S(2)}, u32[]{:S(2)}) collective-permute-start(f32[2,1,512]{2,1,0:T(1,128)} %get-tuple-element.32), channel_id=1, source_target_pairs={{0,1},{1,2},{2,3},{3,4},{4,5},{5,6},{6,7},{7,8},{8,9},{9,10},{10,1... | collective-permute-start | bytes 12296 | tf_op jit(solution)/shard_map/ppermute | solution.py:341
  53.5 0.9 collective-permute-done.a_8_
  54.5 0.6 copy-done.14
  55.1 12.6 %drag.2 = (f32[2,128,512]{2,1,0:T(8,128)}, f32[128,4,128]{2,1,0:T(4,128)}) custom-call(s32[32,128]{1,0:T(8,128)} %get-tuple-element.25.bnd.a_0_, f32[2]{0:T(128)} %a_1_.3, s32[256,128]{1,0:T(8,128)} %get-tuple-element.26.cell.a_2_, s32[128,256]{1,0:T(8,128)} %get-tuple-element.27.a_3_, f32[128,256]{1,0:T(8,128)} %bitcast_select_fusion.gain.a_4_, ...), custom_call_target="tpu_custom_call" | custom-call | tf_op jit(solution)/shard_map/drag/pallas_call | solution.py:280
  67.7 10.9 %all-to-all-start.1 = ((f32[128,4,128]{2,1,0:T(4,128)}), f32[128,4,128]{2,1,0:T(4,128)S(1)}, u32[]{:S(2)}, u32[]{:S(2)}) async-start(f32[128,4,128]{2,1,0:T(4,128)} %get-tuple-element.33), calls=%async_computation.1 | async-start | bytes 524288 | tf_op jit(solution)/shard_map/all_to_all | solution.py:301
  78.6 0.8 fusion.3
  79.4 3.3 %collective-permute-start.1 = (f32[2,1,32,128]{3,2,1,0:T(8,128)S(1)}, f32[2,1,32,128]{3,2,1,0:T(8,128)S(1)}, u32[]{:S(2)}, u32[]{:S(2)}) collective-permute-start(f32[2,1,32,128]{3,2,1,0:T(8,128)S(1)} %get-tuple-element.49), channel_id=1, source_target_pairs={{0,16},{16,32},{32,48},{48,64},{64,80},{80,96},{96,112},{1,17},{17... | collective-permute-start | bytes 98312 | tf_op jit(solution)/shard_map/ppermute | solution.py:295
  82.7 5.5 %collective-permute-start.2 = (f32[2,1,32,128]{3,2,1,0:T(8,128)S(1)}, f32[2,1,32,128]{3,2,1,0:T(8,128)S(1)}, u32[]{:S(2)}, u32[]{:S(2)}) collective-permute-start(f32[2,1,32,128]{3,2,1,0:T(8,128)S(1)} %get-tuple-element.48), channel_id=1, source_target_pairs={{16,0},{32,16},{48,32},{64,48},{80,64},{96,80},{112,96},{17,1},{33... | collective-permute-start | bytes 98312 | tf_op jit(solution)/shard_map/ppermute | solution.py:296
  88.3 1.0 fusion.2
  89.3 4.0 %collective-permute-start.3 = (f32[2,16,1,128]{3,2,1,0:T(1,128)S(1)}, f32[2,16,1,128]{3,2,1,0:T(1,128)S(1)}, u32[]{:S(2)}, u32[]{:S(2)}) collective-permute-start(f32[2,16,1,128]{3,2,1,0:T(1,128)S(1)} %get-tuple-element.47), channel_id=1, source_target_pairs={{0,1},{1,2},{2,3},{3,4},{4,5},{5,6},{6,7},{7,8},{8,9},{9,10},{10,1... | collective-permute-start | bytes 49160 | tf_op jit(solution)/shard_map/ppermute | solution.py:295
  93.3 1.9 collective-permute-start.4
  95.2 0.0 collective-permute-done.3.ylo
  95.2 4.0 %collective-permute-done.4.yhi = f32[2,16,1,128]{3,2,1,0:T(1,128)S(1)} collective-permute-done((f32[2,16,1,128]{3,2,1,0:T(1,128)S(1)}, f32[2,16,1,128]{3,2,1,0:T(1,128)S(1)}, u32[]{:S(2)}, u32[]{:S(2)}) %collective-permute-start.4) | collective-permute-done | bytes 16416 | tf_op jit(solution)/shard_map/ppermute | solution.py:296
  99.3 0.0 copy-start.2
  99.3 0.5 copy-done.11
  99.8 0.0 copy-done.5
  99.8 0.0 copy-done.7
  99.9 0.1 copy-done.2
  100.0 25.4 %mid.1 = (f32[2,512,128]{2,1,0:T(8,128)}, f32[128,4,128]{2,1,0:T(4,128)}) custom-call(s32[32,128]{1,0:T(8,128)} %get-tuple-element.22.bnd, s32[256,128]{1,0:T(8,128)} %get-tuple-element.23.cell, s32[128,256]{1,0:T(8,128)} %get-tuple-element.24.pos, s32[128,256]{1,0:T(8,128)} %get-tuple-element.29.inv, f32[128,4,128]{2,1,0:T(4,128)} %copy-done.2, ...), custom_call_target="tpu_custom_call" | custom-call | tf_op jit(solution)/shard_map/mid/pallas_call | solution.py:280
  125.3 14.4 %all_to_all.20.wire = f32[128,4,128]{2,1,0:T(4,128)} all-to-all(f32[128,4,128]{2,1,0:T(4,128)} %get-tuple-element.34), channel_id=1, replica_groups=mesh['gx'=8,'gy'=16] {'gx','gy'}, dimensions={0} | all-to-all | bytes 524288 | tf_op jit(solution)/shard_map/all_to_all | solution.py:301
  139.8 12.2 %tube.3 = (f32[2,128,512]{2,1,0:T(8,128)}, f32[2,128,512]{2,1,0:T(8,128)}, f32[2,1,512]{2,1,0:T(1,128)}) custom-call(s32[32,128]{1,0:T(8,128)} %get-tuple-element.25.bnd.a_0_, f32[2,2]{1,0:T(2,128)} %coupling.3, s32[256,128]{1,0:T(8,128)} %get-tuple-element.26.cell.a_2_, s32[128,256]{1,0:T(8,128)} %get-tuple-element.28.pos, ...), custom_call_target="tpu_custom_call" | custom-call | tf_op jit(solution)/shard_map/tube/pallas_call | solution.py:280
  152.0 3.0 %collective-permute-start.5 = (f32[2,1,512]{2,1,0:T(1,128)}, f32[2,1,512]{2,1,0:T(1,128)S(1)}, u32[]{:S(2)}, u32[]{:S(2)}) collective-permute-start(f32[2,1,512]{2,1,0:T(1,128)} %get-tuple-element.38), channel_id=1, source_target_pairs={{0,1},{1,2},{2,3},{3,4},{4,5},{5,6},{6,7},{7,8},{8,9},{9,10},{10,1... | collective-permute-start | bytes 12296 | tf_op jit(solution)/shard_map/ppermute | solution.py:341
  154.9 0.9 collective-permute-done.5.a_8_
  155.9 0.6 copy-done.13
  156.5 12.6 %drag.3 = (f32[2,128,512]{2,1,0:T(8,128)}, f32[128,4,128]{2,1,0:T(4,128)}) custom-call(s32[32,128]{1,0:T(8,128)} %get-tuple-element.25.bnd.a_0_, f32[2]{0:T(128)} %a_1_.3, s32[256,128]{1,0:T(8,128)} %get-tuple-element.26.cell.a_2_, s32[128,256]{1,0:T(8,128)} %get-tuple-element.27.a_3_, f32[128,256]{1,0:T(8,128)} %bitcast_select_fusion.gain.a_4_, ...), custom_call_target="tpu_custom_call" | custom-call | tf_op jit(solution)/shard_map/drag/pallas_call | solution.py:280
  169.1 11.0 %all-to-all-start.3 = ((f32[128,4,128]{2,1,0:T(4,128)}), f32[128,4,128]{2,1,0:T(4,128)S(1)}, u32[]{:S(2)}, u32[]{:S(2)}) async-start(f32[128,4,128]{2,1,0:T(4,128)} %get-tuple-element.39), calls=%async_computation.3 | async-start | bytes 524288 | tf_op jit(solution)/shard_map/all_to_all | solution.py:301
  180.1 0.8 fusion.1
  180.9 3.3 %collective-permute-start.6 = (f32[2,1,32,128]{3,2,1,0:T(8,128)S(1)}, f32[2,1,32,128]{3,2,1,0:T(8,128)S(1)}, u32[]{:S(2)}, u32[]{:S(2)}) collective-permute-start(f32[2,1,32,128]{3,2,1,0:T(8,128)S(1)} %get-tuple-element.45), channel_id=1, source_target_pairs={{0,16},{16,32},{32,48},{48,64},{64,80},{80,96},{96,112},{1,17},{17... | collective-permute-start | bytes 98312 | tf_op jit(solution)/shard_map/ppermute | solution.py:295
  184.2 5.5 %collective-permute-start.7 = (f32[2,1,32,128]{3,2,1,0:T(8,128)S(1)}, f32[2,1,32,128]{3,2,1,0:T(8,128)S(1)}, u32[]{:S(2)}, u32[]{:S(2)}) collective-permute-start(f32[2,1,32,128]{3,2,1,0:T(8,128)S(1)} %get-tuple-element.44), channel_id=1, source_target_pairs={{16,0},{32,16},{48,32},{64,48},{80,64},{96,80},{112,96},{17,1},{33... | collective-permute-start | bytes 98312 | tf_op jit(solution)/shard_map/ppermute | solution.py:296
  189.8 1.0 fusion
  190.8 4.0 %collective-permute-start.8 = (f32[2,16,1,128]{3,2,1,0:T(1,128)S(1)}, f32[2,16,1,128]{3,2,1,0:T(1,128)S(1)}, u32[]{:S(2)}, u32[]{:S(2)}) collective-permute-start(f32[2,16,1,128]{3,2,1,0:T(1,128)S(1)} %get-tuple-element.43), channel_id=1, source_target_pairs={{0,1},{1,2},{2,3},{3,4},{4,5},{5,6},{6,7},{7,8},{8,9},{9,10},{10,1... | collective-permute-start | bytes 49160 | tf_op jit(solution)/shard_map/ppermute | solution.py:295
  194.7 1.9 collective-permute-start.9
  196.7 4.0 %collective-permute-done.9.yhi = f32[2,16,1,128]{3,2,1,0:T(1,128)S(1)} collective-permute-done((f32[2,16,1,128]{3,2,1,0:T(1,128)S(1)}, f32[2,16,1,128]{3,2,1,0:T(1,128)S(1)}, u32[]{:S(2)}, u32[]{:S(2)}) %collective-permute-start.9) | collective-permute-done | bytes 16416 | tf_op jit(solution)/shard_map/ppermute | solution.py:296
  200.7 0.6 copy-done.12
  201.3 0.0 copy-done.6
  201.3 0.0 copy-done.8
  201.3 0.7 copy-done.1
  202.0 14.7 %end.1 = f32[2,16,32,128]{3,2,1,0:T(8,128)} custom-call(s32[32,128]{1,0:T(8,128)} %get-tuple-element.22.bnd, s32[256,128]{1,0:T(8,128)} %get-tuple-element.23.cell, s32[128,256]{1,0:T(8,128)} %get-tuple-element.24.pos, f32[128,4,128]{2,1,0:T(4,128)} %copy-done.1, f32[2,16,32,128]{3,2,1,0:T(8,128)} %start.1, f32[2,16,32,128]{3,2,1,0:T(8,128)} %bitcast.8, ...), custom_call_target="tpu_custom_call" | custom-call | tf_op jit(solution)/shard_map/end/pallas_call | solution.py:280
  (26 shorter events, 0.1 us)
Async XLA Ops:
  0.6 28.3 %copy-start = (s32[128,128]{1,0:T(8,128)S(1)}, s32[128,128]{1,0:T(8,128)}, u32[]{:S(2)}) copy-start(s32[128,128]{1,0:T(8,128)} %param.27) | copy-start | bytes 196612
  18.9 10.2 %copy-start.4 = (f32[1,128,256]{2,1,0:T(8,128)S(1)}, f32[1,128,256]{2,1,0:T(8,128)}, u32[]{:S(2)}) copy-start(f32[1,128,256]{2,1,0:T(8,128)} %param.26) | copy-start | bytes 393220
  18.9 18.1 %all-to-all-start = ((f32[128,4,128]{2,1,0:T(4,128)}), f32[128,4,128]{2,1,0:T(4,128)S(1)}, u32[]{:S(2)}, u32[]{:S(2)}) async-start(f32[128,4,128]{2,1,0:T(4,128)} %first.1), calls=%async_computation | async-start | bytes 524288 | tf_op jit(solution)/shard_map/all_to_all | solution.py:301
  37.0 1.4 copy-start.3
  37.0 0.7 copy-start.15
  50.6 3.9 %collective-permute-start = (f32[2,1,512]{2,1,0:T(1,128)}, f32[2,1,512]{2,1,0:T(1,128)S(1)}, u32[]{:S(2)}, u32[]{:S(2)}) collective-permute-start(f32[2,1,512]{2,1,0:T(1,128)} %get-tuple-element.32), channel_id=1, source_target_pairs={{0,1},{1,2},{2,3},{3,4},{4,5},{5,6},{6,7},{7,8},{8,9},{9,10},{10,1... | collective-permute-start | bytes 12296 | tf_op jit(solution)/shard_map/ppermute | solution.py:341
  54.5 0.6 copy-start.14
  67.7 31.6 %all-to-all-start.1 = ((f32[128,4,128]{2,1,0:T(4,128)}), f32[128,4,128]{2,1,0:T(4,128)S(1)}, u32[]{:S(2)}, u32[]{:S(2)}) async-start(f32[128,4,128]{2,1,0:T(4,128)} %get-tuple-element.33), calls=%async_computation.1 | async-start | bytes 524288 | tf_op jit(solution)/shard_map/all_to_all | solution.py:301
  79.4 19.8 %collective-permute-start.1 = (f32[2,1,32,128]{3,2,1,0:T(8,128)S(1)}, f32[2,1,32,128]{3,2,1,0:T(8,128)S(1)}, u32[]{:S(2)}, u32[]{:S(2)}) collective-permute-start(f32[2,1,32,128]{3,2,1,0:T(8,128)S(1)} %get-tuple-element.49), channel_id=1, source_target_pairs={{0,16},{16,32},{32,48},{48,64},{64,80},{80,96},{96,112},{1,17},{17... | collective-permute-start | bytes 98312 | tf_op jit(solution)/shard_map/ppermute | solution.py:295
  82.7 16.5 %collective-permute-start.2 = (f32[2,1,32,128]{3,2,1,0:T(8,128)S(1)}, f32[2,1,32,128]{3,2,1,0:T(8,128)S(1)}, u32[]{:S(2)}, u32[]{:S(2)}) collective-permute-start(f32[2,1,32,128]{3,2,1,0:T(8,128)S(1)} %get-tuple-element.48), channel_id=1, source_target_pairs={{16,0},{32,16},{48,32},{64,48},{80,64},{96,80},{112,96},{17,1},{33... | collective-permute-start | bytes 98312 | tf_op jit(solution)/shard_map/ppermute | solution.py:296
  89.3 5.9 %collective-permute-start.3 = (f32[2,16,1,128]{3,2,1,0:T(1,128)S(1)}, f32[2,16,1,128]{3,2,1,0:T(1,128)S(1)}, u32[]{:S(2)}, u32[]{:S(2)}) collective-permute-start(f32[2,16,1,128]{3,2,1,0:T(1,128)S(1)} %get-tuple-element.47), channel_id=1, source_target_pairs={{0,1},{1,2},{2,3},{3,4},{4,5},{5,6},{6,7},{7,8},{8,9},{9,10},{10,1... | collective-permute-start | bytes 49160 | tf_op jit(solution)/shard_map/ppermute | solution.py:295
  93.3 6.0 %collective-permute-start.4 = (f32[2,16,1,128]{3,2,1,0:T(1,128)S(1)}, f32[2,16,1,128]{3,2,1,0:T(1,128)S(1)}, u32[]{:S(2)}, u32[]{:S(2)}) collective-permute-start(f32[2,16,1,128]{3,2,1,0:T(1,128)S(1)} %get-tuple-element.46), channel_id=1, source_target_pairs={{1,0},{2,1},{3,2},{4,3},{5,4},{6,5},{7,6},{8,7},{9,8},{10,9},{11,1... | collective-permute-start | bytes 49160 | tf_op jit(solution)/shard_map/ppermute | solution.py:296
  95.2 4.1 %copy-start.9 = (f32[2,16,1,128]{3,2,1,0:T(1,128)}, f32[2,16,1,128]{3,2,1,0:T(1,128)S(1)}, u32[]{:S(2)}) copy-start(f32[2,16,1,128]{3,2,1,0:T(1,128)S(1)} %collective-permute-done.3.ylo) | copy-start | bytes 49156
  99.2 0.6 copy-start.11
  99.2 0.6 copy-start.5
  99.2 0.6 copy-start.7
  99.3 0.7 copy-start.2
  152.0 3.9 %collective-permute-start.5 = (f32[2,1,512]{2,1,0:T(1,128)}, f32[2,1,512]{2,1,0:T(1,128)S(1)}, u32[]{:S(2)}, u32[]{:S(2)}) collective-permute-start(f32[2,1,512]{2,1,0:T(1,128)} %get-tuple-element.38), channel_id=1, source_target_pairs={{0,1},{1,2},{2,3},{3,4},{4,5},{5,6},{6,7},{7,8},{8,9},{9,10},{10,1... | collective-permute-start | bytes 12296 | tf_op jit(solution)/shard_map/ppermute | solution.py:341
  155.9 0.6 copy-start.13
  169.1 31.6 %all-to-all-start.3 = ((f32[128,4,128]{2,1,0:T(4,128)}), f32[128,4,128]{2,1,0:T(4,128)S(1)}, u32[]{:S(2)}, u32[]{:S(2)}) async-start(f32[128,4,128]{2,1,0:T(4,128)} %get-tuple-element.39), calls=%async_computation.3 | async-start | bytes 524288 | tf_op jit(solution)/shard_map/all_to_all | solution.py:301
  180.9 19.8 %collective-permute-start.6 = (f32[2,1,32,128]{3,2,1,0:T(8,128)S(1)}, f32[2,1,32,128]{3,2,1,0:T(8,128)S(1)}, u32[]{:S(2)}, u32[]{:S(2)}) collective-permute-start(f32[2,1,32,128]{3,2,1,0:T(8,128)S(1)} %get-tuple-element.45), channel_id=1, source_target_pairs={{0,16},{16,32},{32,48},{48,64},{64,80},{80,96},{96,112},{1,17},{17... | collective-permute-start | bytes 98312 | tf_op jit(solution)/shard_map/ppermute | solution.py:295
  184.2 16.5 %collective-permute-start.7 = (f32[2,1,32,128]{3,2,1,0:T(8,128)S(1)}, f32[2,1,32,128]{3,2,1,0:T(8,128)S(1)}, u32[]{:S(2)}, u32[]{:S(2)}) collective-permute-start(f32[2,1,32,128]{3,2,1,0:T(8,128)S(1)} %get-tuple-element.44), channel_id=1, source_target_pairs={{16,0},{32,16},{48,32},{64,48},{80,64},{96,80},{112,96},{17,1},{33... | collective-permute-start | bytes 98312 | tf_op jit(solution)/shard_map/ppermute | solution.py:296
  190.8 5.9 %collective-permute-start.8 = (f32[2,16,1,128]{3,2,1,0:T(1,128)S(1)}, f32[2,16,1,128]{3,2,1,0:T(1,128)S(1)}, u32[]{:S(2)}, u32[]{:S(2)}) collective-permute-start(f32[2,16,1,128]{3,2,1,0:T(1,128)S(1)} %get-tuple-element.43), channel_id=1, source_target_pairs={{0,1},{1,2},{2,3},{3,4},{4,5},{5,6},{6,7},{7,8},{8,9},{9,10},{10,1... | collective-permute-start | bytes 49160 | tf_op jit(solution)/shard_map/ppermute | solution.py:295
  194.7 6.0 %collective-permute-start.9 = (f32[2,16,1,128]{3,2,1,0:T(1,128)S(1)}, f32[2,16,1,128]{3,2,1,0:T(1,128)S(1)}, u32[]{:S(2)}, u32[]{:S(2)}) collective-permute-start(f32[2,16,1,128]{3,2,1,0:T(1,128)S(1)} %get-tuple-element.42), channel_id=1, source_target_pairs={{1,0},{2,1},{3,2},{4,3},{5,4},{6,5},{7,6},{8,7},{9,8},{10,9},{11,1... | collective-permute-start | bytes 49160 | tf_op jit(solution)/shard_map/ppermute | solution.py:296
  196.7 4.1 %copy-start.10 = (f32[2,16,1,128]{3,2,1,0:T(1,128)}, f32[2,16,1,128]{3,2,1,0:T(1,128)S(1)}, u32[]{:S(2)}) copy-start(f32[2,16,1,128]{3,2,1,0:T(1,128)S(1)} %collective-permute-done.8.ylo) | copy-start | bytes 49156
  200.7 0.6 copy-start.12
  200.7 0.6 copy-start.6
  200.7 0.6 copy-start.8
  201.3 0.7 copy-start.1

commit v3 on v2

--- a/solution.py
+++ b/solution.py
@@ -75,18 +75,36 @@
     lane = lax.broadcasted_iota(i32, (C//8, 128), 1)
     bnd_ref[...] = jnp.where(lane == 0, lo, hi)
 
-def sort_kernel(col, lev, tub, pnt, cellA, posA, invA, bndA, cellB, posB, invB, bndB):
-    def key(row, lane):
-        return ((row & 255) << 8) + ((row >> 8) << 7) + lane
-
-    sort_side(key(col[0], lev[0]), cellA, posA, invA, bndA)
+def cell_key(row, lane):
+    return ((row & 255) << 8) + ((row >> 8) << 7) + lane
+
+
+def put_edges(get, xa, xb, ya, yb):
+    for k in range(2):
+        xa[k, 0] = get(k, 0)
+        n = ya.shape[1]
+        xb[k, 0] = get(k, n-1)
+        for i in range(n):
+            u = get(k, i)
+            ya[k, i] = u[:1]
+            yb[k, i] = u[-1:]
+
+
+def tile_sort_kernel(col, lev, wind, cell, pos, inv, bnd, *edge):
+    sort_side(cell_key(col[0], lev[0]), cell, pos, inv, bnd)
+    put_edges(lambda k, i: wind[k, i], *edge)
+
+
+def tube_sort_kernel(tub, pnt, weight, count, drift, cell, pos, inv, bnd, gain, drift_out):
     p = pnt[0]
-    sort_side(key((p >> 7)*128 + tub[0], p & 127), cellB, posB, invB, bndB)
-
-def sort_call(col, lev, tub, pnt):
-    P, C = col.shape[1:]
-    side = [jax.ShapeDtypeStruct((C, P), i32), jax.ShapeDtypeStruct((P, C), i32), jax.ShapeDtypeStruct((P, C), i32), jax.ShapeDtypeStruct((C//8, 128), i32)]
-    return pl.pallas_call(sort_kernel, out_shape=side*2, in_specs=[VM]*4, out_specs=[VM]*8, name="sort")(col, lev, tub, pnt)
+    sort_side(cell_key((p >> 7)*128 + tub[0], p & 127), cell, pos, inv, bnd)
+    own = lax.axis_index("gx") * lax.axis_size("gy") + lax.axis_index("gy")
+    lane = lax.broadcasted_iota(i32, (128, 128), 1)
+    live = jnp.sum(jnp.where(lane == own, count[...], 0).astype(f32), axis=1, keepdims=True)
+    c = lax.broadcasted_iota(i32, (128, 256), 1).astype(f32)
+    gain[...] = jnp.where(c < live, weight[0], 0.0)
+    drift_out[...] = jnp.broadcast_to(drift[...], (128, 128)).T
+
 
 def permute_lanes(x, idx):
     outs = []
@@ -253,7 +271,7 @@
             emit(k, i, u, v * (b - 6.0 * u) + acc[k, (i*CY) % 256:(i*CY) % 256 + CY, (i*CY)//256*128:(i*CY)//256*128 + 128] + forcing[k, i])
 
 
-def mid_kernel(bnd, cell, pos, inv, wire, wind, forcing, visc, xlo, xhi, ylo, yhi, mid, wire_out, val, acc, s):
+def mid_kernel(bnd, cell, pos, inv, wire, wind, forcing, visc, xlo, xhi, ylo, yhi, mid, wire_out, xa, xb, ya, yb, val, acc, s):
     from_wire(pos, wire, val)
     scatter_add(bnd, cell, val, acc)
     CY = wind.shape[2]
@@ -262,6 +280,7 @@
         mid[k, i*CY:(i+1)*CY, :] = u + neutral_step * f
 
     tend_all(wind, forcing, visc, xlo, xhi, ylo, yhi, acc, emit)
+    put_edges(lambda k, i: mid[k, i*CY:(i+1)*CY, :], xa, xb, ya, yb)
     lookup(bnd, cell, mid, s)
     to_wire(inv, s, wire_out)
 
@@ -287,14 +306,14 @@
     )(*args)
 
 
-def edges(wind):
-    out = []
-    for axis, dim in (("gx", 1), ("gy", 2)):
-        peers, length = lax.axis_size(axis), wind.shape[dim]
-        up = [(i, i + 1) for i in range(peers - 1)]
-        out.append(lax.ppermute(lax.slice_in_dim(wind, length - 1, length, axis=dim), axis, up))
-        out.append(lax.ppermute(lax.slice_in_dim(wind, 0, 1, axis=dim), axis, [(b, a) for a, b in up]))
-    return out
+def beside(axis, first, last):
+    peers = lax.axis_size(axis)
+    up = [(i, i + 1) for i in range(peers - 1)]
+    return [lax.ppermute(last, axis, up), lax.ppermute(first, axis, [(b, a) for a, b in up])]
+
+
+def tied(*arrays):
+    return lax.optimization_barrier(arrays)
 
 
 def exchange(x):
@@ -317,12 +336,6 @@
     recv_weight,
     pair_count,
 ):
-    own = lax.axis_index(("gx", "gy"))
-    cap = recv_weight.shape[2]
-    incoming = lax.dynamic_slice_in_dim(pair_count, own, 1, 1)
-    position = lax.broadcasted_iota(i32, (128, cap), 1)
-    gain = recv_weight[0] * (position < incoming).astype(f32)
-    drift = jnp.broadcast_to(drift_fraction[:, None], (128, 128))
     visc = viscosity[None, :]
     sd = jax.ShapeDtypeStruct
     wire_t = sd((128, 4, 128), f32)
@@ -330,31 +343,50 @@
     vals = pltpu.VMEM((2, 256, 128), f32)
     accs = pltpu.VMEM((2, 256 + W, 256), f32)
     tabs = pltpu.VMEM((2, 512, 128), f32)
-    cA, pA, iA, bA, cB, pB, iB, bB = sort_call(outgoing_column, send_level, recv_tube, recv_point)
     flat = (2, 512, 128)
     up_route = [(i, i + 1) for i in range(lax.axis_size("gy") - 1)]
-
-    def tubes(wire, ions, last):
+    CX, CY = neutral_wind.shape[1:3]
+    edge_t = (sd((2, 1, CY, 128), f32),)*2 + (sd((2, CX, 1, 128), f32),)*2
+    side_t = (sd((256, 128), i32), sd((128, 256), i32), sd((128, 256), i32), sd((32, 128), i32))
+
+    cA, pA, iA, bA, xa, xb, ya, yb = call(
+        tile_sort_kernel, side_t + edge_t, [], outgoing_column, send_level, neutral_wind, smem=0, name="tilesort")
+    wire = call(gather_kernel, wire_t, [vals], bA, cA, iA, neutral_wind.reshape(flat), name="first")
+    came = exchange(wire)
+    wire, tub, xa, xb = tied(wire, recv_tube, xa, xb)
+    cB, pB, iB, bB, gain, drift = call(
+        tube_sort_kernel, side_t + (sd((128, 256), f32), sd((128, 128), f32)), [],
+        tub, recv_point, recv_weight, pair_count, drift_fraction[None, :], smem=0, name="tubesort")
+    halo = beside("gx", xa, xb)
+    came, *halo = tied(came, *halo)
+
+    def tubes(came, ions, last):
         w, smooth, out_last = call(
             tube_kernel, (tube_t, tube_t, sd((2, 1, 512), f32)), [vals, accs],
-            bB, coupling, cB, pB, gain, drift, wire, ions, inverse, smem=2, name="tube")
+            bB, coupling, cB, pB, gain, drift, came, ions, inverse, smem=2, name="tube")
         up = lax.ppermute(out_last, "gy", up_route)
         return call(
             lambda *a: drag_kernel(last, *a), (tube_t, wire_t), [tabs, vals],
             bB, drag_rate, cB, iB, gain, drift, w, smooth, up, ion_density, smem=2, name="drag")
 
-    halo = edges(neutral_wind)
-    wire = call(gather_kernel, wire_t, [vals], bA, cA, iA, neutral_wind.reshape(flat), name="first")
-    n1, wire = tubes(exchange(wire), ion_density, False)
-    mid, wire = call(
-        mid_kernel, (sd(flat, f32), wire_t), [vals, accs, vals],
-        bA, cA, pA, iA, exchange(wire), neutral_wind, forcing, visc, *halo, name="mid")
+    n1, wire = tubes(came, ion_density, False)
+    came = exchange(wire)
+    wire, ya, yb = tied(wire, ya, yb)
+    halo += beside("gy", ya, yb)
+    mid, wire, xa, xb, ya, yb = call(
+        mid_kernel, (sd(flat, f32), wire_t) + edge_t, [vals, accs, vals],
+        bA, cA, pA, iA, came, neutral_wind, forcing, visc, *halo, name="mid")
     mid = mid.reshape(neutral_wind.shape)
-    halo = edges(mid)
-    ion_out, wire = tubes(exchange(wire), n1, True)
+    came = exchange(wire)
+    halo = beside("gx", xa, xb)
+    came, *halo = tied(came, *halo)
+    ion_out, wire = tubes(came, n1, True)
+    came = exchange(wire)
+    wire, ya, yb = tied(wire, ya, yb)
+    halo += beside("gy", ya, yb)
     wind_out = call(
         end_kernel, sd(neutral_wind.shape, f32), [vals, accs],
-        bA, cA, pA, exchange(wire), neutral_wind, mid, forcing, visc, *halo, name="end")
+        bA, cA, pA, came, neutral_wind, mid, forcing, visc, *halo, name="end")
     return (wind_out, ion_out)
 
 

time: 216 us -> 207 us (0.958)
  the two profiles are of different devices: /device:TPU:23 before, /device:TPU:1 now
where the time goes in v3:
time: 207 us; the launch traced here: 204 us
  Pallas kernels  103 us (50%)
  starting transfers between devices  74.2 us (36%)
  waiting for transfers between devices  21.7 us (10%)
  local copies, waits for them, and re-layouts  4.05 us (2%)
    pallas_call x9, Pallas kernels, call(): pl.pallas_call(kernel, out_shape=outs, in_specs=[SM] * smem + [VM] * (len...  103 us
    all_to_all x4, starting transfers between devices, exchange(): lax.all_to_all(x, ('gx', 'gy'), split_axis=0, concat_axis=0, tiled=True)  47.1 us
    ppermute x4, starting transfers between devices, beside(): lax.ppermute(last, axis, up)  13.9 us
    ppermute x4, waiting for transfers between devices, beside(): lax.ppermute(first, axis, [(b, a) for a, b in up])  10.5 us
    all_to_all x4, waiting for transfers between devices, exchange(): lax.all_to_all(x, ('gx', 'gy'), split_axis=0, concat_axis=0, tiled=True)  9.23 us
    ppermute x4, starting transfers between devices, beside(): lax.ppermute(first, axis, [(b, a) for a, b in up])  6.61 us
    ppermute x2, starting transfers between devices, tubes(): up = lax.ppermute(out_last, 'gy', up_route)  6.6 us
  transfers between devices with their start and end apart: 14, of which 10 were waited for; matrix products, arithmetic and copies ran while one was open for 0% of the time, Pallas kernels for 2%

profile of v3, /device:TPU:1, one launch (start us, length us, event | category | flops | bytes accessed | tf_op | source)
XLA Modules:
  0.0 203.5 jit_solution(17982249239294613702)
XLA Ops:
  0.6 3.7 %tilesort.1 = (s32[256,128]{1,0:T(8,128)}, s32[128,256]{1,0:T(8,128)}, s32[128,256]{1,0:T(8,128)}, s32[32,128]{1,0:T(8,128)}, f32[2,1,32,128]{3,2,1,0:T(8,128)},...) custom-call(s32[1,128,256]{2,1,0:T(8,128)} %col.1, s32[1,128,256]{2,1,0:T(8,128)} %lev.1, ...), custom_call_target="tpu_custom_call" | custom-call | tf_op jit(solution)/shard_map/tilesort/pallas_call | solution.py:299
  4.4 11.3 %first.1 = f32[128,4,128]{2,1,0:T(4,128)} custom-call(s32[32,128]{1,0:T(8,128)} %get-tuple-element.45.bnd, s32[256,128]{1,0:T(8,128)} %get-tuple-element.46.cell, s32[128,256]{1,0:T(8,128)} %get-tuple-element.48.inv, f32[2,512,128]{2,1,0:T(8,128)} %bitcast.4), custom_call_target="tpu_custom_call" | custom-call | tf_op jit(solution)/shard_map/first/pallas_call | solution.py:299
  15.7 12.6 %all-to-all-start = ((f32[128,4,128]{2,1,0:T(4,128)}), f32[128,4,128]{2,1,0:T(4,128)S(1)}, u32[]{:S(2)}, u32[]{:S(2)}) async-start(f32[128,4,128]{2,1,0:T(4,128)} %first.1), calls=%async_computation | async-start | bytes 524288 | tf_op jit(solution)/shard_map/all_to_all | solution.py:320
  28.3 0.0 copy-done.15
  28.3 3.4 %collective-permute-start = (f32[2,1,32,128]{3,2,1,0:T(8,128)S(1)}, f32[2,1,32,128]{3,2,1,0:T(8,128)S(1)}, u32[]{:S(2)}, u32[]{:S(2)}) collective-permute-start(f32[2,1,32,128]{3,2,1,0:T(8,128)S(1)} %copy-done.15), channel_id=1, source_target_pairs={{0,16},{16,32},{32,48},{48,64},{64,80},{80,96},{96,112},{1,17},{17... | collective-permute-start | bytes 98312 | tf_op jit(solution)/shard_map/ppermute | solution.py:312
  31.7 1.3 collective-permute-start.1
  33.0 3.7 %tubesort.1 = (s32[256,128]{1,0:T(8,128)}, s32[128,256]{1,0:T(8,128)}, s32[128,256]{1,0:T(8,128)}, s32[32,128]{1,0:T(8,128)}, f32[128,256]{1,0:T(8,128)}, /*index=5*/f32[128,128]{1,0:T(8,128)}) custom-call(s32[1,128,256]{2,1,0:T(8,128)} %tub, s32[1,128,256]{2,1,0:T(8,128)} %pnt.1, f32[1,128,256]{2,1,0:T(8,128)} %weight.1, s32[128,128]{1,0:T(8,128)} %count.1, ...), custom_call_target="tpu_custom_call" | custom-call | tf_op jit(solution)/shard_map/tubesort/pallas_call | solution.py:299
  36.7 0.0 collective-permute-done.xlo
  36.7 0.1 collective-permute-done.1.xhi
  36.8 2.5 %all-to-all-done.wire = f32[128,4,128]{2,1,0:T(4,128)S(1)} async-done(((f32[128,4,128]{2,1,0:T(4,128)}), f32[128,4,128]{2,1,0:T(4,128)S(1)}, u32[]{:S(2)}, u32[]{:S(2)}) %all-to-all-start) | async-done | bytes 262176 | tf_op jit(solution)/shard_map/all_to_all | solution.py:320
  39.3 0.7 copy-done.2
  40.0 12.7 %tube.2 = (f32[2,128,512]{2,1,0:T(8,128)}, f32[2,128,512]{2,1,0:T(8,128)}, f32[2,1,512]{2,1,0:T(1,128)}) custom-call(s32[32,128]{1,0:T(8,128)} %get-tuple-element.52.bnd.a_0_, f32[2,2]{1,0:T(2,128)} %coupling.3, s32[256,128]{1,0:T(8,128)} %get-tuple-element.53.cell.a_2_, s32[128,256]{1,0:T(8,128)} %get-tuple-element.57.pos, ...), custom_call_target="tpu_custom_call" | custom-call | tf_op jit(solution)/shard_map/tube/pallas_call | solution.py:299
  52.8 3.3 %collective-permute-start.2 = (f32[2,1,512]{2,1,0:T(1,128)}, f32[2,1,512]{2,1,0:T(1,128)S(1)}, u32[]{:S(2)}, u32[]{:S(2)}) collective-permute-start(f32[2,1,512]{2,1,0:T(1,128)} %get-tuple-element.63), channel_id=1, source_target_pairs={{0,1},{1,2},{2,3},{3,4},{4,5},{5,6},{6,7},{7,8},{8,9},{9,10},{10,1... | collective-permute-start | bytes 12296 | tf_op jit(solution)/shard_map/ppermute | solution.py:367
  56.1 1.0 collective-permute-done.2.a_8_
  57.1 0.6 copy-done.13
  57.6 12.3 %drag.2 = (f32[2,128,512]{2,1,0:T(8,128)}, f32[128,4,128]{2,1,0:T(4,128)}) custom-call(s32[32,128]{1,0:T(8,128)} %get-tuple-element.52.bnd.a_0_, f32[2]{0:T(128)} %a_1_.3, s32[256,128]{1,0:T(8,128)} %get-tuple-element.53.cell.a_2_, s32[128,256]{1,0:T(8,128)} %get-tuple-element.54.a_3_, f32[128,256]{1,0:T(8,128)} %get-tuple-element.55.gain.a_4_, ...), custom_call_target="tpu_custom_call" | custom-call | tf_op jit(solution)/shard_map/drag/pallas_call | solution.py:299
  69.9 12.2 %all-to-all-start.1 = ((f32[128,4,128]{2,1,0:T(4,128)}), f32[128,4,128]{2,1,0:T(4,128)S(1)}, u32[]{:S(2)}, u32[]{:S(2)}) async-start(f32[128,4,128]{2,1,0:T(4,128)} %get-tuple-element.64), calls=%async_computation.1 | async-start | bytes 524288 | tf_op jit(solution)/shard_map/all_to_all | solution.py:320
  82.1 0.0 copy-done.21
  82.1 3.5 %collective-permute-start.3 = (f32[2,16,1,128]{3,2,1,0:T(1,128)S(1)}, f32[2,16,1,128]{3,2,1,0:T(1,128)S(1)}, u32[]{:S(2)}, u32[]{:S(2)}) collective-permute-start(f32[2,16,1,128]{3,2,1,0:T(1,128)S(1)} %copy-done.21), channel_id=1, source_target_pairs={{0,1},{1,2},{2,3},{3,4},{4,5},{5,6},{6,7},{7,8},{8,9},{9,10},{10,1... | collective-permute-start | bytes 49160 | tf_op jit(solution)/shard_map/ppermute | solution.py:312
  85.7 1.9 collective-permute-start.4
  87.6 0.0 collective-permute-done.3.ylo
  87.6 0.0 copy-start.8
  87.6 3.4 %collective-permute-done.4.yhi = f32[2,16,1,128]{3,2,1,0:T(1,128)S(1)} collective-permute-done((f32[2,16,1,128]{3,2,1,0:T(1,128)S(1)}, f32[2,16,1,128]{3,2,1,0:T(1,128)S(1)}, u32[]{:S(2)}, u32[]{:S(2)}) %collective-permute-start.4) | collective-permute-done | bytes 16416 | tf_op jit(solution)/shard_map/ppermute | solution.py:312
  91.0 2.1 %all-to-all-done.1.wire = f32[128,4,128]{2,1,0:T(4,128)S(1)} async-done(((f32[128,4,128]{2,1,0:T(4,128)}), f32[128,4,128]{2,1,0:T(4,128)S(1)}, u32[]{:S(2)}, u32[]{:S(2)}) %all-to-all-start.1) | async-done | bytes 262176 | tf_op jit(solution)/shard_map/all_to_all | solution.py:320
  93.2 0.7 copy-done.1
  93.9 21.6 %mid.1 = (f32[2,512,128]{2,1,0:T(8,128)}, f32[128,4,128]{2,1,0:T(4,128)}, f32[2,1,32,128]{3,2,1,0:T(8,128)}, f32[2,1,32,128]{3,2,1,0:T(8,128)}, f32[2,16,1,128]{3,2,1,0:T(1,128)}, /*index=5*/f32[2,16,1,128]{3,2,1,0:T(1,128)}) custom-call(s32[32,128]{1,0:T(8,128)} %get-tuple-element.45.bnd, s32[256,128]{1,0:T(8,128)} %get-tuple-element.46.cell, ...), custom_call_target="tpu_custom_call" | custom-call | tf_op jit(solution)/shard_map/mid/pallas_call | solution.py:299
  115.4 0.0 copy-start.16
  115.4 10.1 %all-to-all-start.2 = ((f32[128,4,128]{2,1,0:T(4,128)}), f32[128,4,128]{2,1,0:T(4,128)S(1)}, u32[]{:S(2)}, u32[]{:S(2)}) async-start(f32[128,4,128]{2,1,0:T(4,128)} %get-tuple-element.71), calls=%async_computation.2 | async-start | bytes 524288 | tf_op jit(solution)/shard_map/all_to_all | solution.py:320
  125.6 3.4 %collective-permute-start.5 = (f32[2,1,32,128]{3,2,1,0:T(8,128)S(1)}, f32[2,1,32,128]{3,2,1,0:T(8,128)S(1)}, u32[]{:S(2)}, u32[]{:S(2)}) collective-permute-start(f32[2,1,32,128]{3,2,1,0:T(8,128)S(1)} %copy-done.17), channel_id=1, source_target_pairs={{0,16},{16,32},{32,48},{48,64},{64,80},{80,96},{96,112},{1,17},{17... | collective-permute-start | bytes 98312 | tf_op jit(solution)/shard_map/ppermute | solution.py:312
  129.0 1.5 collective-permute-start.6
  130.5 0.0 collective-permute-done.5.xlo
  130.5 3.6 %collective-permute-done.6.xhi = f32[2,1,32,128]{3,2,1,0:T(8,128)S(1)} collective-permute-done((f32[2,1,32,128]{3,2,1,0:T(8,128)S(1)}, f32[2,1,32,128]{3,2,1,0:T(8,128)S(1)}, u32[]{:S(2)}, u32[]{:S(2)}) %collective-permute-start.6) | collective-permute-done | bytes 32800 | tf_op jit(solution)/shard_map/ppermute | solution.py:312
  134.1 2.5 %all-to-all-done.2.wire = f32[128,4,128]{2,1,0:T(4,128)S(1)} async-done(((f32[128,4,128]{2,1,0:T(4,128)}), f32[128,4,128]{2,1,0:T(4,128)S(1)}, u32[]{:S(2)}, u32[]{:S(2)}) %all-to-all-start.2) | async-done | bytes 262176 | tf_op jit(solution)/shard_map/all_to_all | solution.py:320
  136.6 0.7 copy-done.3
  137.3 12.7 %tube.3 = (f32[2,128,512]{2,1,0:T(8,128)}, f32[2,128,512]{2,1,0:T(8,128)}, f32[2,1,512]{2,1,0:T(1,128)}) custom-call(s32[32,128]{1,0:T(8,128)} %get-tuple-element.52.bnd.a_0_, f32[2,2]{1,0:T(2,128)} %coupling.3, s32[256,128]{1,0:T(8,128)} %get-tuple-element.53.cell.a_2_, s32[128,256]{1,0:T(8,128)} %get-tuple-element.57.pos, ...), custom_call_target="tpu_custom_call" | custom-call | tf_op jit(solution)/shard_map/tube/pallas_call | solution.py:299
  150.0 3.3 %collective-permute-start.7 = (f32[2,1,512]{2,1,0:T(1,128)}, f32[2,1,512]{2,1,0:T(1,128)S(1)}, u32[]{:S(2)}, u32[]{:S(2)}) collective-permute-start(f32[2,1,512]{2,1,0:T(1,128)} %get-tuple-element.78), channel_id=1, source_target_pairs={{0,1},{1,2},{2,3},{3,4},{4,5},{5,6},{6,7},{7,8},{8,9},{9,10},{10,1... | collective-permute-start | bytes 12296 | tf_op jit(solution)/shard_map/ppermute | solution.py:367
  153.3 1.0 collective-permute-done.7.a_8_
  154.3 0.6 copy-done.12
  154.9 12.3 %drag.3 = (f32[2,128,512]{2,1,0:T(8,128)}, f32[128,4,128]{2,1,0:T(4,128)}) custom-call(s32[32,128]{1,0:T(8,128)} %get-tuple-element.52.bnd.a_0_, f32[2]{0:T(128)} %a_1_.3, s32[256,128]{1,0:T(8,128)} %get-tuple-element.53.cell.a_2_, s32[128,256]{1,0:T(8,128)} %get-tuple-element.54.a_3_, f32[128,256]{1,0:T(8,128)} %get-tuple-element.55.gain.a_4_, ...), custom_call_target="tpu_custom_call" | custom-call | tf_op jit(solution)/shard_map/drag/pallas_call | solution.py:299
  167.2 12.2 %all-to-all-start.3 = ((f32[128,4,128]{2,1,0:T(4,128)}), f32[128,4,128]{2,1,0:T(4,128)S(1)}, u32[]{:S(2)}, u32[]{:S(2)}) async-start(f32[128,4,128]{2,1,0:T(4,128)} %get-tuple-element.79), calls=%async_computation.3 | async-start | bytes 524288 | tf_op jit(solution)/shard_map/all_to_all | solution.py:320
  179.4 3.5 %collective-permute-start.8 = (f32[2,16,1,128]{3,2,1,0:T(1,128)S(1)}, f32[2,16,1,128]{3,2,1,0:T(1,128)S(1)}, u32[]{:S(2)}, u32[]{:S(2)}) collective-permute-start(f32[2,16,1,128]{3,2,1,0:T(1,128)S(1)} %copy-done.20), channel_id=1, source_target_pairs={{0,1},{1,2},{2,3},{3,4},{4,5},{5,6},{6,7},{7,8},{8,9},{9,10},{10,1... | collective-permute-start | bytes 49160 | tf_op jit(solution)/shard_map/ppermute | solution.py:312
  183.0 0.0 copy-done.18
  183.0 1.9 collective-permute-start.9
  184.9 0.0 collective-permute-done.8.ylo
  184.9 3.4 %collective-permute-done.9.yhi = f32[2,16,1,128]{3,2,1,0:T(1,128)S(1)} collective-permute-done((f32[2,16,1,128]{3,2,1,0:T(1,128)S(1)}, f32[2,16,1,128]{3,2,1,0:T(1,128)S(1)}, u32[]{:S(2)}, u32[]{:S(2)}) %collective-permute-start.9) | collective-permute-done | bytes 16416 | tf_op jit(solution)/shard_map/ppermute | solution.py:312
  188.3 2.1 %all-to-all-done.3.wire = f32[128,4,128]{2,1,0:T(4,128)S(1)} async-done(((f32[128,4,128]{2,1,0:T(4,128)}), f32[128,4,128]{2,1,0:T(4,128)S(1)}, u32[]{:S(2)}, u32[]{:S(2)}) %all-to-all-start.3) | async-done | bytes 262176 | tf_op jit(solution)/shard_map/all_to_all | solution.py:320
  190.5 0.7 copy-done
  191.2 12.4 %end.1 = f32[2,16,32,128]{3,2,1,0:T(8,128)} custom-call(s32[32,128]{1,0:T(8,128)} %get-tuple-element.45.bnd, s32[256,128]{1,0:T(8,128)} %get-tuple-element.46.cell, s32[128,256]{1,0:T(8,128)} %get-tuple-element.47.pos, f32[128,4,128]{2,1,0:T(4,128)} %copy-done, f32[2,16,32,128]{3,2,1,0:T(8,128)} %start.1, f32[2,16,32,128]{3,2,1,0:T(8,128)} %bitcast.5, ...), custom_call_target="tpu_custom_call" | custom-call | tf_op jit(solution)/shard_map/end/pallas_call | solution.py:299
  (33 shorter events, 0.1 us)
Async XLA Ops:
  15.7 12.6 %copy-start.15 = (f32[2,1,32,128]{3,2,1,0:T(8,128)S(1)}, f32[2,1,32,128]{3,2,1,0:T(8,128)}, u32[]{:S(2)}) copy-start(f32[2,1,32,128]{3,2,1,0:T(8,128)} %get-tuple-element.58) | copy-start | bytes 98308
  15.7 16.0 %copy-start.14 = (f32[2,1,32,128]{3,2,1,0:T(8,128)S(1)}, f32[2,1,32,128]{3,2,1,0:T(8,128)}, u32[]{:S(2)}) copy-start(f32[2,1,32,128]{3,2,1,0:T(8,128)} %get-tuple-element.59) | copy-start | bytes 98308
  15.7 23.6 %all-to-all-start = ((f32[128,4,128]{2,1,0:T(4,128)}), f32[128,4,128]{2,1,0:T(4,128)S(1)}, u32[]{:S(2)}, u32[]{:S(2)}) async-start(f32[128,4,128]{2,1,0:T(4,128)} %first.1), calls=%async_computation | async-start | bytes 524288 | tf_op jit(solution)/shard_map/all_to_all | solution.py:320
  28.3 8.4 %collective-permute-start = (f32[2,1,32,128]{3,2,1,0:T(8,128)S(1)}, f32[2,1,32,128]{3,2,1,0:T(8,128)S(1)}, u32[]{:S(2)}, u32[]{:S(2)}) collective-permute-start(f32[2,1,32,128]{3,2,1,0:T(8,128)S(1)} %copy-done.15), channel_id=1, source_target_pairs={{0,16},{16,32},{32,48},{48,64},{64,80},{80,96},{96,112},{1,17},{17... | collective-permute-start | bytes 98312 | tf_op jit(solution)/shard_map/ppermute | solution.py:312
  31.7 5.1 %collective-permute-start.1 = (f32[2,1,32,128]{3,2,1,0:T(8,128)S(1)}, f32[2,1,32,128]{3,2,1,0:T(8,128)S(1)}, u32[]{:S(2)}, u32[]{:S(2)}) collective-permute-start(f32[2,1,32,128]{3,2,1,0:T(8,128)S(1)} %copy-done.14), channel_id=1, source_target_pairs={{16,0},{32,16},{48,32},{64,48},{80,64},{96,80},{112,96},{17,1},{33... | collective-permute-start | bytes 98312 | tf_op jit(solution)/shard_map/ppermute | solution.py:312
  36.7 16.0 %copy-start.4 = (f32[2,1,32,128]{3,2,1,0:T(8,128)}, f32[2,1,32,128]{3,2,1,0:T(8,128)S(1)}, u32[]{:S(2)}) copy-start(f32[2,1,32,128]{3,2,1,0:T(8,128)S(1)} %collective-permute-done.xlo) | copy-start | bytes 98308
  36.8 15.9 %copy-start.5 = (f32[2,1,32,128]{3,2,1,0:T(8,128)}, f32[2,1,32,128]{3,2,1,0:T(8,128)S(1)}, u32[]{:S(2)}) copy-start(f32[2,1,32,128]{3,2,1,0:T(8,128)S(1)} %collective-permute-done.1.xhi) | copy-start | bytes 98308
  39.3 0.7 copy-start.2
  52.8 4.3 %collective-permute-start.2 = (f32[2,1,512]{2,1,0:T(1,128)}, f32[2,1,512]{2,1,0:T(1,128)S(1)}, u32[]{:S(2)}, u32[]{:S(2)}) collective-permute-start(f32[2,1,512]{2,1,0:T(1,128)} %get-tuple-element.63), channel_id=1, source_target_pairs={{0,1},{1,2},{2,3},{3,4},{4,5},{5,6},{6,7},{7,8},{8,9},{9,10},{10,1... | collective-permute-start | bytes 12296 | tf_op jit(solution)/shard_map/ppermute | solution.py:367
  57.1 0.6 copy-start.13
  69.9 12.2 %copy-start.21 = (f32[2,16,1,128]{3,2,1,0:T(1,128)S(1)}, f32[2,16,1,128]{3,2,1,0:T(1,128)}, u32[]{:S(2)}) copy-start(f32[2,16,1,128]{3,2,1,0:T(1,128)} %get-tuple-element.69) | copy-start | bytes 49156
  69.9 15.8 %copy-start.19 = (f32[2,16,1,128]{3,2,1,0:T(1,128)S(1)}, f32[2,16,1,128]{3,2,1,0:T(1,128)}, u32[]{:S(2)}) copy-start(f32[2,16,1,128]{3,2,1,0:T(1,128)} %get-tuple-element.70) | copy-start | bytes 49156
  69.9 23.3 %all-to-all-start.1 = ((f32[128,4,128]{2,1,0:T(4,128)}), f32[128,4,128]{2,1,0:T(4,128)S(1)}, u32[]{:S(2)}, u32[]{:S(2)}) async-start(f32[128,4,128]{2,1,0:T(4,128)} %get-tuple-element.64), calls=%async_computation.1 | async-start | bytes 524288 | tf_op jit(solution)/shard_map/all_to_all | solution.py:320
  82.1 5.5 %collective-permute-start.3 = (f32[2,16,1,128]{3,2,1,0:T(1,128)S(1)}, f32[2,16,1,128]{3,2,1,0:T(1,128)S(1)}, u32[]{:S(2)}, u32[]{:S(2)}) collective-permute-start(f32[2,16,1,128]{3,2,1,0:T(1,128)S(1)} %copy-done.21), channel_id=1, source_target_pairs={{0,1},{1,2},{2,3},{3,4},{4,5},{5,6},{6,7},{7,8},{8,9},{9,10},{10,1... | collective-permute-start | bytes 49160 | tf_op jit(solution)/shard_map/ppermute | solution.py:312
  85.7 5.4 %collective-permute-start.4 = (f32[2,16,1,128]{3,2,1,0:T(1,128)S(1)}, f32[2,16,1,128]{3,2,1,0:T(1,128)S(1)}, u32[]{:S(2)}, u32[]{:S(2)}) collective-permute-start(f32[2,16,1,128]{3,2,1,0:T(1,128)S(1)} %copy-done.19), channel_id=1, source_target_pairs={{1,0},{2,1},{3,2},{4,3},{5,4},{6,5},{7,6},{8,7},{9,8},{10,9},{11,1... | collective-permute-start | bytes 49160 | tf_op jit(solution)/shard_map/ppermute | solution.py:312
  87.6 5.5 %copy-start.8 = (f32[2,16,1,128]{3,2,1,0:T(1,128)}, f32[2,16,1,128]{3,2,1,0:T(1,128)S(1)}, u32[]{:S(2)}) copy-start(f32[2,16,1,128]{3,2,1,0:T(1,128)S(1)} %collective-permute-done.3.ylo) | copy-start | bytes 49156
  91.0 2.1 %copy-start.9 = (f32[2,16,1,128]{3,2,1,0:T(1,128)}, f32[2,16,1,128]{3,2,1,0:T(1,128)S(1)}, u32[]{:S(2)}) copy-start(f32[2,16,1,128]{3,2,1,0:T(1,128)S(1)} %collective-permute-done.4.yhi) | copy-start | bytes 49156
  93.2 0.7 copy-start.1
  115.4 10.1 %copy-start.17 = (f32[2,1,32,128]{3,2,1,0:T(8,128)S(1)}, f32[2,1,32,128]{3,2,1,0:T(8,128)}, u32[]{:S(2)}) copy-start(f32[2,1,32,128]{3,2,1,0:T(8,128)} %get-tuple-element.72) | copy-start | bytes 98308
  115.4 13.5 %copy-start.16 = (f32[2,1,32,128]{3,2,1,0:T(8,128)S(1)}, f32[2,1,32,128]{3,2,1,0:T(8,128)}, u32[]{:S(2)}) copy-start(f32[2,1,32,128]{3,2,1,0:T(8,128)} %get-tuple-element.73) | copy-start | bytes 98308
  115.4 21.2 %all-to-all-start.2 = ((f32[128,4,128]{2,1,0:T(4,128)}), f32[128,4,128]{2,1,0:T(4,128)S(1)}, u32[]{:S(2)}, u32[]{:S(2)}) async-start(f32[128,4,128]{2,1,0:T(4,128)} %get-tuple-element.71), calls=%async_computation.2 | async-start | bytes 524288 | tf_op jit(solution)/shard_map/all_to_all | solution.py:320
  125.6 4.9 %collective-permute-start.5 = (f32[2,1,32,128]{3,2,1,0:T(8,128)S(1)}, f32[2,1,32,128]{3,2,1,0:T(8,128)S(1)}, u32[]{:S(2)}, u32[]{:S(2)}) collective-permute-start(f32[2,1,32,128]{3,2,1,0:T(8,128)S(1)} %copy-done.17), channel_id=1, source_target_pairs={{0,16},{16,32},{32,48},{48,64},{64,80},{80,96},{96,112},{1,17},{17... | collective-permute-start | bytes 98312 | tf_op jit(solution)/shard_map/ppermute | solution.py:312
  129.0 5.1 %collective-permute-start.6 = (f32[2,1,32,128]{3,2,1,0:T(8,128)S(1)}, f32[2,1,32,128]{3,2,1,0:T(8,128)S(1)}, u32[]{:S(2)}, u32[]{:S(2)}) collective-permute-start(f32[2,1,32,128]{3,2,1,0:T(8,128)S(1)} %copy-done.16), channel_id=1, source_target_pairs={{16,0},{32,16},{48,32},{64,48},{80,64},{96,80},{112,96},{17,1},{33... | collective-permute-start | bytes 98312 | tf_op jit(solution)/shard_map/ppermute | solution.py:312
  130.5 19.6 %copy-start.6 = (f32[2,1,32,128]{3,2,1,0:T(8,128)}, f32[2,1,32,128]{3,2,1,0:T(8,128)S(1)}, u32[]{:S(2)}) copy-start(f32[2,1,32,128]{3,2,1,0:T(8,128)S(1)} %collective-permute-done.5.xlo) | copy-start | bytes 98308
  134.1 15.9 %copy-start.7 = (f32[2,1,32,128]{3,2,1,0:T(8,128)}, f32[2,1,32,128]{3,2,1,0:T(8,128)S(1)}, u32[]{:S(2)}) copy-start(f32[2,1,32,128]{3,2,1,0:T(8,128)S(1)} %collective-permute-done.6.xhi) | copy-start | bytes 98308
  136.6 0.7 copy-start.3
  150.0 4.3 %collective-permute-start.7 = (f32[2,1,512]{2,1,0:T(1,128)}, f32[2,1,512]{2,1,0:T(1,128)S(1)}, u32[]{:S(2)}, u32[]{:S(2)}) collective-permute-start(f32[2,1,512]{2,1,0:T(1,128)} %get-tuple-element.78), channel_id=1, source_target_pairs={{0,1},{1,2},{2,3},{3,4},{4,5},{5,6},{6,7},{7,8},{8,9},{9,10},{10,1... | collective-permute-start | bytes 12296 | tf_op jit(solution)/shard_map/ppermute | solution.py:367
  154.3 0.6 copy-start.12
  167.2 12.2 %copy-start.20 = (f32[2,16,1,128]{3,2,1,0:T(1,128)S(1)}, f32[2,16,1,128]{3,2,1,0:T(1,128)}, u32[]{:S(2)}) copy-start(f32[2,16,1,128]{3,2,1,0:T(1,128)} %get-tuple-element.85) | copy-start | bytes 49156
  167.2 15.8 %copy-start.18 = (f32[2,16,1,128]{3,2,1,0:T(1,128)S(1)}, f32[2,16,1,128]{3,2,1,0:T(1,128)}, u32[]{:S(2)}) copy-start(f32[2,16,1,128]{3,2,1,0:T(1,128)} %get-tuple-element.86) | copy-start | bytes 49156
  167.2 23.3 %all-to-all-start.3 = ((f32[128,4,128]{2,1,0:T(4,128)}), f32[128,4,128]{2,1,0:T(4,128)S(1)}, u32[]{:S(2)}, u32[]{:S(2)}) async-start(f32[128,4,128]{2,1,0:T(4,128)} %get-tuple-element.79), calls=%async_computation.3 | async-start | bytes 524288 | tf_op jit(solution)/shard_map/all_to_all | solution.py:320
  179.4 5.5 %collective-permute-start.8 = (f32[2,16,1,128]{3,2,1,0:T(1,128)S(1)}, f32[2,16,1,128]{3,2,1,0:T(1,128)S(1)}, u32[]{:S(2)}, u32[]{:S(2)}) collective-permute-start(f32[2,16,1,128]{3,2,1,0:T(1,128)S(1)} %copy-done.20), channel_id=1, source_target_pairs={{0,1},{1,2},{2,3},{3,4},{4,5},{5,6},{6,7},{7,8},{8,9},{9,10},{10,1... | collective-permute-start | bytes 49160 | tf_op jit(solution)/shard_map/ppermute | solution.py:312
  183.0 5.4 %collective-permute-start.9 = (f32[2,16,1,128]{3,2,1,0:T(1,128)S(1)}, f32[2,16,1,128]{3,2,1,0:T(1,128)S(1)}, u32[]{:S(2)}, u32[]{:S(2)}) collective-permute-start(f32[2,16,1,128]{3,2,1,0:T(1,128)S(1)} %copy-done.18), channel_id=1, source_target_pairs={{1,0},{2,1},{3,2},{4,3},{5,4},{6,5},{7,6},{8,7},{9,8},{10,9},{11,1... | collective-permute-start | bytes 49160 | tf_op jit(solution)/shard_map/ppermute | solution.py:312
  184.9 5.5 %copy-start.10 = (f32[2,16,1,128]{3,2,1,0:T(1,128)}, f32[2,16,1,128]{3,2,1,0:T(1,128)S(1)}, u32[]{:S(2)}) copy-start(f32[2,16,1,128]{3,2,1,0:T(1,128)S(1)} %collective-permute-done.8.ylo) | copy-start | bytes 49156
  188.3 2.1 %copy-start.11 = (f32[2,16,1,128]{3,2,1,0:T(1,128)}, f32[2,16,1,128]{3,2,1,0:T(1,128)S(1)}, u32[]{:S(2)}) copy-start(f32[2,16,1,128]{3,2,1,0:T(1,128)S(1)} %collective-permute-done.9.yhi) | copy-start | bytes 49156
  190.5 0.7 copy-start

commit v4 on v3

--- a/solution.py
+++ b/solution.py
@@ -8,7 +8,7 @@
 i32, f32, bf16 = jnp.int32, jnp.float32, jnp.bfloat16
 VM = pl.BlockSpec(memory_space=pltpu.VMEM)
 SM = pl.BlockSpec(memory_space=pltpu.SMEM)
-W, NB, LB, LR = 64, 16, 8, 16
+W, NB = 64, 16
 neutral_step = 0.4
 ion_factor = 0.5
 
@@ -57,23 +57,56 @@
         k *= 2
     return x.reshape(n, L)
 
-def sort_side(key16, cell_ref, pos_ref, inv_ref, bnd_ref):
+def take(x, idx):
+    return jnp.take_along_axis(x, idx, axis=1, mode="promise_in_bounds")
+
+
+def take2(x, idx):
+    low = idx & 127
+    return jnp.where(idx < 128, take(x[:, :128], low), take(x[:, 128:], low))
+
+
+def slot_keys(order, first, turn, slots):
+    lane = lax.broadcasted_iota(i32, (128, 128), 1)
+    for j in range(8):
+        idx = take(first[...], 8*j + (lane >> 4)) + 16*turn + (lane & 15)
+        slots[j*128:(j+1)*128, :] = (take2(order, jnp.minimum(idx, 255)) & 1023).T
+
+
+def sort_side(key16, cell_ref, pos_ref, bnd_ref, slot_ref, order_ref, first_ref, place_ref, ctl_ref):
     P, C = key16.shape
     c = lax.broadcasted_iota(i32, (P, C), 1)
-    k = (key16 * 256 + c).T
-    s = bitonic(k)
+    s = bitonic((key16 * 256 + c).T)
     cell = s >> 8
-    pos = s & 255
     cell_ref[...] = cell
-    pos_ref[...] = pos.T
-    r = lax.broadcasted_iota(i32, (C, P), 0)
-    inv = bitonic(pos*256 + r) & 255
-    inv_ref[...] = inv.T
+    pos = (s & 255).T
+    pos_ref[...] = pos
     row = (cell >> 7).reshape(C//8, 8, P)
     lo = jnp.min(jnp.min(row, axis=1), axis=1, keepdims=True)
     hi = jnp.max(jnp.max(row, axis=1), axis=1, keepdims=True)
     lane = lax.broadcasted_iota(i32, (C//8, 128), 1)
     bnd_ref[...] = jnp.where(lane == 0, lo, hi)
+    tall = cell.reshape(C//8, 8, P)
+    below = []
+    for b in range(64):
+        n = jnp.sum(jnp.where(tall < b*1024, 1.0, 0.0), axis=0)
+        below.append(jnp.sum(n, axis=0, keepdims=True))
+    full = jnp.full((64, P), float(C), f32)
+    below = jnp.concatenate(below + [full], axis=0)
+    most = jnp.max(pltpu.roll(below, 127, 0)[:64] - below[:64], axis=1, keepdims=True)
+    most = jnp.max(jnp.broadcast_to(most, (64, 128)).reshape(8, 8, 128), axis=1)
+    top = jnp.max(most, axis=0, keepdims=True)
+    ctl_ref[...] = jnp.where(lane[:8] == 0, most, jnp.broadcast_to(top, (8, 128))).astype(i32)
+    first = below.T.astype(i32)
+    first_ref[...] = first
+    order = cell.T
+    order_ref[...] = order
+    slot_keys(order, first_ref, 0, slot_ref)
+    b = order >> 10
+    w = c - jnp.concatenate([take(first, b[:, :128]), take(first, b[:, 128:])], axis=1)
+    place = (pos << 14) + ((w >> 4) << 10) + (b << 4) + (w & 15)
+    place_ref[...] = (bitonic(place.T) & 16383).T
+
 
 def cell_key(row, lane):
     return ((row & 255) << 8) + ((row >> 8) << 7) + lane
@@ -90,14 +123,16 @@
             yb[k, i] = u[-1:]
 
 
-def tile_sort_kernel(col, lev, wind, cell, pos, inv, bnd, *edge):
-    sort_side(cell_key(col[0], lev[0]), cell, pos, inv, bnd)
+def tile_sort_kernel(col, lev, wind, *outs):
+    side, edge = outs[:8], outs[8:]
+    sort_side(cell_key(col[0], lev[0]), *side)
     put_edges(lambda k, i: wind[k, i], *edge)
 
 
-def tube_sort_kernel(tub, pnt, weight, count, drift, cell, pos, inv, bnd, gain, drift_out):
+def tube_sort_kernel(tub, pnt, weight, count, drift, *outs):
+    side, gain, drift_out = outs[:8], outs[8], outs[9]
     p = pnt[0]
-    sort_side(cell_key((p >> 7)*128 + tub[0], p & 127), cell, pos, inv, bnd)
+    sort_side(cell_key((p >> 7)*128 + tub[0], p & 127), *side)
     own = lax.axis_index("gx") * lax.axis_size("gy") + lax.axis_index("gy")
     lane = lax.broadcasted_iota(i32, (128, 128), 1)
     live = jnp.sum(jnp.where(lane == own, count[...], 0).astype(f32), axis=1, keepdims=True)
@@ -107,50 +142,54 @@
 
 
 def permute_lanes(x, idx):
-    outs = []
-    for h in range(2):
-        ix = idx[:, h*128:(h+1)*128]
-        low = ix & 127
-        a = jnp.take_along_axis(x[:, :128], low, axis=1)
-        b = jnp.take_along_axis(x[:, 128:], low, axis=1)
-        outs.append(jnp.where(ix < 128, a, b))
-    return outs
-
-def lookup(bnd, cell_ref, t_ref, s_ref):
+    return [take2(x, idx[:, :128]), take2(x, idx[:, 128:])]
+
+
+def lookup(ctl, slot, order, first, place, t_ref, wire, s_ref, key_ref, gain=None):
     half = t_ref.shape[1] // 2
-
-    def blocks(u, _):
-        row, lev, start, count = [], [], [], None
-        for i in range(LB):
-            v = u*LB + i
-            key = cell_ref[pl.ds(pl.multiple_of(v*8, 8), 8), :]
-            row.append(key >> 7)
-            lev.append(key & 127)
-            lo = bnd[v, 0] >> 1
-            start.append(lo)
-            need = (bnd[v, 1] - 2*lo) // LR + 1
-            count = need if count is None else jnp.maximum(count, need)
-
-        def rows(g, acc):
-            acc = list(acc)
-            for i in range(LB):
-                base = jnp.minimum(start[i] + g*(LR//2), half - LR//2)
-                rel = row[i] - 2*base
-                for j in range(LR):
-                    m = rel == j
-                    for k in range(2):
-                        x = t_ref[k, pl.ds(base + (j//2) + (j % 2)*half, 1), :]
-                        x = jnp.take_along_axis(jnp.broadcast_to(x, (8, 128)), lev[i], axis=1, mode="promise_in_bounds")
-                        acc[2*i+k] = jnp.where(m, x, acc[2*i+k])
-            return tuple(acc)
-
-        acc = lax.fori_loop(0, count, rows, (jnp.zeros((8, 128), f32),)*(2*LB))
-        for i in range(LB):
+    key_ref[...] = slot[...]
+
+    def turn(t, _):
+        @pl.when(t > 0)
+        def _():
+            slot_keys(order[...], first, t, key_ref)
+
+        def group(g, _):
+            @pl.when(ctl[g, 0] > 16*t)
+            def _():
+                for b in range(8):
+                    rows = []
+                    for j in range(8):
+                        at = g*32 + 4*b + j//2 + (j % 2)*half
+                        rows.append([jnp.broadcast_to(t_ref[k, pl.ds(at, 1), :], (8, 128)) for k in range(2)])
+                    for i in range(2):
+                        sl = pl.ds(pl.multiple_of(g*128 + b*16 + i*8, 8), 8)
+                        key = key_ref[sl, :]
+                        sub, lev = key >> 7, key & 127
+                        acc = [take(rows[0][k], lev) for k in range(2)]
+                        for j in range(1, 8):
+                            m = sub == j
+                            for k in range(2):
+                                acc[k] = jnp.where(m, take(rows[j][k], lev), acc[k])
+                        for k in range(2):
+                            s_ref[k, sl, :] = acc[k]
+            return 0
+
+        lax.fori_loop(0, 8, group, 0)
+        parts = [[s_ref[k, j*128:(j+1)*128, :].T for j in range(8)] for k in range(2)]
+        for h in range(2):
+            at = place[:, h*128:(h+1)*128]
+            low, tile, mine = at & 127, (at >> 7) & 7, (at >> 10) == t
             for k in range(2):
-                s_ref[k, pl.ds(pl.multiple_of((u*LB + i)*8, 8), 8), :] = acc[2*i+k]
+                x = take(parts[k][0], low)
+                for j in range(1, 8):
+                    x = jnp.where(tile == j, take(parts[k][j], low), x)
+                if gain is not None:
+                    x = x * gain[:, h*128:(h+1)*128]
+                wire[:, 2*k+h, :] = jnp.where(mine, x, wire[:, 2*k+h, :])
         return 0
 
-    lax.fori_loop(0, 32//LB, blocks, 0)
+    lax.fori_loop(0, (ctl[0, 1] + 15) // 16, turn, 0)
 
 
 def scatter_add(bnd, cell_ref, val_ref, acc_ref):
@@ -192,16 +231,6 @@
     lax.fori_loop(0, 256//NB, block, 0)
 
 
-def to_wire(inv, s, out, gain=None):
-    for k in range(2):
-        o = permute_lanes(s[k].T, inv[...])
-        for h in range(2):
-            x = o[h]
-            if gain is not None:
-                x = x * gain[:, h*128:(h+1)*128]
-            out[:, 2*k+h, :] = x
-
-
 def from_wire(pos, wire, val, gain=None):
     for k in range(2):
         x = [wire[:, 2*k+h, :] for h in range(2)]
@@ -212,9 +241,8 @@
         val[k, 128:, :] = o[1].T
 
 
-def gather_kernel(bnd, cell, inv, t, out, s):
-    lookup(bnd, cell, t, s)
-    to_wire(inv, s, out)
+def gather_kernel(ctl, slot, order, first, place, t, wire, s, keys):
+    lookup(ctl, slot, order, first, place, t, wire, s, keys)
 
 
 def tube_kernel(bnd, coupling, cell, pos, gain, drift, wire, ions, inverse, w_out, smooth_out, last_out, val, acc):
@@ -234,7 +262,7 @@
         last_out[k] = drift[127:128, :1] * sm[127:128, :]
 
 
-def drag_kernel(last, bnd, drag, cell, inv, gain, drift, w, smooth, up, ions, n_out, wire, t, s):
+def drag_kernel(last, ctl, drag, slot, order, first_at, place, gain, drift, w, smooth, up, ions, n_out, wire, t, s, keys):
     first = lax.broadcasted_iota(i32, (128, 128), 0) == 0
     d = drift[...]
     n = [[], []]
@@ -251,8 +279,7 @@
         f = -(drag[0] * n[0][j] + drag[1] * n[1][j])
         for k in range(2):
             t[k, j*128:(j+1)*128, :] = f * w[k, :, j*128:(j+1)*128]
-    lookup(bnd, cell, t, s)
-    to_wire(inv, s, wire, gain)
+    lookup(ctl, slot, order, first_at, place, t, wire, s, keys, gain)
 
 
 def tend_all(wind, forcing, visc, xlo, xhi, ylo, yhi, acc, emit):
@@ -271,7 +298,7 @@
             emit(k, i, u, v * (b - 6.0 * u) + acc[k, (i*CY) % 256:(i*CY) % 256 + CY, (i*CY)//256*128:(i*CY)//256*128 + 128] + forcing[k, i])
 
 
-def mid_kernel(bnd, cell, pos, inv, wire, wind, forcing, visc, xlo, xhi, ylo, yhi, mid, wire_out, xa, xb, ya, yb, val, acc, s):
+def mid_kernel(bnd, ctl, cell, pos, slot, order, first, place, wire, wind, forcing, visc, xlo, xhi, ylo, yhi, mid, wire_out, xa, xb, ya, yb, val, acc, s, keys):
     from_wire(pos, wire, val)
     scatter_add(bnd, cell, val, acc)
     CY = wind.shape[2]
@@ -281,8 +308,7 @@
 
     tend_all(wind, forcing, visc, xlo, xhi, ylo, yhi, acc, emit)
     put_edges(lambda k, i: mid[k, i*CY:(i+1)*CY, :], xa, xb, ya, yb)
-    lookup(bnd, cell, mid, s)
-    to_wire(inv, s, wire_out)
+    lookup(ctl, slot, order, first, place, mid, wire_out, s, keys)
 
 
 def end_kernel(bnd, cell, pos, wire, start, wind, forcing, visc, xlo, xhi, ylo, yhi, out, val, acc):
@@ -347,14 +373,16 @@
     up_route = [(i, i + 1) for i in range(lax.axis_size("gy") - 1)]
     CX, CY = neutral_wind.shape[1:3]
     edge_t = (sd((2, 1, CY, 128), f32),)*2 + (sd((2, CX, 1, 128), f32),)*2
-    side_t = (sd((256, 128), i32), sd((128, 256), i32), sd((128, 256), i32), sd((32, 128), i32))
-
-    cA, pA, iA, bA, xa, xb, ya, yb = call(
+    side_t = (sd((256, 128), i32), sd((128, 256), i32), sd((32, 128), i32), sd((1024, 128), i32))
+    side_t += (sd((128, 256), i32), sd((128, 128), i32), sd((128, 256), i32), sd((8, 128), i32))
+    seek = [pltpu.VMEM((2, 1024, 128), f32), pltpu.VMEM((1024, 128), i32)]
+
+    cA, pA, bA, *gA, ctA, xa, xb, ya, yb = call(
         tile_sort_kernel, side_t + edge_t, [], outgoing_column, send_level, neutral_wind, smem=0, name="tilesort")
-    wire = call(gather_kernel, wire_t, [vals], bA, cA, iA, neutral_wind.reshape(flat), name="first")
+    wire = call(gather_kernel, wire_t, seek, ctA, *gA, neutral_wind.reshape(flat), name="first")
     came = exchange(wire)
     wire, tub, xa, xb = tied(wire, recv_tube, xa, xb)
-    cB, pB, iB, bB, gain, drift = call(
+    cB, pB, bB, *gB, ctB, gain, drift = call(
         tube_sort_kernel, side_t + (sd((128, 256), f32), sd((128, 128), f32)), [],
         tub, recv_point, recv_weight, pair_count, drift_fraction[None, :], smem=0, name="tubesort")
     halo = beside("gx", xa, xb)
@@ -366,16 +394,16 @@
             bB, coupling, cB, pB, gain, drift, came, ions, inverse, smem=2, name="tube")
         up = lax.ppermute(out_last, "gy", up_route)
         return call(
-            lambda *a: drag_kernel(last, *a), (tube_t, wire_t), [tabs, vals],
-            bB, drag_rate, cB, iB, gain, drift, w, smooth, up, ion_density, smem=2, name="drag")
+            lambda *a: drag_kernel(last, *a), (tube_t, wire_t), [tabs] + seek,
+            ctB, drag_rate, *gB, gain, drift, w, smooth, up, ion_density, smem=2, name="drag")
 
     n1, wire = tubes(came, ion_density, False)
     came = exchange(wire)
     wire, ya, yb = tied(wire, ya, yb)
     halo += beside("gy", ya, yb)
     mid, wire, xa, xb, ya, yb = call(
-        mid_kernel, (sd(flat, f32), wire_t) + edge_t, [vals, accs, vals],
-        bA, cA, pA, iA, came, neutral_wind, forcing, visc, *halo, name="mid")
+        mid_kernel, (sd(flat, f32), wire_t) + edge_t, [vals, accs] + seek,
+        bA, ctA, cA, pA, *gA, came, neutral_wind, forcing, visc, *halo, smem=2, name="mid")
     mid = mid.reshape(neutral_wind.shape)
     came = exchange(wire)
     halo = beside("gx", xa, xb)

time: 207 us -> 192 us (0.928)
  Pallas kernels: 103 us -> 93.3 us
  starting transfers between devices: 74.2 us -> 71.2 us
  waiting for transfers between devices: 21.7 us -> 19.4 us
    pallas_call x9, Pallas kernels: 103 us -> 93.3 us  [call(): pl.pallas_call(kernel, out_shape=outs, in_specs=[SM] * smem + [VM] * (len...]
    all_to_all x4, starting transfers between devices: 47.1 us -> 44.4 us  [exchange(): lax.all_to_all(x, ('gx', 'gy'), split_axis=0, concat_axis=0, tiled=True)]
    all_to_all x4, waiting for transfers between devices: 9.23 us -> 6.84 us  [exchange(): lax.all_to_all(x, ('gx', 'gy'), split_axis=0, concat_axis=0, tiled=True)]
  transfers between devices with their start and end apart: 14 -> 14, of which waited for: 10 -> 9; matrix products, arithmetic and copies ran while one was open for 0% -> 0% of each run, Pallas kernels for 2% -> 3%
where the time goes in v4:
time: 192 us; the launch traced here: 189 us
  Pallas kernels  93.3 us (49%)
  starting transfers between devices  71.2 us (37%)
  waiting for transfers between devices  19.4 us (10%)
  local copies, waits for them, and re-layouts  4.06 us (2%)
    pallas_call x9, Pallas kernels, call(): pl.pallas_call(kernel, out_shape=outs, in_specs=[SM] * smem + [VM] * (len...  93.3 us
    all_to_all x4, starting transfers between devices, exchange(): lax.all_to_all(x, ('gx', 'gy'), split_axis=0, concat_axis=0, tiled=True)  44.4 us
    ppermute x4, starting transfers between devices, beside(): lax.ppermute(last, axis, up)  13.9 us
    ppermute x4, waiting for transfers between devices, beside(): lax.ppermute(first, axis, [(b, a) for a, b in up])  10.6 us
    all_to_all x4, waiting for transfers between devices, exchange(): lax.all_to_all(x, ('gx', 'gy'), split_axis=0, concat_axis=0, tiled=True)  6.84 us
    ppermute x4, starting transfers between devices, beside(): lax.ppermute(first, axis, [(b, a) for a, b in up])  6.61 us
    ppermute x2, starting transfers between devices, tubes(): up = lax.ppermute(out_last, 'gy', up_route)  6.34 us
    unnamed x44, local copies, waits for them, and re-layouts  4.06 us
  transfers between devices with their start and end apart: 14, of which 9 were waited for; matrix products, arithmetic and copies ran while one was open for 0% of the time, Pallas kernels for 3%

profile of v4, /device:TPU:1, one launch (start us, length us, event | category | flops | bytes accessed | tf_op | source)
XLA Modules:
  0.0 188.8 jit_solution(5042574128352488836)
XLA Ops:
  0.6 6.1 %tilesort.1 = (s32[256,128]{1,0:T(8,128)}, s32[128,256]{1,0:T(8,128)}, s32[32,128]{1,0:T(8,128)}, s32[1024,128]{1,0:T(8,128)}, s32[128,256]{1,0:T(8,128)}, /*ind...) custom-call(s32[1,128,256]{2,1,0:T(8,128)} %col.1, ...), custom_call_target="tpu_custom_call" | custom-call | tf_op jit(solution)/shard_map/tilesort/pallas_call | solution.py:325
  6.7 7.1 %first.1 = f32[128,4,128]{2,1,0:T(4,128)} custom-call(s32[8,128]{1,0:T(8,128)} %get-tuple-element.56.ctl, s32[1024,128]{1,0:T(8,128)} %get-tuple-element.57.slot, s32[128,256]{1,0:T(8,128)} %get-tuple-element.58.order, s32[128,128]{1,0:T(8,128)} %get-tuple-element.59.first, s32[128,256]{1,0:T(8,128)} %get-tuple-element.60.place, f32[2,512,128]{2,1,0:T(8,128)} %bitcast.4), custom_call_target="tpu_custom_call" | custom-call | tf_op jit(solution)/shard_map/first/pallas_call | solution.py:325
  13.8 11.5 %all-to-all-start = ((f32[128,4,128]{2,1,0:T(4,128)}), f32[128,4,128]{2,1,0:T(4,128)S(1)}, u32[]{:S(2)}, u32[]{:S(2)}) async-start(f32[128,4,128]{2,1,0:T(4,128)} %first.1), calls=%async_computation | async-start | bytes 524288 | tf_op jit(solution)/shard_map/all_to_all | solution.py:346
  25.3 3.4 %collective-permute-start = (f32[2,1,32,128]{3,2,1,0:T(8,128)S(1)}, f32[2,1,32,128]{3,2,1,0:T(8,128)S(1)}, u32[]{:S(2)}, u32[]{:S(2)}) collective-permute-start(f32[2,1,32,128]{3,2,1,0:T(8,128)S(1)} %copy-done.15), channel_id=1, source_target_pairs={{0,16},{16,32},{32,48},{48,64},{64,80},{80,96},{96,112},{1,17},{17... | collective-permute-start | bytes 98312 | tf_op jit(solution)/shard_map/ppermute | solution.py:338
  28.7 1.5 collective-permute-start.1
  30.2 6.0 %tubesort.1 = (s32[256,128]{1,0:T(8,128)}, s32[128,256]{1,0:T(8,128)}, s32[32,128]{1,0:T(8,128)}, s32[1024,128]{1,0:T(8,128)}, s32[128,256]{1,0:T(8,128)}, /*ind...) custom-call(s32[1,128,256]{2,1,0:T(8,128)} %tub, ...), custom_call_target="tpu_custom_call" | custom-call | tf_op jit(solution)/shard_map/tubesort/pallas_call | solution.py:325
  36.2 0.0 collective-permute-done.xlo
  36.2 0.0 collective-permute-done.1.xhi
  36.2 0.0 copy-start.5
  36.2 0.1 all-to-all-done.wire
  36.3 0.7 copy-done.1
  37.1 13.7 %tube.2 = (f32[2,128,512]{2,1,0:T(8,128)}, f32[2,128,512]{2,1,0:T(8,128)}, f32[2,1,512]{2,1,0:T(1,128)}) custom-call(s32[32,128]{1,0:T(8,128)} %get-tuple-element.71.bnd, f32[2,2]{1,0:T(2,128)} %coupling.3, s32[256,128]{1,0:T(8,128)} %get-tuple-element.72.cell, s32[128,256]{1,0:T(8,128)} %get-tuple-element.73.pos, f32[128,256]{1,0:T(8,128)} %get-tuple-element.69.gain.a_6_, ...), custom_call_target="tpu_custom_call" | custom-call | tf_op jit(solution)/shard_map/tube/pallas_call | solution.py:325
  50.8 0.0 copy-done.5
  50.8 3.5 %collective-permute-start.2 = (f32[2,1,512]{2,1,0:T(1,128)}, f32[2,1,512]{2,1,0:T(1,128)S(1)}, u32[]{:S(2)}, u32[]{:S(2)}) collective-permute-start(f32[2,1,512]{2,1,0:T(1,128)} %get-tuple-element.79), channel_id=1, source_target_pairs={{0,1},{1,2},{2,3},{3,4},{4,5},{5,6},{6,7},{7,8},{8,9},{9,10},{10,1... | collective-permute-start | bytes 12296 | tf_op jit(solution)/shard_map/ppermute | solution.py:395
  54.3 0.9 collective-permute-done.2.a_10_
  55.3 0.6 copy-done.13
  55.9 7.8 %drag.2 = (f32[2,128,512]{2,1,0:T(8,128)}, f32[128,4,128]{2,1,0:T(4,128)}) custom-call(s32[8,128]{1,0:T(8,128)} %get-tuple-element.64.a_0_, f32[2]{0:T(128)} %a_1_.3, s32[1024,128]{1,0:T(8,128)} %get-tuple-element.65.a_2_, s32[128,256]{1,0:T(8,128)} %get-tuple-element.66.a_3_, s32[128,128]{1,0:T(8,128)} %get-tuple-element.67.a_4_, ...), custom_call_target="tpu_custom_call" | custom-call | tf_op jit(solution)/shard_map/drag/pallas_call | solution.py:325
  63.7 12.3 %all-to-all-start.1 = ((f32[128,4,128]{2,1,0:T(4,128)}), f32[128,4,128]{2,1,0:T(4,128)S(1)}, u32[]{:S(2)}, u32[]{:S(2)}) async-start(f32[128,4,128]{2,1,0:T(4,128)} %get-tuple-element.80), calls=%async_computation.1 | async-start | bytes 524288 | tf_op jit(solution)/shard_map/all_to_all | solution.py:346
  76.1 3.5 %collective-permute-start.3 = (f32[2,16,1,128]{3,2,1,0:T(1,128)S(1)}, f32[2,16,1,128]{3,2,1,0:T(1,128)S(1)}, u32[]{:S(2)}, u32[]{:S(2)}) collective-permute-start(f32[2,16,1,128]{3,2,1,0:T(1,128)S(1)} %copy-done.21), channel_id=1, source_target_pairs={{0,1},{1,2},{2,3},{3,4},{4,5},{5,6},{6,7},{7,8},{8,9},{9,10},{10,1... | collective-permute-start | bytes 49160 | tf_op jit(solution)/shard_map/ppermute | solution.py:338
  79.6 1.9 %collective-permute-start.4 = (f32[2,16,1,128]{3,2,1,0:T(1,128)S(1)}, f32[2,16,1,128]{3,2,1,0:T(1,128)S(1)}, u32[]{:S(2)}, u32[]{:S(2)}) collective-permute-start(f32[2,16,1,128]{3,2,1,0:T(1,128)S(1)} %copy-done.19), channel_id=1, source_target_pairs={{1,0},{2,1},{3,2},{4,3},{5,4},{6,5},{7,6},{8,7},{9,8},{10,9},{11,1... | collective-permute-start | bytes 49160 | tf_op jit(solution)/shard_map/ppermute | solution.py:338
  81.6 0.0 collective-permute-done.3.ylo
  81.6 3.4 %collective-permute-done.4.yhi = f32[2,16,1,128]{3,2,1,0:T(1,128)S(1)} collective-permute-done((f32[2,16,1,128]{3,2,1,0:T(1,128)S(1)}, f32[2,16,1,128]{3,2,1,0:T(1,128)S(1)}, u32[]{:S(2)}, u32[]{:S(2)}) %collective-permute-start.4) | collective-permute-done | bytes 16416 | tf_op jit(solution)/shard_map/ppermute | solution.py:338
  85.0 2.1 %all-to-all-done.1.wire = f32[128,4,128]{2,1,0:T(4,128)S(1)} async-done(((f32[128,4,128]{2,1,0:T(4,128)}), f32[128,4,128]{2,1,0:T(4,128)S(1)}, u32[]{:S(2)}, u32[]{:S(2)}) %all-to-all-start.1) | async-done | bytes 262176 | tf_op jit(solution)/shard_map/all_to_all | solution.py:346
  87.1 0.0 copy-done.9
  87.1 0.7 copy-done.2
  87.8 18.1 %mid.1 = (f32[2,512,128]{2,1,0:T(8,128)}, f32[128,4,128]{2,1,0:T(4,128)}, f32[2,1,32,128]{3,2,1,0:T(8,128)}, f32[2,1,32,128]{3,2,1,0:T(8,128)}, f32[2,16,1,128]{3,2,1,0:T(1,128)}, /*index=5*/f32[2,16,1,128]{3,2,1,0:T(1,128)}) custom-call(s32[32,128]{1,0:T(8,128)} %get-tuple-element.53.bnd, s32[8,128]{1,0:T(8,128)} %get-tuple-element.56.ctl, ...), custom_call_target="tpu_custom_call" | custom-call | tf_op jit(solution)/shard_map/mid/pallas_call | solution.py:325
  106.0 8.5 %all-to-all-start.2 = ((f32[128,4,128]{2,1,0:T(4,128)}), f32[128,4,128]{2,1,0:T(4,128)S(1)}, u32[]{:S(2)}, u32[]{:S(2)}) async-start(f32[128,4,128]{2,1,0:T(4,128)} %get-tuple-element.87), calls=%async_computation.2 | async-start | bytes 524288 | tf_op jit(solution)/shard_map/all_to_all | solution.py:346
  114.5 3.4 %collective-permute-start.5 = (f32[2,1,32,128]{3,2,1,0:T(8,128)S(1)}, f32[2,1,32,128]{3,2,1,0:T(8,128)S(1)}, u32[]{:S(2)}, u32[]{:S(2)}) collective-permute-start(f32[2,1,32,128]{3,2,1,0:T(8,128)S(1)} %copy-done.17), channel_id=1, source_target_pairs={{0,16},{16,32},{32,48},{48,64},{64,80},{80,96},{96,112},{1,17},{17... | collective-permute-start | bytes 98312 | tf_op jit(solution)/shard_map/ppermute | solution.py:338
  117.9 1.3 collective-permute-start.6
  119.2 0.0 collective-permute-done.5.xlo
  119.2 3.8 %collective-permute-done.6.xhi = f32[2,1,32,128]{3,2,1,0:T(8,128)S(1)} collective-permute-done((f32[2,1,32,128]{3,2,1,0:T(8,128)S(1)}, f32[2,1,32,128]{3,2,1,0:T(8,128)S(1)}, u32[]{:S(2)}, u32[]{:S(2)}) %collective-permute-start.6) | collective-permute-done | bytes 32800 | tf_op jit(solution)/shard_map/ppermute | solution.py:338
  123.0 2.5 %all-to-all-done.2.wire = f32[128,4,128]{2,1,0:T(4,128)S(1)} async-done(((f32[128,4,128]{2,1,0:T(4,128)}), f32[128,4,128]{2,1,0:T(4,128)S(1)}, u32[]{:S(2)}, u32[]{:S(2)}) %all-to-all-start.2) | async-done | bytes 262176 | tf_op jit(solution)/shard_map/all_to_all | solution.py:346
  125.5 0.7 copy-done.3
  126.2 13.7 %tube.3 = (f32[2,128,512]{2,1,0:T(8,128)}, f32[2,128,512]{2,1,0:T(8,128)}, f32[2,1,512]{2,1,0:T(1,128)}) custom-call(s32[32,128]{1,0:T(8,128)} %get-tuple-element.71.bnd, f32[2,2]{1,0:T(2,128)} %coupling.3, s32[256,128]{1,0:T(8,128)} %get-tuple-element.72.cell, s32[128,256]{1,0:T(8,128)} %get-tuple-element.73.pos, f32[128,256]{1,0:T(8,128)} %get-tuple-element.69.gain.a_6_, ...), custom_call_target="tpu_custom_call" | custom-call | tf_op jit(solution)/shard_map/tube/pallas_call | solution.py:325
  139.9 2.8 %collective-permute-start.7 = (f32[2,1,512]{2,1,0:T(1,128)}, f32[2,1,512]{2,1,0:T(1,128)S(1)}, u32[]{:S(2)}, u32[]{:S(2)}) collective-permute-start(f32[2,1,512]{2,1,0:T(1,128)} %get-tuple-element.94), channel_id=1, source_target_pairs={{0,1},{1,2},{2,3},{3,4},{4,5},{5,6},{6,7},{7,8},{8,9},{9,10},{10,1... | collective-permute-start | bytes 12296 | tf_op jit(solution)/shard_map/ppermute | solution.py:395
  142.7 0.9 collective-permute-done.7.a_10_
  143.7 0.6 copy-done.12
  144.2 7.9 %drag.3 = (f32[2,128,512]{2,1,0:T(8,128)}, f32[128,4,128]{2,1,0:T(4,128)}) custom-call(s32[8,128]{1,0:T(8,128)} %get-tuple-element.64.a_0_, f32[2]{0:T(128)} %a_1_.3, s32[1024,128]{1,0:T(8,128)} %get-tuple-element.65.a_2_, s32[128,256]{1,0:T(8,128)} %get-tuple-element.66.a_3_, s32[128,128]{1,0:T(8,128)} %get-tuple-element.67.a_4_, ...), custom_call_target="tpu_custom_call" | custom-call | tf_op jit(solution)/shard_map/drag/pallas_call | solution.py:325
  152.1 12.1 %all-to-all-start.3 = ((f32[128,4,128]{2,1,0:T(4,128)}), f32[128,4,128]{2,1,0:T(4,128)S(1)}, u32[]{:S(2)}, u32[]{:S(2)}) async-start(f32[128,4,128]{2,1,0:T(4,128)} %get-tuple-element.95), calls=%async_computation.3 | async-start | bytes 524288 | tf_op jit(solution)/shard_map/all_to_all | solution.py:346
  164.2 0.0 copy-done.20
  164.2 3.5 %collective-permute-start.8 = (f32[2,16,1,128]{3,2,1,0:T(1,128)S(1)}, f32[2,16,1,128]{3,2,1,0:T(1,128)S(1)}, u32[]{:S(2)}, u32[]{:S(2)}) collective-permute-start(f32[2,16,1,128]{3,2,1,0:T(1,128)S(1)} %copy-done.20), channel_id=1, source_target_pairs={{0,1},{1,2},{2,3},{3,4},{4,5},{5,6},{6,7},{7,8},{8,9},{9,10},{10,1... | collective-permute-start | bytes 49160 | tf_op jit(solution)/shard_map/ppermute | solution.py:338
  167.8 1.9 %collective-permute-start.9 = (f32[2,16,1,128]{3,2,1,0:T(1,128)S(1)}, f32[2,16,1,128]{3,2,1,0:T(1,128)S(1)}, u32[]{:S(2)}, u32[]{:S(2)}) collective-permute-start(f32[2,16,1,128]{3,2,1,0:T(1,128)S(1)} %copy-done.18), channel_id=1, source_target_pairs={{1,0},{2,1},{3,2},{4,3},{5,4},{6,5},{7,6},{8,7},{9,8},{10,9},{11,1... | collective-permute-start | bytes 49160 | tf_op jit(solution)/shard_map/ppermute | solution.py:338
  169.7 0.0 collective-permute-done.8.ylo
  169.7 0.0 copy-start.10
  169.7 3.4 %collective-permute-done.9.yhi = f32[2,16,1,128]{3,2,1,0:T(1,128)S(1)} collective-permute-done((f32[2,16,1,128]{3,2,1,0:T(1,128)S(1)}, f32[2,16,1,128]{3,2,1,0:T(1,128)S(1)}, u32[]{:S(2)}, u32[]{:S(2)}) %collective-permute-start.9) | collective-permute-done | bytes 16416 | tf_op jit(solution)/shard_map/ppermute | solution.py:338
  173.2 2.1 %all-to-all-done.3.wire = f32[128,4,128]{2,1,0:T(4,128)S(1)} async-done(((f32[128,4,128]{2,1,0:T(4,128)}), f32[128,4,128]{2,1,0:T(4,128)S(1)}, u32[]{:S(2)}, u32[]{:S(2)}) %all-to-all-start.3) | async-done | bytes 262176 | tf_op jit(solution)/shard_map/all_to_all | solution.py:346
  175.3 0.7 copy-done
  176.0 12.8 %end.1 = f32[2,16,32,128]{3,2,1,0:T(8,128)} custom-call(s32[32,128]{1,0:T(8,128)} %get-tuple-element.53.bnd, s32[256,128]{1,0:T(8,128)} %get-tuple-element.54.cell, s32[128,256]{1,0:T(8,128)} %get-tuple-element.55.pos, f32[128,4,128]{2,1,0:T(4,128)} %copy-done, f32[2,16,32,128]{3,2,1,0:T(8,128)} %start.1, f32[2,16,32,128]{3,2,1,0:T(8,128)} %bitcast.5, ...), custom_call_target="tpu_custom_call" | custom-call | tf_op jit(solution)/shard_map/end/pallas_call | solution.py:325
  (33 shorter events, 0.1 us)
Async XLA Ops:
  13.8 11.5 %copy-start.15 = (f32[2,1,32,128]{3,2,1,0:T(8,128)S(1)}, f32[2,1,32,128]{3,2,1,0:T(8,128)}, u32[]{:S(2)}) copy-start(f32[2,1,32,128]{3,2,1,0:T(8,128)} %get-tuple-element.74) | copy-start | bytes 98308
  13.8 14.9 %copy-start.14 = (f32[2,1,32,128]{3,2,1,0:T(8,128)S(1)}, f32[2,1,32,128]{3,2,1,0:T(8,128)}, u32[]{:S(2)}) copy-start(f32[2,1,32,128]{3,2,1,0:T(8,128)} %get-tuple-element.75) | copy-start | bytes 98308
  13.8 22.5 %all-to-all-start = ((f32[128,4,128]{2,1,0:T(4,128)}), f32[128,4,128]{2,1,0:T(4,128)S(1)}, u32[]{:S(2)}, u32[]{:S(2)}) async-start(f32[128,4,128]{2,1,0:T(4,128)} %first.1), calls=%async_computation | async-start | bytes 524288 | tf_op jit(solution)/shard_map/all_to_all | solution.py:346
  25.3 10.9 %collective-permute-start = (f32[2,1,32,128]{3,2,1,0:T(8,128)S(1)}, f32[2,1,32,128]{3,2,1,0:T(8,128)S(1)}, u32[]{:S(2)}, u32[]{:S(2)}) collective-permute-start(f32[2,1,32,128]{3,2,1,0:T(8,128)S(1)} %copy-done.15), channel_id=1, source_target_pairs={{0,16},{16,32},{32,48},{48,64},{64,80},{80,96},{96,112},{1,17},{17... | collective-permute-start | bytes 98312 | tf_op jit(solution)/shard_map/ppermute | solution.py:338
  28.7 7.5 %collective-permute-start.1 = (f32[2,1,32,128]{3,2,1,0:T(8,128)S(1)}, f32[2,1,32,128]{3,2,1,0:T(8,128)S(1)}, u32[]{:S(2)}, u32[]{:S(2)}) collective-permute-start(f32[2,1,32,128]{3,2,1,0:T(8,128)S(1)} %copy-done.14), channel_id=1, source_target_pairs={{16,0},{32,16},{48,32},{64,48},{80,64},{96,80},{112,96},{17,1},{33... | collective-permute-start | bytes 98312 | tf_op jit(solution)/shard_map/ppermute | solution.py:338
  36.2 14.6 %copy-start.4 = (f32[2,1,32,128]{3,2,1,0:T(8,128)}, f32[2,1,32,128]{3,2,1,0:T(8,128)S(1)}, u32[]{:S(2)}) copy-start(f32[2,1,32,128]{3,2,1,0:T(8,128)S(1)} %collective-permute-done.xlo) | copy-start | bytes 98308
  36.2 14.5 %copy-start.5 = (f32[2,1,32,128]{3,2,1,0:T(8,128)}, f32[2,1,32,128]{3,2,1,0:T(8,128)S(1)}, u32[]{:S(2)}) copy-start(f32[2,1,32,128]{3,2,1,0:T(8,128)S(1)} %collective-permute-done.1.xhi) | copy-start | bytes 98308
  36.3 0.7 copy-start.1
  50.8 4.5 %collective-permute-start.2 = (f32[2,1,512]{2,1,0:T(1,128)}, f32[2,1,512]{2,1,0:T(1,128)S(1)}, u32[]{:S(2)}, u32[]{:S(2)}) collective-permute-start(f32[2,1,512]{2,1,0:T(1,128)} %get-tuple-element.79), channel_id=1, source_target_pairs={{0,1},{1,2},{2,3},{3,4},{4,5},{5,6},{6,7},{7,8},{8,9},{9,10},{10,1... | collective-permute-start | bytes 12296 | tf_op jit(solution)/shard_map/ppermute | solution.py:395
  55.3 0.6 copy-start.13
  63.7 12.4 %copy-start.21 = (f32[2,16,1,128]{3,2,1,0:T(1,128)S(1)}, f32[2,16,1,128]{3,2,1,0:T(1,128)}, u32[]{:S(2)}) copy-start(f32[2,16,1,128]{3,2,1,0:T(1,128)} %get-tuple-element.85) | copy-start | bytes 49156
  63.7 15.9 %copy-start.19 = (f32[2,16,1,128]{3,2,1,0:T(1,128)S(1)}, f32[2,16,1,128]{3,2,1,0:T(1,128)}, u32[]{:S(2)}) copy-start(f32[2,16,1,128]{3,2,1,0:T(1,128)} %get-tuple-element.86) | copy-start | bytes 49156
  63.7 23.4 %all-to-all-start.1 = ((f32[128,4,128]{2,1,0:T(4,128)}), f32[128,4,128]{2,1,0:T(4,128)S(1)}, u32[]{:S(2)}, u32[]{:S(2)}) async-start(f32[128,4,128]{2,1,0:T(4,128)} %get-tuple-element.80), calls=%async_computation.1 | async-start | bytes 524288 | tf_op jit(solution)/shard_map/all_to_all | solution.py:346
  76.1 5.5 %collective-permute-start.3 = (f32[2,16,1,128]{3,2,1,0:T(1,128)S(1)}, f32[2,16,1,128]{3,2,1,0:T(1,128)S(1)}, u32[]{:S(2)}, u32[]{:S(2)}) collective-permute-start(f32[2,16,1,128]{3,2,1,0:T(1,128)S(1)} %copy-done.21), channel_id=1, source_target_pairs={{0,1},{1,2},{2,3},{3,4},{4,5},{5,6},{6,7},{7,8},{8,9},{9,10},{10,1... | collective-permute-start | bytes 49160 | tf_op jit(solution)/shard_map/ppermute | solution.py:338
  79.6 5.4 %collective-permute-start.4 = (f32[2,16,1,128]{3,2,1,0:T(1,128)S(1)}, f32[2,16,1,128]{3,2,1,0:T(1,128)S(1)}, u32[]{:S(2)}, u32[]{:S(2)}) collective-permute-start(f32[2,16,1,128]{3,2,1,0:T(1,128)S(1)} %copy-done.19), channel_id=1, source_target_pairs={{1,0},{2,1},{3,2},{4,3},{5,4},{6,5},{7,6},{8,7},{9,8},{10,9},{11,1... | collective-permute-start | bytes 49160 | tf_op jit(solution)/shard_map/ppermute | solution.py:338
  81.6 5.5 %copy-start.8 = (f32[2,16,1,128]{3,2,1,0:T(1,128)}, f32[2,16,1,128]{3,2,1,0:T(1,128)S(1)}, u32[]{:S(2)}) copy-start(f32[2,16,1,128]{3,2,1,0:T(1,128)S(1)} %collective-permute-done.3.ylo) | copy-start | bytes 49156
  85.0 2.1 %copy-start.9 = (f32[2,16,1,128]{3,2,1,0:T(1,128)}, f32[2,16,1,128]{3,2,1,0:T(1,128)S(1)}, u32[]{:S(2)}) copy-start(f32[2,16,1,128]{3,2,1,0:T(1,128)S(1)} %collective-permute-done.4.yhi) | copy-start | bytes 49156
  87.1 0.7 copy-start.2
  105.9 8.5 %copy-start.17 = (f32[2,1,32,128]{3,2,1,0:T(8,128)S(1)}, f32[2,1,32,128]{3,2,1,0:T(8,128)}, u32[]{:S(2)}) copy-start(f32[2,1,32,128]{3,2,1,0:T(8,128)} %get-tuple-element.88) | copy-start | bytes 98308
  106.0 11.9 %copy-start.16 = (f32[2,1,32,128]{3,2,1,0:T(8,128)S(1)}, f32[2,1,32,128]{3,2,1,0:T(8,128)}, u32[]{:S(2)}) copy-start(f32[2,1,32,128]{3,2,1,0:T(8,128)} %get-tuple-element.89) | copy-start | bytes 98308
  106.0 19.6 %all-to-all-start.2 = ((f32[128,4,128]{2,1,0:T(4,128)}), f32[128,4,128]{2,1,0:T(4,128)S(1)}, u32[]{:S(2)}, u32[]{:S(2)}) async-start(f32[128,4,128]{2,1,0:T(4,128)} %get-tuple-element.87), calls=%async_computation.2 | async-start | bytes 524288 | tf_op jit(solution)/shard_map/all_to_all | solution.py:346
  114.5 4.7 %collective-permute-start.5 = (f32[2,1,32,128]{3,2,1,0:T(8,128)S(1)}, f32[2,1,32,128]{3,2,1,0:T(8,128)S(1)}, u32[]{:S(2)}, u32[]{:S(2)}) collective-permute-start(f32[2,1,32,128]{3,2,1,0:T(8,128)S(1)} %copy-done.17), channel_id=1, source_target_pairs={{0,16},{16,32},{32,48},{48,64},{64,80},{80,96},{96,112},{1,17},{17... | collective-permute-start | bytes 98312 | tf_op jit(solution)/shard_map/ppermute | solution.py:338
  117.9 5.1 %collective-permute-start.6 = (f32[2,1,32,128]{3,2,1,0:T(8,128)S(1)}, f32[2,1,32,128]{3,2,1,0:T(8,128)S(1)}, u32[]{:S(2)}, u32[]{:S(2)}) collective-permute-start(f32[2,1,32,128]{3,2,1,0:T(8,128)S(1)} %copy-done.16), channel_id=1, source_target_pairs={{16,0},{32,16},{48,32},{64,48},{80,64},{96,80},{112,96},{17,1},{33... | collective-permute-start | bytes 98312 | tf_op jit(solution)/shard_map/ppermute | solution.py:338
  119.2 20.7 %copy-start.6 = (f32[2,1,32,128]{3,2,1,0:T(8,128)}, f32[2,1,32,128]{3,2,1,0:T(8,128)S(1)}, u32[]{:S(2)}) copy-start(f32[2,1,32,128]{3,2,1,0:T(8,128)S(1)} %collective-permute-done.5.xlo) | copy-start | bytes 98308
  123.0 16.9 %copy-start.7 = (f32[2,1,32,128]{3,2,1,0:T(8,128)}, f32[2,1,32,128]{3,2,1,0:T(8,128)S(1)}, u32[]{:S(2)}) copy-start(f32[2,1,32,128]{3,2,1,0:T(8,128)S(1)} %collective-permute-done.6.xhi) | copy-start | bytes 98308
  125.5 0.7 copy-start.3
  139.9 3.8 %collective-permute-start.7 = (f32[2,1,512]{2,1,0:T(1,128)}, f32[2,1,512]{2,1,0:T(1,128)S(1)}, u32[]{:S(2)}, u32[]{:S(2)}) collective-permute-start(f32[2,1,512]{2,1,0:T(1,128)} %get-tuple-element.94), channel_id=1, source_target_pairs={{0,1},{1,2},{2,3},{3,4},{4,5},{5,6},{6,7},{7,8},{8,9},{9,10},{10,1... | collective-permute-start | bytes 12296 | tf_op jit(solution)/shard_map/ppermute | solution.py:395
  143.7 0.6 copy-start.12
  152.1 12.1 %copy-start.20 = (f32[2,16,1,128]{3,2,1,0:T(1,128)S(1)}, f32[2,16,1,128]{3,2,1,0:T(1,128)}, u32[]{:S(2)}) copy-start(f32[2,16,1,128]{3,2,1,0:T(1,128)} %get-tuple-element.101) | copy-start | bytes 49156
  152.1 15.7 %copy-start.18 = (f32[2,16,1,128]{3,2,1,0:T(1,128)S(1)}, f32[2,16,1,128]{3,2,1,0:T(1,128)}, u32[]{:S(2)}) copy-start(f32[2,16,1,128]{3,2,1,0:T(1,128)} %get-tuple-element.102) | copy-start | bytes 49156
  152.1 23.1 %all-to-all-start.3 = ((f32[128,4,128]{2,1,0:T(4,128)}), f32[128,4,128]{2,1,0:T(4,128)S(1)}, u32[]{:S(2)}, u32[]{:S(2)}) async-start(f32[128,4,128]{2,1,0:T(4,128)} %get-tuple-element.95), calls=%async_computation.3 | async-start | bytes 524288 | tf_op jit(solution)/shard_map/all_to_all | solution.py:346
  164.2 5.5 %collective-permute-start.8 = (f32[2,16,1,128]{3,2,1,0:T(1,128)S(1)}, f32[2,16,1,128]{3,2,1,0:T(1,128)S(1)}, u32[]{:S(2)}, u32[]{:S(2)}) collective-permute-start(f32[2,16,1,128]{3,2,1,0:T(1,128)S(1)} %copy-done.20), channel_id=1, source_target_pairs={{0,1},{1,2},{2,3},{3,4},{4,5},{5,6},{6,7},{7,8},{8,9},{9,10},{10,1... | collective-permute-start | bytes 49160 | tf_op jit(solution)/shard_map/ppermute | solution.py:338
  167.8 5.4 %collective-permute-start.9 = (f32[2,16,1,128]{3,2,1,0:T(1,128)S(1)}, f32[2,16,1,128]{3,2,1,0:T(1,128)S(1)}, u32[]{:S(2)}, u32[]{:S(2)}) collective-permute-start(f32[2,16,1,128]{3,2,1,0:T(1,128)S(1)} %copy-done.18), channel_id=1, source_target_pairs={{1,0},{2,1},{3,2},{4,3},{5,4},{6,5},{7,6},{8,7},{9,8},{10,9},{11,1... | collective-permute-start | bytes 49160 | tf_op jit(solution)/shard_map/ppermute | solution.py:338
  169.7 5.5 %copy-start.10 = (f32[2,16,1,128]{3,2,1,0:T(1,128)}, f32[2,16,1,128]{3,2,1,0:T(1,128)S(1)}, u32[]{:S(2)}) copy-start(f32[2,16,1,128]{3,2,1,0:T(1,128)S(1)} %collective-permute-done.8.ylo) | copy-start | bytes 49156
  173.1 2.1 %copy-start.11 = (f32[2,16,1,128]{3,2,1,0:T(1,128)}, f32[2,16,1,128]{3,2,1,0:T(1,128)S(1)}, u32[]{:S(2)}) copy-start(f32[2,16,1,128]{3,2,1,0:T(1,128)S(1)} %collective-permute-done.9.yhi) | copy-start | bytes 49156
  175.3 0.7 copy-start

commit v5 on v4

--- a/solution.py
+++ b/solution.py
@@ -8,7 +8,7 @@
 i32, f32, bf16 = jnp.int32, jnp.float32, jnp.bfloat16
 VM = pl.BlockSpec(memory_space=pltpu.VMEM)
 SM = pl.BlockSpec(memory_space=pltpu.SMEM)
-W, NB = 64, 16
+W, NB, UN = 80, 16, 2
 neutral_step = 0.4
 ion_factor = 0.5
 
@@ -66,11 +66,10 @@
     return jnp.where(idx < 128, take(x[:, :128], low), take(x[:, 128:], low))
 
 
-def slot_keys(order, first, turn, slots):
+def slot_tile(order, first, turn, j, slots):
     lane = lax.broadcasted_iota(i32, (128, 128), 1)
-    for j in range(8):
-        idx = take(first[...], 8*j + (lane >> 4)) + 16*turn + (lane & 15)
-        slots[j*128:(j+1)*128, :] = (take2(order, jnp.minimum(idx, 255)) & 1023).T
+    idx = take(first[...], 8*j + (lane >> 4)) + 16*turn + (lane & 15)
+    slots[pl.ds(pl.multiple_of(j*128, 128), 128), :] = (take2(order, jnp.minimum(idx, 255)) & 1023).T
 
 
 def sort_side(key16, cell_ref, pos_ref, bnd_ref, slot_ref, order_ref, first_ref, place_ref, ctl_ref):
@@ -101,7 +100,8 @@
     first_ref[...] = first
     order = cell.T
     order_ref[...] = order
-    slot_keys(order, first_ref, 0, slot_ref)
+    for j in range(8):
+        slot_tile(order, first_ref, 0, j, slot_ref)
     b = order >> 10
     w = c - jnp.concatenate([take(first, b[:, :128]), take(first, b[:, 128:])], axis=1)
     place = (pos << 14) + ((w >> 4) << 10) + (b << 4) + (w & 15)
@@ -147,49 +147,62 @@
 
 def lookup(ctl, slot, order, first, place, t_ref, wire, s_ref, key_ref, gain=None):
     half = t_ref.shape[1] // 2
-    key_ref[...] = slot[...]
+
+    def group(g, keys):
+        for b in range(8):
+            rows = []
+            for j in range(8):
+                at = g*32 + 4*b + j//2 + (j % 2)*half
+                rows.append([jnp.broadcast_to(t_ref[k, pl.ds(at, 1), :], (8, 128)) for k in range(2)])
+            for i in range(2):
+                sl = pl.ds(pl.multiple_of(g*128 + b*16 + i*8, 8), 8)
+                key = keys[sl, :]
+                sub, lev = key >> 7, key & 127
+                acc = [take(rows[0][k], lev) for k in range(2)]
+                for j in range(1, 8):
+                    m = sub == j
+                    for k in range(2):
+                        acc[k] = jnp.where(m, take(rows[j][k], lev), acc[k])
+                for k in range(2):
+                    s_ref[k, sl, :] = acc[k]
+
+    def each(g, _):
+        group(g, slot)
+        return 0
+
+    def scaled(x, h):
+        return x if gain is None else x * gain[:, h*128:(h+1)*128]
+
+    lax.fori_loop(0, 8, each, 0)
+    parts = [[s_ref[k, j*128:(j+1)*128, :].T for j in range(8)] for k in range(2)]
+    for h in range(2):
+        at = place[:, h*128:(h+1)*128]
+        low, tile = at & 127, (at >> 7) & 7
+        for k in range(2):
+            x = take(parts[k][0], low)
+            for j in range(1, 8):
+                x = jnp.where(tile == j, take(parts[k][j], low), x)
+            wire[:, 2*k+h, :] = scaled(x, h)
 
     def turn(t, _):
-        @pl.when(t > 0)
-        def _():
-            slot_keys(order[...], first, t, key_ref)
-
-        def group(g, _):
+        def late(g, _):
             @pl.when(ctl[g, 0] > 16*t)
             def _():
-                for b in range(8):
-                    rows = []
-                    for j in range(8):
-                        at = g*32 + 4*b + j//2 + (j % 2)*half
-                        rows.append([jnp.broadcast_to(t_ref[k, pl.ds(at, 1), :], (8, 128)) for k in range(2)])
-                    for i in range(2):
-                        sl = pl.ds(pl.multiple_of(g*128 + b*16 + i*8, 8), 8)
-                        key = key_ref[sl, :]
-                        sub, lev = key >> 7, key & 127
-                        acc = [take(rows[0][k], lev) for k in range(2)]
-                        for j in range(1, 8):
-                            m = sub == j
-                            for k in range(2):
-                                acc[k] = jnp.where(m, take(rows[j][k], lev), acc[k])
-                        for k in range(2):
-                            s_ref[k, sl, :] = acc[k]
+                slot_tile(order[...], first, t, g, key_ref)
+                group(g, key_ref)
+                tile = pl.ds(pl.multiple_of(g*128, 128), 128)
+                for h in range(2):
+                    at = place[:, h*128:(h+1)*128]
+                    mine = (at >> 7) == 8*t + g
+                    for k in range(2):
+                        x = take(s_ref[k, tile, :].T, at & 127)
+                        wire[:, 2*k+h, :] = jnp.where(mine, scaled(x, h), wire[:, 2*k+h, :])
             return 0
 
-        lax.fori_loop(0, 8, group, 0)
-        parts = [[s_ref[k, j*128:(j+1)*128, :].T for j in range(8)] for k in range(2)]
-        for h in range(2):
-            at = place[:, h*128:(h+1)*128]
-            low, tile, mine = at & 127, (at >> 7) & 7, (at >> 10) == t
-            for k in range(2):
-                x = take(parts[k][0], low)
-                for j in range(1, 8):
-                    x = jnp.where(tile == j, take(parts[k][j], low), x)
-                if gain is not None:
-                    x = x * gain[:, h*128:(h+1)*128]
-                wire[:, 2*k+h, :] = jnp.where(mine, x, wire[:, 2*k+h, :])
+        lax.fori_loop(0, 8, late, 0)
         return 0
 
-    lax.fori_loop(0, (ctl[0, 1] + 15) // 16, turn, 0)
+    lax.fori_loop(1, (ctl[0, 1] + 15) // 16, turn, 0)
 
 
 def scatter_add(bnd, cell_ref, val_ref, acc_ref):
@@ -200,35 +213,45 @@
     def spread(x, n):
         return jnp.broadcast_to(x, (n, 128)).astype(bf16)
 
-    def block(v, _):
+    def begin(v):
+        return ((bnd[v*(NB//8), 0] >> 1) // 8) * 8
+
+    def window(v, rb):
+        rb = pl.multiple_of(rb, 8)
         sl = pl.ds(pl.multiple_of(v*NB, 8), NB)
         key = cell_ref[sl, :]
-        q, lane = key >> 8, (key & 255).astype(f32)
-        lo, hi = bnd[v*(NB//8), 0] >> 1, bnd[(v+1)*(NB//8) - 1, 1] >> 1
-        base = (lo // 8) * 8
+        rel, lane = ((key >> 8) - rb).astype(f32), (key & 255).astype(f32)
         vals = []
         for k in range(2):
             x = val_ref[k, sl, :]
             h = x.astype(bf16).astype(f32)
             vals += [h, x - h]
-        lanes = jnp.concatenate([jnp.where(iota == spread(lane[r:r+1], 256), one, zero) for r in range(NB)], axis=1)
-
-        def window(it, _):
-            rb = pl.multiple_of(base + it*W, 8)
-            rel = (q - rb).astype(f32)
-            rows = []
-            for r in range(NB):
-                m = iota[:W] == spread(rel[r:r+1], W)
-                rows.append(jnp.concatenate([jnp.where(m, spread(x[r:r+1], W), zero[:W]) for x in vals], axis=0))
-            z = lax.dot_general(jnp.concatenate(rows, axis=1), lanes, (((1,), (1,)), ((), ())), preferred_element_type=f32)
-            for k in range(2):
-                acc_ref[k, pl.ds(rb, W), :] += z[2*k*W:(2*k+1)*W] + z[(2*k+1)*W:(2*k+2)*W]
+        rows, lanes = [], []
+        for r in range(NB):
+            lanes.append(jnp.where(iota == spread(lane[r:r+1], 256), one, zero))
+            m = iota[:W] == spread(rel[r:r+1], W)
+            rows.append(jnp.concatenate([jnp.where(m, spread(x[r:r+1], W), zero[:W]) for x in vals], axis=0))
+        z = lax.dot_general(
+            jnp.concatenate(rows, axis=1), jnp.concatenate(lanes, axis=1),
+            (((1,), (1,)), ((), ())), preferred_element_type=f32)
+        for k in range(2):
+            acc_ref[k, pl.ds(rb, W), :] += z[2*k*W:(2*k+1)*W] + z[(2*k+1)*W:(2*k+2)*W]
+
+    def block(v, _):
+        window(v, begin(v))
+        return 0
+
+    def rest(v, _):
+        base = begin(v)
+
+        def more(it, _):
+            window(v, base + it*W)
             return 0
 
-        lax.fori_loop(0, (hi - base)//W + 1, window, 0)
-        return 0
-
-    lax.fori_loop(0, 256//NB, block, 0)
+        return lax.fori_loop(1, ((bnd[(v+1)*(NB//8) - 1, 1] >> 1) - base)//W + 1, more, 0)
+
+    lax.fori_loop(0, 256//NB, block, 0, unroll=UN)
+    lax.fori_loop(0, 256//NB, rest, 0)
 
 
 def from_wire(pos, wire, val, gain=None):

time: 192 us -> 181 us (0.943); the launches traced: 189 us -> 180 us
  Pallas kernels: 93.3 us -> 84.1 us
    pallas_call x9, Pallas kernels: 93.3 us -> 84.1 us  [call(): pl.pallas_call(kernel, out_shape=outs, in_specs=[SM] * smem + [VM] * (len...]
where the time goes in v5:
time: 181 us; the launch traced here: 180 us
  Pallas kernels  84.1 us (46%)
  starting transfers between devices  72 us (40%)
  waiting for transfers between devices  19.4 us (11%)
  local copies, waits for them, and re-layouts  4.06 us (2%)
    pallas_call x9, Pallas kernels, call(): pl.pallas_call(kernel, out_shape=outs, in_specs=[SM] * smem + [VM] * (len...  84.1 us
    all_to_all x4, starting transfers between devices, exchange(): lax.all_to_all(x, ('gx', 'gy'), split_axis=0, concat_axis=0, tiled=True)  45.1 us
    ppermute x4, starting transfers between devices, beside(): lax.ppermute(last, axis, up)  13.9 us
    ppermute x4, waiting for transfers between devices, beside(): lax.ppermute(first, axis, [(b, a) for a, b in up])  10.6 us
    all_to_all x4, waiting for transfers between devices, exchange(): lax.all_to_all(x, ('gx', 'gy'), split_axis=0, concat_axis=0, tiled=True)  6.84 us
    ppermute x4, starting transfers between devices, beside(): lax.ppermute(first, axis, [(b, a) for a, b in up])  6.61 us
    ppermute x2, starting transfers between devices, tubes(): up = lax.ppermute(out_last, 'gy', up_route)  6.37 us
    unnamed x44, local copies, waits for them, and re-layouts  4.06 us
  transfers between devices with their start and end apart: 14, of which 9 were waited for; matrix products, arithmetic and copies ran while one was open for 0% of the time, Pallas kernels for 3%

profile of v5, /device:TPU:1, one launch (start us, length us, event | category | flops | bytes accessed | tf_op | source)
XLA Modules:
  0.0 180.4 jit_solution(9925146769798031129)
XLA Ops:
  0.6 6.1 %tilesort.1 = (s32[256,128]{1,0:T(8,128)}, s32[128,256]{1,0:T(8,128)}, s32[32,128]{1,0:T(8,128)}, s32[1024,128]{1,0:T(8,128)}, s32[128,256]{1,0:T(8,128)}, /*ind...) custom-call(s32[1,128,256]{2,1,0:T(8,128)} %col.1, ...), custom_call_target="tpu_custom_call" | custom-call | tf_op jit(solution)/shard_map/tilesort/pallas_call | solution.py:348
  6.7 7.0 %first.1 = f32[128,4,128]{2,1,0:T(4,128)} custom-call(s32[8,128]{1,0:T(8,128)} %get-tuple-element.56.ctl, s32[1024,128]{1,0:T(8,128)} %get-tuple-element.57.slot, s32[128,256]{1,0:T(8,128)} %get-tuple-element.58.order, s32[128,128]{1,0:T(8,128)} %get-tuple-element.59.first, s32[128,256]{1,0:T(8,128)} %get-tuple-element.60.place, f32[2,512,128]{2,1,0:T(8,128)} %bitcast.4), custom_call_target="tpu_custom_call" | custom-call | tf_op jit(solution)/shard_map/first/pallas_call | solution.py:348
  13.7 12.4 %all-to-all-start = ((f32[128,4,128]{2,1,0:T(4,128)}), f32[128,4,128]{2,1,0:T(4,128)S(1)}, u32[]{:S(2)}, u32[]{:S(2)}) async-start(f32[128,4,128]{2,1,0:T(4,128)} %first.1), calls=%async_computation | async-start | bytes 524288 | tf_op jit(solution)/shard_map/all_to_all | solution.py:369
  26.1 3.4 %collective-permute-start = (f32[2,1,32,128]{3,2,1,0:T(8,128)S(1)}, f32[2,1,32,128]{3,2,1,0:T(8,128)S(1)}, u32[]{:S(2)}, u32[]{:S(2)}) collective-permute-start(f32[2,1,32,128]{3,2,1,0:T(8,128)S(1)} %copy-done.15), channel_id=1, source_target_pairs={{0,16},{16,32},{32,48},{48,64},{64,80},{80,96},{96,112},{1,17},{17... | collective-permute-start | bytes 98312 | tf_op jit(solution)/shard_map/ppermute | solution.py:361
  29.6 1.5 collective-permute-start.1
  31.0 6.0 %tubesort.1 = (s32[256,128]{1,0:T(8,128)}, s32[128,256]{1,0:T(8,128)}, s32[32,128]{1,0:T(8,128)}, s32[1024,128]{1,0:T(8,128)}, s32[128,256]{1,0:T(8,128)}, /*ind...) custom-call(s32[1,128,256]{2,1,0:T(8,128)} %tub, ...), custom_call_target="tpu_custom_call" | custom-call | tf_op jit(solution)/shard_map/tubesort/pallas_call | solution.py:348
  37.0 0.0 collective-permute-done.xlo
  37.1 0.0 collective-permute-done.1.xhi
  37.1 0.1 all-to-all-done.wire
  37.2 0.7 copy-done.1
  37.9 11.0 %tube.2 = (f32[2,128,512]{2,1,0:T(8,128)}, f32[2,128,512]{2,1,0:T(8,128)}, f32[2,1,512]{2,1,0:T(1,128)}) custom-call(s32[32,128]{1,0:T(8,128)} %get-tuple-element.71.bnd, f32[2,2]{1,0:T(2,128)} %coupling.3, s32[256,128]{1,0:T(8,128)} %get-tuple-element.72.cell, s32[128,256]{1,0:T(8,128)} %get-tuple-element.73.pos, f32[128,256]{1,0:T(8,128)} %get-tuple-element.69.gain.a_6_, ...), custom_call_target="tpu_custom_call" | custom-call | tf_op jit(solution)/shard_map/tube/pallas_call | solution.py:348
  48.9 0.0 copy-done.4
  48.9 3.6 %collective-permute-start.2 = (f32[2,1,512]{2,1,0:T(1,128)}, f32[2,1,512]{2,1,0:T(1,128)S(1)}, u32[]{:S(2)}, u32[]{:S(2)}) collective-permute-start(f32[2,1,512]{2,1,0:T(1,128)} %get-tuple-element.79), channel_id=1, source_target_pairs={{0,1},{1,2},{2,3},{3,4},{4,5},{5,6},{6,7},{7,8},{8,9},{9,10},{10,1... | collective-permute-start | bytes 12296 | tf_op jit(solution)/shard_map/ppermute | solution.py:418
  52.5 0.9 collective-permute-done.2.a_10_
  53.4 0.6 copy-done.13
  54.0 7.8 %drag.2 = (f32[2,128,512]{2,1,0:T(8,128)}, f32[128,4,128]{2,1,0:T(4,128)}) custom-call(s32[8,128]{1,0:T(8,128)} %get-tuple-element.64.a_0_, f32[2]{0:T(128)} %a_1_.3, s32[1024,128]{1,0:T(8,128)} %get-tuple-element.65.a_2_, s32[128,256]{1,0:T(8,128)} %get-tuple-element.66.a_3_, s32[128,128]{1,0:T(8,128)} %get-tuple-element.67.a_4_, ...), custom_call_target="tpu_custom_call" | custom-call | tf_op jit(solution)/shard_map/drag/pallas_call | solution.py:348
  61.8 13.0 %all-to-all-start.1 = ((f32[128,4,128]{2,1,0:T(4,128)}), f32[128,4,128]{2,1,0:T(4,128)S(1)}, u32[]{:S(2)}, u32[]{:S(2)}) async-start(f32[128,4,128]{2,1,0:T(4,128)} %get-tuple-element.80), calls=%async_computation.1 | async-start | bytes 524288 | tf_op jit(solution)/shard_map/all_to_all | solution.py:369
  74.8 3.5 %collective-permute-start.3 = (f32[2,16,1,128]{3,2,1,0:T(1,128)S(1)}, f32[2,16,1,128]{3,2,1,0:T(1,128)S(1)}, u32[]{:S(2)}, u32[]{:S(2)}) collective-permute-start(f32[2,16,1,128]{3,2,1,0:T(1,128)S(1)} %copy-done.21), channel_id=1, source_target_pairs={{0,1},{1,2},{2,3},{3,4},{4,5},{5,6},{6,7},{7,8},{8,9},{9,10},{10,1... | collective-permute-start | bytes 49160 | tf_op jit(solution)/shard_map/ppermute | solution.py:361
  78.4 1.9 %collective-permute-start.4 = (f32[2,16,1,128]{3,2,1,0:T(1,128)S(1)}, f32[2,16,1,128]{3,2,1,0:T(1,128)S(1)}, u32[]{:S(2)}, u32[]{:S(2)}) collective-permute-start(f32[2,16,1,128]{3,2,1,0:T(1,128)S(1)} %copy-done.19), channel_id=1, source_target_pairs={{1,0},{2,1},{3,2},{4,3},{5,4},{6,5},{7,6},{8,7},{9,8},{10,9},{11,1... | collective-permute-start | bytes 49160 | tf_op jit(solution)/shard_map/ppermute | solution.py:361
  80.3 0.0 collective-permute-done.3.ylo
  80.3 0.0 copy-start.8
  80.3 3.4 %collective-permute-done.4.yhi = f32[2,16,1,128]{3,2,1,0:T(1,128)S(1)} collective-permute-done((f32[2,16,1,128]{3,2,1,0:T(1,128)S(1)}, f32[2,16,1,128]{3,2,1,0:T(1,128)S(1)}, u32[]{:S(2)}, u32[]{:S(2)}) %collective-permute-start.4) | collective-permute-done | bytes 16416 | tf_op jit(solution)/shard_map/ppermute | solution.py:361
  83.7 2.1 %all-to-all-done.1.wire = f32[128,4,128]{2,1,0:T(4,128)S(1)} async-done(((f32[128,4,128]{2,1,0:T(4,128)}), f32[128,4,128]{2,1,0:T(4,128)S(1)}, u32[]{:S(2)}, u32[]{:S(2)}) %all-to-all-start.1) | async-done | bytes 262176 | tf_op jit(solution)/shard_map/all_to_all | solution.py:369
  85.9 0.7 copy-done.2
  86.6 16.5 %mid.1 = (f32[2,512,128]{2,1,0:T(8,128)}, f32[128,4,128]{2,1,0:T(4,128)}, f32[2,1,32,128]{3,2,1,0:T(8,128)}, f32[2,1,32,128]{3,2,1,0:T(8,128)}, f32[2,16,1,128]{3,2,1,0:T(1,128)}, /*index=5*/f32[2,16,1,128]{3,2,1,0:T(1,128)}) custom-call(s32[32,128]{1,0:T(8,128)} %get-tuple-element.53.bnd, s32[8,128]{1,0:T(8,128)} %get-tuple-element.56.ctl, ...), custom_call_target="tpu_custom_call" | custom-call | tf_op jit(solution)/shard_map/mid/pallas_call | solution.py:348
  103.0 7.6 %all-to-all-start.2 = ((f32[128,4,128]{2,1,0:T(4,128)}), f32[128,4,128]{2,1,0:T(4,128)S(1)}, u32[]{:S(2)}, u32[]{:S(2)}) async-start(f32[128,4,128]{2,1,0:T(4,128)} %get-tuple-element.87), calls=%async_computation.2 | async-start | bytes 524288 | tf_op jit(solution)/shard_map/all_to_all | solution.py:369
  110.6 0.0 copy-done.17
  110.6 3.4 %collective-permute-start.5 = (f32[2,1,32,128]{3,2,1,0:T(8,128)S(1)}, f32[2,1,32,128]{3,2,1,0:T(8,128)S(1)}, u32[]{:S(2)}, u32[]{:S(2)}) collective-permute-start(f32[2,1,32,128]{3,2,1,0:T(8,128)S(1)} %copy-done.17), channel_id=1, source_target_pairs={{0,16},{16,32},{32,48},{48,64},{64,80},{80,96},{96,112},{1,17},{17... | collective-permute-start | bytes 98312 | tf_op jit(solution)/shard_map/ppermute | solution.py:361
  114.0 1.3 collective-permute-start.6
  115.3 0.0 collective-permute-done.5.xlo
  115.4 3.8 %collective-permute-done.6.xhi = f32[2,1,32,128]{3,2,1,0:T(8,128)S(1)} collective-permute-done((f32[2,1,32,128]{3,2,1,0:T(8,128)S(1)}, f32[2,1,32,128]{3,2,1,0:T(8,128)S(1)}, u32[]{:S(2)}, u32[]{:S(2)}) %collective-permute-start.6) | collective-permute-done | bytes 32800 | tf_op jit(solution)/shard_map/ppermute | solution.py:361
  119.2 2.5 %all-to-all-done.2.wire = f32[128,4,128]{2,1,0:T(4,128)S(1)} async-done(((f32[128,4,128]{2,1,0:T(4,128)}), f32[128,4,128]{2,1,0:T(4,128)S(1)}, u32[]{:S(2)}, u32[]{:S(2)}) %all-to-all-start.2) | async-done | bytes 262176 | tf_op jit(solution)/shard_map/all_to_all | solution.py:369
  121.7 0.7 copy-done.3
  122.4 11.0 %tube.3 = (f32[2,128,512]{2,1,0:T(8,128)}, f32[2,128,512]{2,1,0:T(8,128)}, f32[2,1,512]{2,1,0:T(1,128)}) custom-call(s32[32,128]{1,0:T(8,128)} %get-tuple-element.71.bnd, f32[2,2]{1,0:T(2,128)} %coupling.3, s32[256,128]{1,0:T(8,128)} %get-tuple-element.72.cell, s32[128,256]{1,0:T(8,128)} %get-tuple-element.73.pos, f32[128,256]{1,0:T(8,128)} %get-tuple-element.69.gain.a_6_, ...), custom_call_target="tpu_custom_call" | custom-call | tf_op jit(solution)/shard_map/tube/pallas_call | solution.py:348
  133.3 0.0 copy-done.6
  133.3 2.8 %collective-permute-start.7 = (f32[2,1,512]{2,1,0:T(1,128)}, f32[2,1,512]{2,1,0:T(1,128)S(1)}, u32[]{:S(2)}, u32[]{:S(2)}) collective-permute-start(f32[2,1,512]{2,1,0:T(1,128)} %get-tuple-element.94), channel_id=1, source_target_pairs={{0,1},{1,2},{2,3},{3,4},{4,5},{5,6},{6,7},{7,8},{8,9},{9,10},{10,1... | collective-permute-start | bytes 12296 | tf_op jit(solution)/shard_map/ppermute | solution.py:418
  136.2 0.9 collective-permute-done.7.a_10_
  137.1 0.6 copy-done.12
  137.7 7.8 %drag.3 = (f32[2,128,512]{2,1,0:T(8,128)}, f32[128,4,128]{2,1,0:T(4,128)}) custom-call(s32[8,128]{1,0:T(8,128)} %get-tuple-element.64.a_0_, f32[2]{0:T(128)} %a_1_.3, s32[1024,128]{1,0:T(8,128)} %get-tuple-element.65.a_2_, s32[128,256]{1,0:T(8,128)} %get-tuple-element.66.a_3_, s32[128,128]{1,0:T(8,128)} %get-tuple-element.67.a_4_, ...), custom_call_target="tpu_custom_call" | custom-call | tf_op jit(solution)/shard_map/drag/pallas_call | solution.py:348
  145.5 12.1 %all-to-all-start.3 = ((f32[128,4,128]{2,1,0:T(4,128)}), f32[128,4,128]{2,1,0:T(4,128)S(1)}, u32[]{:S(2)}, u32[]{:S(2)}) async-start(f32[128,4,128]{2,1,0:T(4,128)} %get-tuple-element.95), calls=%async_computation.3 | async-start | bytes 524288 | tf_op jit(solution)/shard_map/all_to_all | solution.py:369
  157.6 3.5 %collective-permute-start.8 = (f32[2,16,1,128]{3,2,1,0:T(1,128)S(1)}, f32[2,16,1,128]{3,2,1,0:T(1,128)S(1)}, u32[]{:S(2)}, u32[]{:S(2)}) collective-permute-start(f32[2,16,1,128]{3,2,1,0:T(1,128)S(1)} %copy-done.20), channel_id=1, source_target_pairs={{0,1},{1,2},{2,3},{3,4},{4,5},{5,6},{6,7},{7,8},{8,9},{9,10},{10,1... | collective-permute-start | bytes 49160 | tf_op jit(solution)/shard_map/ppermute | solution.py:361
  161.2 0.0 copy-done.18
  161.2 1.9 %collective-permute-start.9 = (f32[2,16,1,128]{3,2,1,0:T(1,128)S(1)}, f32[2,16,1,128]{3,2,1,0:T(1,128)S(1)}, u32[]{:S(2)}, u32[]{:S(2)}) collective-permute-start(f32[2,16,1,128]{3,2,1,0:T(1,128)S(1)} %copy-done.18), channel_id=1, source_target_pairs={{1,0},{2,1},{3,2},{4,3},{5,4},{6,5},{7,6},{8,7},{9,8},{10,9},{11,1... | collective-permute-start | bytes 49160 | tf_op jit(solution)/shard_map/ppermute | solution.py:361
  163.1 0.0 collective-permute-done.8.ylo
  163.1 3.4 %collective-permute-done.9.yhi = f32[2,16,1,128]{3,2,1,0:T(1,128)S(1)} collective-permute-done((f32[2,16,1,128]{3,2,1,0:T(1,128)S(1)}, f32[2,16,1,128]{3,2,1,0:T(1,128)S(1)}, u32[]{:S(2)}, u32[]{:S(2)}) %collective-permute-start.9) | collective-permute-done | bytes 16416 | tf_op jit(solution)/shard_map/ppermute | solution.py:361
  166.5 2.1 %all-to-all-done.3.wire = f32[128,4,128]{2,1,0:T(4,128)S(1)} async-done(((f32[128,4,128]{2,1,0:T(4,128)}), f32[128,4,128]{2,1,0:T(4,128)S(1)}, u32[]{:S(2)}, u32[]{:S(2)}) %all-to-all-start.3) | async-done | bytes 262176 | tf_op jit(solution)/shard_map/all_to_all | solution.py:369
  168.7 0.7 copy-done
  169.4 11.0 %end.1 = f32[2,16,32,128]{3,2,1,0:T(8,128)} custom-call(s32[32,128]{1,0:T(8,128)} %get-tuple-element.53.bnd, s32[256,128]{1,0:T(8,128)} %get-tuple-element.54.cell, s32[128,256]{1,0:T(8,128)} %get-tuple-element.55.pos, f32[128,4,128]{2,1,0:T(4,128)} %copy-done, f32[2,16,32,128]{3,2,1,0:T(8,128)} %start.1, f32[2,16,32,128]{3,2,1,0:T(8,128)} %bitcast.5, ...), custom_call_target="tpu_custom_call" | custom-call | tf_op jit(solution)/shard_map/end/pallas_call | solution.py:348
  (33 shorter events, 0.1 us)
Async XLA Ops:
  13.7 12.4 %copy-start.15 = (f32[2,1,32,128]{3,2,1,0:T(8,128)S(1)}, f32[2,1,32,128]{3,2,1,0:T(8,128)}, u32[]{:S(2)}) copy-start(f32[2,1,32,128]{3,2,1,0:T(8,128)} %get-tuple-element.74) | copy-start | bytes 98308
  13.7 15.8 %copy-start.14 = (f32[2,1,32,128]{3,2,1,0:T(8,128)S(1)}, f32[2,1,32,128]{3,2,1,0:T(8,128)}, u32[]{:S(2)}) copy-start(f32[2,1,32,128]{3,2,1,0:T(8,128)} %get-tuple-element.75) | copy-start | bytes 98308
  13.7 23.5 %all-to-all-start = ((f32[128,4,128]{2,1,0:T(4,128)}), f32[128,4,128]{2,1,0:T(4,128)S(1)}, u32[]{:S(2)}, u32[]{:S(2)}) async-start(f32[128,4,128]{2,1,0:T(4,128)} %first.1), calls=%async_computation | async-start | bytes 524288 | tf_op jit(solution)/shard_map/all_to_all | solution.py:369
  26.1 10.9 %collective-permute-start = (f32[2,1,32,128]{3,2,1,0:T(8,128)S(1)}, f32[2,1,32,128]{3,2,1,0:T(8,128)S(1)}, u32[]{:S(2)}, u32[]{:S(2)}) collective-permute-start(f32[2,1,32,128]{3,2,1,0:T(8,128)S(1)} %copy-done.15), channel_id=1, source_target_pairs={{0,16},{16,32},{32,48},{48,64},{64,80},{80,96},{96,112},{1,17},{17... | collective-permute-start | bytes 98312 | tf_op jit(solution)/shard_map/ppermute | solution.py:361
  29.6 7.5 %collective-permute-start.1 = (f32[2,1,32,128]{3,2,1,0:T(8,128)S(1)}, f32[2,1,32,128]{3,2,1,0:T(8,128)S(1)}, u32[]{:S(2)}, u32[]{:S(2)}) collective-permute-start(f32[2,1,32,128]{3,2,1,0:T(8,128)S(1)} %copy-done.14), channel_id=1, source_target_pairs={{16,0},{32,16},{48,32},{64,48},{80,64},{96,80},{112,96},{17,1},{33... | collective-permute-start | bytes 98312 | tf_op jit(solution)/shard_map/ppermute | solution.py:361
  37.1 11.9 %copy-start.4 = (f32[2,1,32,128]{3,2,1,0:T(8,128)}, f32[2,1,32,128]{3,2,1,0:T(8,128)S(1)}, u32[]{:S(2)}) copy-start(f32[2,1,32,128]{3,2,1,0:T(8,128)S(1)} %collective-permute-done.xlo) | copy-start | bytes 98308
  37.1 11.8 %copy-start.5 = (f32[2,1,32,128]{3,2,1,0:T(8,128)}, f32[2,1,32,128]{3,2,1,0:T(8,128)S(1)}, u32[]{:S(2)}) copy-start(f32[2,1,32,128]{3,2,1,0:T(8,128)S(1)} %collective-permute-done.1.xhi) | copy-start | bytes 98308
  37.2 0.7 copy-start.1
  48.9 4.5 %collective-permute-start.2 = (f32[2,1,512]{2,1,0:T(1,128)}, f32[2,1,512]{2,1,0:T(1,128)S(1)}, u32[]{:S(2)}, u32[]{:S(2)}) collective-permute-start(f32[2,1,512]{2,1,0:T(1,128)} %get-tuple-element.79), channel_id=1, source_target_pairs={{0,1},{1,2},{2,3},{3,4},{4,5},{5,6},{6,7},{7,8},{8,9},{9,10},{10,1... | collective-permute-start | bytes 12296 | tf_op jit(solution)/shard_map/ppermute | solution.py:418
  53.4 0.6 copy-start.13
  61.8 13.0 %copy-start.21 = (f32[2,16,1,128]{3,2,1,0:T(1,128)S(1)}, f32[2,16,1,128]{3,2,1,0:T(1,128)}, u32[]{:S(2)}) copy-start(f32[2,16,1,128]{3,2,1,0:T(1,128)} %get-tuple-element.85) | copy-start | bytes 49156
  61.8 16.6 %copy-start.19 = (f32[2,16,1,128]{3,2,1,0:T(1,128)S(1)}, f32[2,16,1,128]{3,2,1,0:T(1,128)}, u32[]{:S(2)}) copy-start(f32[2,16,1,128]{3,2,1,0:T(1,128)} %get-tuple-element.86) | copy-start | bytes 49156
  61.8 24.1 %all-to-all-start.1 = ((f32[128,4,128]{2,1,0:T(4,128)}), f32[128,4,128]{2,1,0:T(4,128)S(1)}, u32[]{:S(2)}, u32[]{:S(2)}) async-start(f32[128,4,128]{2,1,0:T(4,128)} %get-tuple-element.80), calls=%async_computation.1 | async-start | bytes 524288 | tf_op jit(solution)/shard_map/all_to_all | solution.py:369
  74.8 5.5 %collective-permute-start.3 = (f32[2,16,1,128]{3,2,1,0:T(1,128)S(1)}, f32[2,16,1,128]{3,2,1,0:T(1,128)S(1)}, u32[]{:S(2)}, u32[]{:S(2)}) collective-permute-start(f32[2,16,1,128]{3,2,1,0:T(1,128)S(1)} %copy-done.21), channel_id=1, source_target_pairs={{0,1},{1,2},{2,3},{3,4},{4,5},{5,6},{6,7},{7,8},{8,9},{9,10},{10,1... | collective-permute-start | bytes 49160 | tf_op jit(solution)/shard_map/ppermute | solution.py:361
  78.4 5.4 %collective-permute-start.4 = (f32[2,16,1,128]{3,2,1,0:T(1,128)S(1)}, f32[2,16,1,128]{3,2,1,0:T(1,128)S(1)}, u32[]{:S(2)}, u32[]{:S(2)}) collective-permute-start(f32[2,16,1,128]{3,2,1,0:T(1,128)S(1)} %copy-done.19), channel_id=1, source_target_pairs={{1,0},{2,1},{3,2},{4,3},{5,4},{6,5},{7,6},{8,7},{9,8},{10,9},{11,1... | collective-permute-start | bytes 49160 | tf_op jit(solution)/shard_map/ppermute | solution.py:361
  80.3 5.5 %copy-start.8 = (f32[2,16,1,128]{3,2,1,0:T(1,128)}, f32[2,16,1,128]{3,2,1,0:T(1,128)S(1)}, u32[]{:S(2)}) copy-start(f32[2,16,1,128]{3,2,1,0:T(1,128)S(1)} %collective-permute-done.3.ylo) | copy-start | bytes 49156
  83.7 2.1 %copy-start.9 = (f32[2,16,1,128]{3,2,1,0:T(1,128)}, f32[2,16,1,128]{3,2,1,0:T(1,128)S(1)}, u32[]{:S(2)}) copy-start(f32[2,16,1,128]{3,2,1,0:T(1,128)S(1)} %collective-permute-done.4.yhi) | copy-start | bytes 49156
  85.9 0.7 copy-start.2
  103.0 7.6 %copy-start.17 = (f32[2,1,32,128]{3,2,1,0:T(8,128)S(1)}, f32[2,1,32,128]{3,2,1,0:T(8,128)}, u32[]{:S(2)}) copy-start(f32[2,1,32,128]{3,2,1,0:T(8,128)} %get-tuple-element.88) | copy-start | bytes 98308
  103.0 11.0 %copy-start.16 = (f32[2,1,32,128]{3,2,1,0:T(8,128)S(1)}, f32[2,1,32,128]{3,2,1,0:T(8,128)}, u32[]{:S(2)}) copy-start(f32[2,1,32,128]{3,2,1,0:T(8,128)} %get-tuple-element.89) | copy-start | bytes 98308
  103.0 18.6 %all-to-all-start.2 = ((f32[128,4,128]{2,1,0:T(4,128)}), f32[128,4,128]{2,1,0:T(4,128)S(1)}, u32[]{:S(2)}, u32[]{:S(2)}) async-start(f32[128,4,128]{2,1,0:T(4,128)} %get-tuple-element.87), calls=%async_computation.2 | async-start | bytes 524288 | tf_op jit(solution)/shard_map/all_to_all | solution.py:369
  110.6 4.7 %collective-permute-start.5 = (f32[2,1,32,128]{3,2,1,0:T(8,128)S(1)}, f32[2,1,32,128]{3,2,1,0:T(8,128)S(1)}, u32[]{:S(2)}, u32[]{:S(2)}) collective-permute-start(f32[2,1,32,128]{3,2,1,0:T(8,128)S(1)} %copy-done.17), channel_id=1, source_target_pairs={{0,16},{16,32},{32,48},{48,64},{64,80},{80,96},{96,112},{1,17},{17... | collective-permute-start | bytes 98312 | tf_op jit(solution)/shard_map/ppermute | solution.py:361
  114.0 5.1 %collective-permute-start.6 = (f32[2,1,32,128]{3,2,1,0:T(8,128)S(1)}, f32[2,1,32,128]{3,2,1,0:T(8,128)S(1)}, u32[]{:S(2)}, u32[]{:S(2)}) collective-permute-start(f32[2,1,32,128]{3,2,1,0:T(8,128)S(1)} %copy-done.16), channel_id=1, source_target_pairs={{16,0},{32,16},{48,32},{64,48},{80,64},{96,80},{112,96},{17,1},{33... | collective-permute-start | bytes 98312 | tf_op jit(solution)/shard_map/ppermute | solution.py:361
  115.3 18.0 %copy-start.6 = (f32[2,1,32,128]{3,2,1,0:T(8,128)}, f32[2,1,32,128]{3,2,1,0:T(8,128)S(1)}, u32[]{:S(2)}) copy-start(f32[2,1,32,128]{3,2,1,0:T(8,128)S(1)} %collective-permute-done.5.xlo) | copy-start | bytes 98308
  119.2 14.2 %copy-start.7 = (f32[2,1,32,128]{3,2,1,0:T(8,128)}, f32[2,1,32,128]{3,2,1,0:T(8,128)S(1)}, u32[]{:S(2)}) copy-start(f32[2,1,32,128]{3,2,1,0:T(8,128)S(1)} %collective-permute-done.6.xhi) | copy-start | bytes 98308
  121.7 0.7 copy-start.3
  133.3 3.8 %collective-permute-start.7 = (f32[2,1,512]{2,1,0:T(1,128)}, f32[2,1,512]{2,1,0:T(1,128)S(1)}, u32[]{:S(2)}, u32[]{:S(2)}) collective-permute-start(f32[2,1,512]{2,1,0:T(1,128)} %get-tuple-element.94), channel_id=1, source_target_pairs={{0,1},{1,2},{2,3},{3,4},{4,5},{5,6},{6,7},{7,8},{8,9},{9,10},{10,1... | collective-permute-start | bytes 12296 | tf_op jit(solution)/shard_map/ppermute | solution.py:418
  137.1 0.6 copy-start.12
  145.5 12.1 %copy-start.20 = (f32[2,16,1,128]{3,2,1,0:T(1,128)S(1)}, f32[2,16,1,128]{3,2,1,0:T(1,128)}, u32[]{:S(2)}) copy-start(f32[2,16,1,128]{3,2,1,0:T(1,128)} %get-tuple-element.101) | copy-start | bytes 49156
  145.5 15.7 %copy-start.18 = (f32[2,16,1,128]{3,2,1,0:T(1,128)S(1)}, f32[2,16,1,128]{3,2,1,0:T(1,128)}, u32[]{:S(2)}) copy-start(f32[2,16,1,128]{3,2,1,0:T(1,128)} %get-tuple-element.102) | copy-start | bytes 49156
  145.5 23.2 %all-to-all-start.3 = ((f32[128,4,128]{2,1,0:T(4,128)}), f32[128,4,128]{2,1,0:T(4,128)S(1)}, u32[]{:S(2)}, u32[]{:S(2)}) async-start(f32[128,4,128]{2,1,0:T(4,128)} %get-tuple-element.95), calls=%async_computation.3 | async-start | bytes 524288 | tf_op jit(solution)/shard_map/all_to_all | solution.py:369
  157.6 5.5 %collective-permute-start.8 = (f32[2,16,1,128]{3,2,1,0:T(1,128)S(1)}, f32[2,16,1,128]{3,2,1,0:T(1,128)S(1)}, u32[]{:S(2)}, u32[]{:S(2)}) collective-permute-start(f32[2,16,1,128]{3,2,1,0:T(1,128)S(1)} %copy-done.20), channel_id=1, source_target_pairs={{0,1},{1,2},{2,3},{3,4},{4,5},{5,6},{6,7},{7,8},{8,9},{9,10},{10,1... | collective-permute-start | bytes 49160 | tf_op jit(solution)/shard_map/ppermute | solution.py:361
  161.2 5.4 %collective-permute-start.9 = (f32[2,16,1,128]{3,2,1,0:T(1,128)S(1)}, f32[2,16,1,128]{3,2,1,0:T(1,128)S(1)}, u32[]{:S(2)}, u32[]{:S(2)}) collective-permute-start(f32[2,16,1,128]{3,2,1,0:T(1,128)S(1)} %copy-done.18), channel_id=1, source_target_pairs={{1,0},{2,1},{3,2},{4,3},{5,4},{6,5},{7,6},{8,7},{9,8},{10,9},{11,1... | collective-permute-start | bytes 49160 | tf_op jit(solution)/shard_map/ppermute | solution.py:361
  163.1 5.5 %copy-start.10 = (f32[2,16,1,128]{3,2,1,0:T(1,128)}, f32[2,16,1,128]{3,2,1,0:T(1,128)S(1)}, u32[]{:S(2)}) copy-start(f32[2,16,1,128]{3,2,1,0:T(1,128)S(1)} %collective-permute-done.8.ylo) | copy-start | bytes 49156
  166.5 2.1 %copy-start.11 = (f32[2,16,1,128]{3,2,1,0:T(1,128)}, f32[2,16,1,128]{3,2,1,0:T(1,128)S(1)}, u32[]{:S(2)}) copy-start(f32[2,16,1,128]{3,2,1,0:T(1,128)S(1)} %collective-permute-done.9.yhi) | copy-start | bytes 49156
  168.7 0.7 copy-start

commit v6 on v5

--- a/solution.py
+++ b/solution.py
@@ -112,28 +112,50 @@
     return ((row & 255) << 8) + ((row >> 8) << 7) + lane
 
 
-def put_edges(get, xa, xb, ya, yb):
-    for k in range(2):
-        xa[k, 0] = get(k, 0)
-        n = ya.shape[1]
-        xb[k, 0] = get(k, n-1)
-        for i in range(n):
-            u = get(k, i)
-            ya[k, i] = u[:1]
-            yb[k, i] = u[-1:]
-
-
-def tile_sort_kernel(col, lev, wind, *outs):
-    side, edge = outs[:8], outs[8:]
+def put_edges(t, wire):
+    CX, CY = 16, t.shape[1] // 16
+    for k in range(2):
+        wire[k*CY:(k+1)*CY, 2, 0, :] = t[k, (CX-1)*CY:CX*CY, :]
+        wire[(2+k)*CY:(3+k)*CY, 2, 0, :] = t[k, :CY, :]
+        for i in range(CX):
+            wire[k*CX+i:k*CX+i+1, 2, 1, :] = t[k, (i+1)*CY-1:(i+1)*CY, :]
+            wire[(2+k)*CX+i:(2+k)*CX+i+1, 2, 1, :] = t[k, i*CY:i*CY+1, :]
+    wire[4*CX:, 2, 1, :] = jnp.zeros((128 - 4*CX, 128), f32)
+
+
+def place_of():
+    x, y = lax.axis_index("gx"), lax.axis_index("gy")
+    return x, y, x * lax.axis_size("gy") + y
+
+
+def pass_edges(wire, out):
+    q = place_of()[2]
+    step = lax.axis_size("gy")
+    for r, (cut, d) in enumerate(((64, step), (32, 1))):
+        x = wire[:, 2, r, :]
+        out[r] = jnp.where(q < cut, pltpu.roll(x, d, 0), pltpu.roll(x, 128-d, 0))
+
+
+def beside_tile(wire):
+    x, y = place_of()[:2]
+    a, b = wire[:, 2, 0, :], wire[:64, 2, 1, :]
+    return (
+        jnp.where(x > 0, a[:64], 0.0),
+        jnp.where(x < lax.axis_size("gx") - 1, a[64:], 0.0),
+        jnp.where(y > 0, b[:32], 0.0),
+        jnp.where(y < lax.axis_size("gy") - 1, b[32:], 0.0),
+    )
+
+
+def tile_sort_kernel(col, lev, *side):
     sort_side(cell_key(col[0], lev[0]), *side)
-    put_edges(lambda k, i: wind[k, i], *edge)
 
 
 def tube_sort_kernel(tub, pnt, weight, count, drift, *outs):
     side, gain, drift_out = outs[:8], outs[8], outs[9]
     p = pnt[0]
     sort_side(cell_key((p >> 7)*128 + tub[0], p & 127), *side)
-    own = lax.axis_index("gx") * lax.axis_size("gy") + lax.axis_index("gy")
+    own = place_of()[2]
     lane = lax.broadcasted_iota(i32, (128, 128), 1)
     live = jnp.sum(jnp.where(lane == own, count[...], 0).astype(f32), axis=1, keepdims=True)
     c = lax.broadcasted_iota(i32, (128, 256), 1).astype(f32)
@@ -182,7 +204,7 @@
             x = take(parts[k][0], low)
             for j in range(1, 8):
                 x = jnp.where(tile == j, take(parts[k][j], low), x)
-            wire[:, 2*k+h, :] = scaled(x, h)
+            wire[:, k, h, :] = scaled(x, h)
 
     def turn(t, _):
         def late(g, _):
@@ -196,7 +218,7 @@
                     mine = (at >> 7) == 8*t + g
                     for k in range(2):
                         x = take(s_ref[k, tile, :].T, at & 127)
-                        wire[:, 2*k+h, :] = jnp.where(mine, scaled(x, h), wire[:, 2*k+h, :])
+                        wire[:, k, h, :] = jnp.where(mine, scaled(x, h), wire[:, k, h, :])
             return 0
 
         lax.fori_loop(0, 8, late, 0)
@@ -256,7 +278,7 @@
 
 def from_wire(pos, wire, val, gain=None):
     for k in range(2):
-        x = [wire[:, 2*k+h, :] for h in range(2)]
+        x = [wire[:, k, h, :] for h in range(2)]
         if gain is not None:
             x = [x[h] * gain[:, h*128:(h+1)*128] for h in range(2)]
         o = permute_lanes(jnp.concatenate(x, axis=1), pos[...])
@@ -265,10 +287,12 @@
 
 
 def gather_kernel(ctl, slot, order, first, place, t, wire, s, keys):
+    put_edges(t, wire)
     lookup(ctl, slot, order, first, place, t, wire, s, keys)
 
 
-def tube_kernel(bnd, coupling, cell, pos, gain, drift, wire, ions, inverse, w_out, smooth_out, last_out, val, acc):
+def tube_kernel(bnd, coupling, cell, pos, gain, drift, wire, ions, inverse, w_out, smooth_out, last_out, edge_out, val, acc):
+    pass_edges(wire, edge_out)
     from_wire(pos, wire, val, gain)
     scatter_add(bnd, cell, val, acc)
     w = []
@@ -285,7 +309,9 @@
         last_out[k] = drift[127:128, :1] * sm[127:128, :]
 
 
-def drag_kernel(last, ctl, drag, slot, order, first_at, place, gain, drift, w, smooth, up, ions, n_out, wire, t, s, keys):
+def drag_kernel(last, ctl, drag, slot, order, first_at, place, gain, drift, w, smooth, up, ions, edge, n_out, wire, t, s, keys):
+    for r in range(2):
+        wire[:, 2, r, :] = edge[r]
     first = lax.broadcasted_iota(i32, (128, 128), 0) == 0
     d = drift[...]
     n = [[], []]
@@ -305,23 +331,24 @@
     lookup(ctl, slot, order, first_at, place, t, wire, s, keys, gain)
 
 
-def tend_all(wind, forcing, visc, xlo, xhi, ylo, yhi, acc, emit):
+def tend_all(wind, forcing, visc, wire, acc, emit):
     CX, CY = wind.shape[1], wind.shape[2]
+    xlo, xhi, ylo, yhi = beside_tile(wire)
     sub = lax.broadcasted_iota(i32, (CY, 128), 0)
     lane = lax.broadcasted_iota(i32, (CY, 128), 1)
     v = jnp.broadcast_to(visc[...], (CY, 128))
     for k in range(2):
         for i in range(CX):
             u = wind[k, i]
-            b = (wind[k, i+1] if i < CX-1 else xhi[k, 0]) + (wind[k, i-1] if i > 0 else xlo[k, 0])
-            nxt = jnp.where(sub == CY-1, jnp.broadcast_to(yhi[k, i], (CY, 128)), pltpu.roll(u, CY-1, 0))
-            prv = jnp.where(sub == 0, jnp.broadcast_to(ylo[k, i], (CY, 128)), pltpu.roll(u, 1, 0))
+            b = (wind[k, i+1] if i < CX-1 else xhi[k*CY:(k+1)*CY]) + (wind[k, i-1] if i > 0 else xlo[k*CY:(k+1)*CY])
+            nxt = jnp.where(sub == CY-1, jnp.broadcast_to(yhi[k*CX+i:k*CX+i+1], (CY, 128)), pltpu.roll(u, CY-1, 0))
+            prv = jnp.where(sub == 0, jnp.broadcast_to(ylo[k*CX+i:k*CX+i+1], (CY, 128)), pltpu.roll(u, 1, 0))
             b = b + nxt + prv
             b = b + jnp.where(lane == 127, 0.0, pltpu.roll(u, 127, 1)) + jnp.where(lane == 0, 0.0, pltpu.roll(u, 1, 1))
             emit(k, i, u, v * (b - 6.0 * u) + acc[k, (i*CY) % 256:(i*CY) % 256 + CY, (i*CY)//256*128:(i*CY)//256*128 + 128] + forcing[k, i])
 
 
-def mid_kernel(bnd, ctl, cell, pos, slot, order, first, place, wire, wind, forcing, visc, xlo, xhi, ylo, yhi, mid, wire_out, xa, xb, ya, yb, val, acc, s, keys):
+def mid_kernel(bnd, ctl, cell, pos, slot, order, first, place, wire, wind, forcing, visc, mid, wire_out, val, acc, s, keys):
     from_wire(pos, wire, val)
     scatter_add(bnd, cell, val, acc)
     CY = wind.shape[2]
@@ -329,19 +356,19 @@
     def emit(k, i, u, f):
         mid[k, i*CY:(i+1)*CY, :] = u + neutral_step * f
 
-    tend_all(wind, forcing, visc, xlo, xhi, ylo, yhi, acc, emit)
-    put_edges(lambda k, i: mid[k, i*CY:(i+1)*CY, :], xa, xb, ya, yb)
+    tend_all(wind, forcing, visc, wire, acc, emit)
+    put_edges(mid, wire_out)
     lookup(ctl, slot, order, first, place, mid, wire_out, s, keys)
 
 
-def end_kernel(bnd, cell, pos, wire, start, wind, forcing, visc, xlo, xhi, ylo, yhi, out, val, acc):
+def end_kernel(bnd, cell, pos, wire, start, wind, forcing, visc, out, val, acc):
     from_wire(pos, wire, val)
     scatter_add(bnd, cell, val, acc)
 
     def emit(k, i, u, f):
         out[k, i] = 0.5 * (start[k, i] + u) + (0.5 * neutral_step) * f
 
-    tend_all(wind, forcing, visc, xlo, xhi, ylo, yhi, acc, emit)
+    tend_all(wind, forcing, visc, wire, acc, emit)
 
 
 def call(kernel, outs, scratch, *args, smem=1, name=None):
@@ -353,12 +380,6 @@
         scratch_shapes=scratch,
         name=name,
     )(*args)
-
-
-def beside(axis, first, last):
-    peers = lax.axis_size(axis)
-    up = [(i, i + 1) for i in range(peers - 1)]
-    return [lax.ppermute(last, axis, up), lax.ppermute(first, axis, [(b, a) for a, b in up])]
 
 
 def tied(*arrays):
@@ -387,57 +408,43 @@
 ):
     visc = viscosity[None, :]
     sd = jax.ShapeDtypeStruct
-    wire_t = sd((128, 4, 128), f32)
+    wire_t = sd((128, 3, 2, 128), f32)
     tube_t = sd(ion_density.shape, f32)
     vals = pltpu.VMEM((2, 256, 128), f32)
     accs = pltpu.VMEM((2, 256 + W, 256), f32)
     tabs = pltpu.VMEM((2, 512, 128), f32)
     flat = (2, 512, 128)
     up_route = [(i, i + 1) for i in range(lax.axis_size("gy") - 1)]
-    CX, CY = neutral_wind.shape[1:3]
-    edge_t = (sd((2, 1, CY, 128), f32),)*2 + (sd((2, CX, 1, 128), f32),)*2
     side_t = (sd((256, 128), i32), sd((128, 256), i32), sd((32, 128), i32), sd((1024, 128), i32))
     side_t += (sd((128, 256), i32), sd((128, 128), i32), sd((128, 256), i32), sd((8, 128), i32))
     seek = [pltpu.VMEM((2, 1024, 128), f32), pltpu.VMEM((1024, 128), i32)]
 
-    cA, pA, bA, *gA, ctA, xa, xb, ya, yb = call(
-        tile_sort_kernel, side_t + edge_t, [], outgoing_column, send_level, neutral_wind, smem=0, name="tilesort")
+    cA, pA, bA, *gA, ctA = call(
+        tile_sort_kernel, side_t, [], outgoing_column, send_level, smem=0, name="tilesort")
     wire = call(gather_kernel, wire_t, seek, ctA, *gA, neutral_wind.reshape(flat), name="first")
     came = exchange(wire)
-    wire, tub, xa, xb = tied(wire, recv_tube, xa, xb)
+    wire, tub = tied(wire, recv_tube)
     cB, pB, bB, *gB, ctB, gain, drift = call(
         tube_sort_kernel, side_t + (sd((128, 256), f32), sd((128, 128), f32)), [],
         tub, recv_point, recv_weight, pair_count, drift_fraction[None, :], smem=0, name="tubesort")
-    halo = beside("gx", xa, xb)
-    came, *halo = tied(came, *halo)
 
     def tubes(came, ions, last):
-        w, smooth, out_last = call(
-            tube_kernel, (tube_t, tube_t, sd((2, 1, 512), f32)), [vals, accs],
+        w, smooth, out_last, edge = call(
+            tube_kernel, (tube_t, tube_t, sd((2, 1, 512), f32), sd((2, 128, 128), f32)), [vals, accs],
             bB, coupling, cB, pB, gain, drift, came, ions, inverse, smem=2, name="tube")
         up = lax.ppermute(out_last, "gy", up_route)
         return call(
             lambda *a: drag_kernel(last, *a), (tube_t, wire_t), [tabs] + seek,
-            ctB, drag_rate, *gB, gain, drift, w, smooth, up, ion_density, smem=2, name="drag")
+            ctB, drag_rate, *gB, gain, drift, w, smooth, up, ion_density, edge, smem=2, name="drag")
 
     n1, wire = tubes(came, ion_density, False)
-    came = exchange(wire)
-    wire, ya, yb = tied(wire, ya, yb)
-    halo += beside("gy", ya, yb)
-    mid, wire, xa, xb, ya, yb = call(
-        mid_kernel, (sd(flat, f32), wire_t) + edge_t, [vals, accs] + seek,
-        bA, ctA, cA, pA, *gA, came, neutral_wind, forcing, visc, *halo, smem=2, name="mid")
-    mid = mid.reshape(neutral_wind.shape)
-    came = exchange(wire)
-    halo = beside("gx", xa, xb)
-    came, *halo = tied(came, *halo)
-    ion_out, wire = tubes(came, n1, True)
-    came = exchange(wire)
-    wire, ya, yb = tied(wire, ya, yb)
-    halo += beside("gy", ya, yb)
+    mid, wire = call(
+        mid_kernel, (sd(flat, f32), wire_t), [vals, accs] + seek,
+        bA, ctA, cA, pA, *gA, exchange(wire), neutral_wind, forcing, visc, smem=2, name="mid")
+    ion_out, wire = tubes(exchange(wire), n1, True)
     wind_out = call(
         end_kernel, sd(neutral_wind.shape, f32), [vals, accs],
-        bA, cA, pA, came, neutral_wind, mid, forcing, visc, *halo, name="end")
+        bA, cA, pA, exchange(wire), neutral_wind, mid.reshape(neutral_wind.shape), forcing, visc, name="end")
     return (wind_out, ion_out)
 
 

time: 181 us -> 169 us (0.934)
  blocking collectives: 0 us -> 55.1 us
  starting transfers between devices: 72 us -> 18.1 us
  waiting for transfers between devices: 19.4 us -> 7.79 us
  local copies, waits for them, and re-layouts: 4.06 us -> 1.92 us
    all_to_all x0 -> x3, blocking collectives: none -> 55.1 us  [exchange(): lax.all_to_all(x, ('gx', 'gy'), split_axis=0, concat_axis=0, tiled=True)]
    all_to_all x4 -> x1, starting transfers between devices: 45.1 us -> 11.5 us  [exchange(): lax.all_to_all(x, ('gx', 'gy'), split_axis=0, concat_axis=0, tiled=True)]
    ppermute x8 -> x0, starting transfers between devices: 20.5 us -> none  [the longest x4 13.9 us: beside(): lax.ppermute(last, axis, up)]
    ppermute x8 -> x0, waiting for transfers between devices: 10.6 us -> none  [the longest x4 10.6 us: beside(): lax.ppermute(first, axis, [(b, a) for a, b in up])]
    unnamed x44 -> x6, local copies, waits for them, and re-layouts: 4.06 us -> 1.92 us
    all_to_all x4 -> x1, waiting for transfers between devices: 6.84 us -> 5.9 us  [exchange(): lax.all_to_all(x, ('gx', 'gy'), split_axis=0, concat_axis=0, tiled=True)]
  transfers between devices with their start and end apart: 14 -> 3, of which waited for: 9 -> 3; matrix products, arithmetic and copies ran while one was open for 0% -> 0% of each run, Pallas kernels for 3% -> 4%
where the time goes in v6:
time: 169 us; the launch traced here: 168 us
  Pallas kernels  84.5 us (50%)
  blocking collectives  55.1 us (33%)
  starting transfers between devices  18.1 us (11%)
  waiting for transfers between devices  7.79 us (5%)
  local copies, waits for them, and re-layouts  1.92 us (1%)
    pallas_call x9, Pallas kernels, call(): pl.pallas_call(kernel, out_shape=outs, in_specs=[SM] * smem + [VM] * (len...  84.5 us
    all_to_all x3, blocking collectives, exchange(): lax.all_to_all(x, ('gx', 'gy'), split_axis=0, concat_axis=0, tiled=True)  55.1 us
    all_to_all x1, starting transfers between devices, exchange(): lax.all_to_all(x, ('gx', 'gy'), split_axis=0, concat_axis=0, tiled=True)  11.5 us
    ppermute x2, starting transfers between devices, tubes(): up = lax.ppermute(out_last, 'gy', up_route)  6.62 us
    all_to_all x1, waiting for transfers between devices, exchange(): lax.all_to_all(x, ('gx', 'gy'), split_axis=0, concat_axis=0, tiled=True)  5.9 us
  transfers between devices with their start and end apart: 3, of which 3 were waited for; matrix products, arithmetic and copies ran while one was open for 0% of the time, Pallas kernels for 4%

profile of v6, /device:TPU:1, one launch (start us, length us, event | category | flops | bytes accessed | tf_op | source)
XLA Modules:
  0.0 168.1 jit_solution(8047794881091030516)
XLA Ops:
  0.6 5.8 %tilesort.1 = (s32[256,128]{1,0:T(8,128)}, s32[128,256]{1,0:T(8,128)}, s32[32,128]{1,0:T(8,128)}, s32[1024,128]{1,0:T(8,128)}, s32[128,256]{1,0:T(8,128)}, /*ind...) custom-call(s32[1,128,256]{2,1,0:T(8,128)} %col.1, s32[1,128,256]{2,1,0:T(8,128)} %lev.1), custom_call_target="tpu_custom_call" | custom-call | tf_op jit(solution)/shard_map/tilesort/pallas_call | solution.py:375
  6.4 7.1 %first.1 = f32[128,3,2,128]{3,2,1,0:T(2,128)} custom-call(s32[8,128]{1,0:T(8,128)} %get-tuple-element.38.ctl, s32[1024,128]{1,0:T(8,128)} %get-tuple-element.39.slot, s32[128,256]{1,0:T(8,128)} %get-tuple-element.40.order, s32[128,128]{1,0:T(8,128)} %get-tuple-element.41.first, s32[128,256]{1,0:T(8,128)} %get-tuple-element.42.place, f32[2,512,128]{2,1,0:T(8,128)} %bitcast.4), custom_call_target="tpu_custom_call" | custom-call | tf_op jit(solution)/shard_map/first/pallas_call | solution.py:375
  13.5 11.5 %all-to-all-start = ((f32[128,3,2,128]{3,2,1,0:T(2,128)}), f32[128,3,2,128]{3,2,1,0:T(2,128)S(1)}, u32[]{:S(2)}, u32[]{:S(2)}) async-start(f32[128,3,2,128]{3,2,1,0:T(2,128)} %first.1), calls=%async_computation | async-start | bytes 786432 | tf_op jit(solution)/shard_map/all_to_all | solution.py:390
  25.0 6.0 %tubesort.1 = (s32[256,128]{1,0:T(8,128)}, s32[128,256]{1,0:T(8,128)}, s32[32,128]{1,0:T(8,128)}, s32[1024,128]{1,0:T(8,128)}, s32[128,256]{1,0:T(8,128)}, /*ind...) custom-call(s32[1,128,256]{2,1,0:T(8,128)} %tub, ...), custom_call_target="tpu_custom_call" | custom-call | tf_op jit(solution)/shard_map/tubesort/pallas_call | solution.py:375
  31.1 5.9 %all-to-all-done.wire = f32[128,3,2,128]{3,2,1,0:T(2,128)S(1)} async-done(((f32[128,3,2,128]{3,2,1,0:T(2,128)}), f32[128,3,2,128]{3,2,1,0:T(2,128)S(1)}, u32[]{:S(2)}, u32[]{:S(2)}) %all-to-all-start) | async-done | bytes 393248 | tf_op jit(solution)/shard_map/all_to_all | solution.py:390
  37.0 0.0 copy-start
  37.0 0.8 copy-done
  37.7 11.1 %tube.2 = (f32[2,128,512]{2,1,0:T(8,128)}, f32[2,128,512]{2,1,0:T(8,128)}, f32[2,1,512]{2,1,0:T(1,128)}, f32[2,128,128]{2,1,0:T(8,128)}) custom-call(s32[32,128]{1,0:T(8,128)} %get-tuple-element.51.bnd, f32[2,2]{1,0:T(2,128)} %coupling.3, s32[256,128]{1,0:T(8,128)} %get-tuple-element.52.cell, s32[128,256]{1,0:T(8,128)} %get-tuple-element.53.pos, ...), custom_call_target="tpu_custom_call" | custom-call | tf_op jit(solution)/shard_map/tube/pallas_call | solution.py:375
  48.8 3.3 %collective-permute-start = (f32[2,1,512]{2,1,0:T(1,128)}, f32[2,1,512]{2,1,0:T(1,128)S(1)}, u32[]{:S(2)}, u32[]{:S(2)}) collective-permute-start(f32[2,1,512]{2,1,0:T(1,128)} %get-tuple-element.56), channel_id=1, source_target_pairs={{0,1},{1,2},{2,3},{3,4},{4,5},{5,6},{6,7},{7,8},{8,9},{9,10},{10,1... | collective-permute-start | bytes 12296 | tf_op jit(solution)/shard_map/ppermute | solution.py:435
  52.1 0.9 collective-permute-done.a_10_
  53.1 0.0 copy-start.2
  53.1 0.6 copy-done.2
  53.6 7.9 %drag.2 = (f32[2,128,512]{2,1,0:T(8,128)}, f32[128,3,2,128]{3,2,1,0:T(2,128)}) custom-call(s32[8,128]{1,0:T(8,128)} %get-tuple-element.44.a_0_, f32[2]{0:T(128)} %a_1_.3, s32[1024,128]{1,0:T(8,128)} %get-tuple-element.45.a_2_, s32[128,256]{1,0:T(8,128)} %get-tuple-element.46.a_3_, s32[128,128]{1,0:T(8,128)} %get-tuple-element.47.a_4_, ...), custom_call_target="tpu_custom_call" | custom-call | tf_op jit(solution)/shard_map/drag/pallas_call | solution.py:375
  61.6 18.8 %all_to_all.20.wire = f32[128,3,2,128]{3,2,1,0:T(2,128)} all-to-all(f32[128,3,2,128]{3,2,1,0:T(2,128)} %get-tuple-element.58), channel_id=1, replica_groups=mesh['gx'=8,'gy'=16] {'gx','gy'}, dimensions={0} | all-to-all | bytes 786432 | tf_op jit(solution)/shard_map/all_to_all | solution.py:390
  80.3 16.5 %mid.1 = (f32[2,512,128]{2,1,0:T(8,128)}, f32[128,3,2,128]{3,2,1,0:T(2,128)}) custom-call(s32[32,128]{1,0:T(8,128)} %get-tuple-element.35.bnd, s32[8,128]{1,0:T(8,128)} %get-tuple-element.38.ctl, s32[256,128]{1,0:T(8,128)} %get-tuple-element.36.cell, s32[128,256]{1,0:T(8,128)} %get-tuple-element.37.pos, s32[1024,128]{1,0:T(8,128)} %get-tuple-element.39.slot, ...), custom_call_target="tpu_custom_call" | custom-call | tf_op jit(solution)/shard_map/mid/pallas_call | solution.py:375
  96.8 17.6 %all_to_all.21.wire = f32[128,3,2,128]{3,2,1,0:T(2,128)} all-to-all(f32[128,3,2,128]{3,2,1,0:T(2,128)} %get-tuple-element.59), channel_id=1, replica_groups=mesh['gx'=8,'gy'=16] {'gx','gy'}, dimensions={0} | all-to-all | bytes 786432 | tf_op jit(solution)/shard_map/all_to_all | solution.py:390
  114.5 11.1 %tube.3 = (f32[2,128,512]{2,1,0:T(8,128)}, f32[2,128,512]{2,1,0:T(8,128)}, f32[2,1,512]{2,1,0:T(1,128)}, f32[2,128,128]{2,1,0:T(8,128)}) custom-call(s32[32,128]{1,0:T(8,128)} %get-tuple-element.51.bnd, f32[2,2]{1,0:T(2,128)} %coupling.3, s32[256,128]{1,0:T(8,128)} %get-tuple-element.52.cell, s32[128,256]{1,0:T(8,128)} %get-tuple-element.53.pos, ...), custom_call_target="tpu_custom_call" | custom-call | tf_op jit(solution)/shard_map/tube/pallas_call | solution.py:375
  125.5 3.3 %collective-permute-start.1 = (f32[2,1,512]{2,1,0:T(1,128)}, f32[2,1,512]{2,1,0:T(1,128)S(1)}, u32[]{:S(2)}, u32[]{:S(2)}) collective-permute-start(f32[2,1,512]{2,1,0:T(1,128)} %get-tuple-element.63), channel_id=1, source_target_pairs={{0,1},{1,2},{2,3},{3,4},{4,5},{5,6},{6,7},{7,8},{8,9},{9,10},{10,1... | collective-permute-start | bytes 12296 | tf_op jit(solution)/shard_map/ppermute | solution.py:435
  128.8 0.9 collective-permute-done.1.a_10_
  129.8 0.0 copy-start.1
  129.8 0.6 copy-done.1
  130.4 7.9 %drag.3 = (f32[2,128,512]{2,1,0:T(8,128)}, f32[128,3,2,128]{3,2,1,0:T(2,128)}) custom-call(s32[8,128]{1,0:T(8,128)} %get-tuple-element.44.a_0_, f32[2]{0:T(128)} %a_1_.3, s32[1024,128]{1,0:T(8,128)} %get-tuple-element.45.a_2_, s32[128,256]{1,0:T(8,128)} %get-tuple-element.46.a_3_, s32[128,128]{1,0:T(8,128)} %get-tuple-element.47.a_4_, ...), custom_call_target="tpu_custom_call" | custom-call | tf_op jit(solution)/shard_map/drag/pallas_call | solution.py:375
  138.3 18.7 %all_to_all.22.wire = f32[128,3,2,128]{3,2,1,0:T(2,128)} all-to-all(f32[128,3,2,128]{3,2,1,0:T(2,128)} %get-tuple-element.65), channel_id=1, replica_groups=mesh['gx'=8,'gy'=16] {'gx','gy'}, dimensions={0} | all-to-all | bytes 786432 | tf_op jit(solution)/shard_map/all_to_all | solution.py:390
  157.0 11.1 %end.1 = f32[2,16,32,128]{3,2,1,0:T(8,128)} custom-call(s32[32,128]{1,0:T(8,128)} %get-tuple-element.35.bnd, s32[256,128]{1,0:T(8,128)} %get-tuple-element.36.cell, s32[128,256]{1,0:T(8,128)} %get-tuple-element.37.pos, f32[128,3,2,128]{3,2,1,0:T(2,128)} %all_to_all.22.wire, f32[2,16,32,128]{3,2,1,0:T(8,128)} %start.1, f32[2,16,32,128]{3,2,1,0:T(8,128)} %bitcast.5, ...), custom_call_target="tpu_custom_call" | custom-call | tf_op jit(solution)/shard_map/end/pallas_call | solution.py:375
Async XLA Ops:
  13.5 23.4 %all-to-all-start = ((f32[128,3,2,128]{3,2,1,0:T(2,128)}), f32[128,3,2,128]{3,2,1,0:T(2,128)S(1)}, u32[]{:S(2)}, u32[]{:S(2)}) async-start(f32[128,3,2,128]{3,2,1,0:T(2,128)} %first.1), calls=%async_computation | async-start | bytes 786432 | tf_op jit(solution)/shard_map/all_to_all | solution.py:390
  37.0 0.8 copy-start
  48.8 4.3 %collective-permute-start = (f32[2,1,512]{2,1,0:T(1,128)}, f32[2,1,512]{2,1,0:T(1,128)S(1)}, u32[]{:S(2)}, u32[]{:S(2)}) collective-permute-start(f32[2,1,512]{2,1,0:T(1,128)} %get-tuple-element.56), channel_id=1, source_target_pairs={{0,1},{1,2},{2,3},{3,4},{4,5},{5,6},{6,7},{7,8},{8,9},{9,10},{10,1... | collective-permute-start | bytes 12296 | tf_op jit(solution)/shard_map/ppermute | solution.py:435
  53.1 0.6 copy-start.2
  125.5 4.3 %collective-permute-start.1 = (f32[2,1,512]{2,1,0:T(1,128)}, f32[2,1,512]{2,1,0:T(1,128)S(1)}, u32[]{:S(2)}, u32[]{:S(2)}) collective-permute-start(f32[2,1,512]{2,1,0:T(1,128)} %get-tuple-element.63), channel_id=1, source_target_pairs={{0,1},{1,2},{2,3},{3,4},{4,5},{5,6},{6,7},{7,8},{8,9},{9,10},{10,1... | collective-permute-start | bytes 12296 | tf_op jit(solution)/shard_map/ppermute | solution.py:435
  129.8 0.6 copy-start.1

commit v7 on v6

--- a/solution.py
+++ b/solution.py
@@ -57,6 +57,10 @@
         k *= 2
     return x.reshape(n, L)
 
+def row_of(r, start=0, count=128):
+    return pl.ds(6*start + r, count, stride=6)
+
+
 def take(x, idx):
     return jnp.take_along_axis(x, idx, axis=1, mode="promise_in_bounds")
 
@@ -75,7 +79,7 @@
 def sort_side(key16, cell_ref, pos_ref, bnd_ref, slot_ref, order_ref, first_ref, place_ref, ctl_ref):
     P, C = key16.shape
     c = lax.broadcasted_iota(i32, (P, C), 1)
-    s = bitonic((key16 * 256 + c).T)
+    s = bitonic((key16 * 256 + c).astype(f32).T).astype(i32)
     cell = s >> 8
     cell_ref[...] = cell
     pos = (s & 255).T
@@ -85,27 +89,24 @@
     hi = jnp.max(jnp.max(row, axis=1), axis=1, keepdims=True)
     lane = lax.broadcasted_iota(i32, (C//8, 128), 1)
     bnd_ref[...] = jnp.where(lane == 0, lo, hi)
-    tall = cell.reshape(C//8, 8, P)
-    below = []
-    for b in range(64):
-        n = jnp.sum(jnp.where(tall < b*1024, 1.0, 0.0), axis=0)
-        below.append(jnp.sum(n, axis=0, keepdims=True))
-    full = jnp.full((64, P), float(C), f32)
-    below = jnp.concatenate(below + [full], axis=0)
-    most = jnp.max(pltpu.roll(below, 127, 0)[:64] - below[:64], axis=1, keepdims=True)
-    most = jnp.max(jnp.broadcast_to(most, (64, 128)).reshape(8, 8, 128), axis=1)
-    top = jnp.max(most, axis=0, keepdims=True)
-    ctl_ref[...] = jnp.where(lane[:8] == 0, most, jnp.broadcast_to(top, (8, 128))).astype(i32)
-    first = below.T.astype(i32)
-    first_ref[...] = first
     order = cell.T
     order_ref[...] = order
+    lane = lax.broadcasted_iota(i32, (P, 128), 1)
+    first = jnp.zeros((P, 128), i32)
+    for step in (128, 64, 32, 16, 8, 4, 2, 1, 1):
+        probe = first + step
+        first = jnp.where(take2(order, probe - 1) < lane*1024, probe, first)
+    first_ref[...] = first
+    most = jnp.max((pltpu.roll(first, 127, 1) - first).astype(f32), axis=0, keepdims=True)
+    most = jnp.where(lane[:1] < 64, most, 0.0)
+    top = jnp.broadcast_to(jnp.max(most, axis=1, keepdims=True), (1, 128))
+    ctl_ref[...] = jnp.broadcast_to(jnp.where(lane[:1] < 64, most, top), (8, 128)).astype(i32)
     for j in range(8):
         slot_tile(order, first_ref, 0, j, slot_ref)
     b = order >> 10
     w = c - jnp.concatenate([take(first, b[:, :128]), take(first, b[:, 128:])], axis=1)
     place = (pos << 14) + ((w >> 4) << 10) + (b << 4) + (w & 15)
-    place_ref[...] = (bitonic(place.T) & 16383).T
+    place_ref[...] = (bitonic(place.astype(f32).T).astype(i32) & 16383).T
 
 
 def cell_key(row, lane):
@@ -115,12 +116,12 @@
 def put_edges(t, wire):
     CX, CY = 16, t.shape[1] // 16
     for k in range(2):
-        wire[k*CY:(k+1)*CY, 2, 0, :] = t[k, (CX-1)*CY:CX*CY, :]
-        wire[(2+k)*CY:(3+k)*CY, 2, 0, :] = t[k, :CY, :]
+        wire[row_of(4, k*CY, CY), :] = t[k, (CX-1)*CY:CX*CY, :]
+        wire[row_of(4, (2+k)*CY, CY), :] = t[k, :CY, :]
         for i in range(CX):
-            wire[k*CX+i:k*CX+i+1, 2, 1, :] = t[k, (i+1)*CY-1:(i+1)*CY, :]
-            wire[(2+k)*CX+i:(2+k)*CX+i+1, 2, 1, :] = t[k, i*CY:i*CY+1, :]
-    wire[4*CX:, 2, 1, :] = jnp.zeros((128 - 4*CX, 128), f32)
+            for q, at in ((k*CX+i, (i+1)*CY-1), ((2+k)*CX+i, i*CY)):
+                wire[6*q+5:6*q+6, :] = t[k, at:at+1, :]
+    wire[row_of(5, 4*CX, 128 - 4*CX), :] = jnp.zeros((128 - 4*CX, 128), f32)
 
 
 def place_of():
@@ -132,23 +133,19 @@
     q = place_of()[2]
     step = lax.axis_size("gy")
     for r, (cut, d) in enumerate(((64, step), (32, 1))):
-        x = wire[:, 2, r, :]
+        x = wire[row_of(4+r), :]
         out[r] = jnp.where(q < cut, pltpu.roll(x, d, 0), pltpu.roll(x, 128-d, 0))
 
 
 def beside_tile(wire):
     x, y = place_of()[:2]
-    a, b = wire[:, 2, 0, :], wire[:64, 2, 1, :]
+    a, b = wire[row_of(4), :], wire[row_of(5, 0, 64), :]
     return (
         jnp.where(x > 0, a[:64], 0.0),
         jnp.where(x < lax.axis_size("gx") - 1, a[64:], 0.0),
         jnp.where(y > 0, b[:32], 0.0),
         jnp.where(y < lax.axis_size("gy") - 1, b[32:], 0.0),
     )
-
-
-def tile_sort_kernel(col, lev, *side):
-    sort_side(cell_key(col[0], lev[0]), *side)
 
 
 def tube_sort_kernel(tub, pnt, weight, count, drift, *outs):
@@ -167,7 +164,7 @@
     return [take2(x, idx[:, :128]), take2(x, idx[:, 128:])]
 
 
-def lookup(ctl, slot, order, first, place, t_ref, wire, s_ref, key_ref, gain=None):
+def lookup(ctl, slot, order, first, place, t_ref, wire, s_ref, key_ref, gain=None, limit_copy=None):
     half = t_ref.shape[1] // 2
 
     def group(g, keys):
@@ -196,6 +193,8 @@
         return x if gain is None else x * gain[:, h*128:(h+1)*128]
 
     lax.fori_loop(0, 8, each, 0)
+    if limit_copy is not None:
+        limit_copy.start()
     parts = [[s_ref[k, j*128:(j+1)*128, :].T for j in range(8)] for k in range(2)]
     for h in range(2):
         at = place[:, h*128:(h+1)*128]
@@ -204,11 +203,15 @@
             x = take(parts[k][0], low)
             for j in range(1, 8):
                 x = jnp.where(tile == j, take(parts[k][j], low), x)
-            wire[:, k, h, :] = scaled(x, h)
+            wire[row_of(2*k+h), :] = scaled(x, h)
 
     def turn(t, _):
         def late(g, _):
-            @pl.when(ctl[g, 0] > 16*t)
+            most = ctl[0, 8*g]
+            for b in range(1, 8):
+                most = jnp.maximum(most, ctl[0, 8*g + b])
+
+            @pl.when(most > 16*t)
             def _():
                 slot_tile(order[...], first, t, g, key_ref)
                 group(g, key_ref)
@@ -218,13 +221,15 @@
                     mine = (at >> 7) == 8*t + g
                     for k in range(2):
                         x = take(s_ref[k, tile, :].T, at & 127)
-                        wire[:, k, h, :] = jnp.where(mine, scaled(x, h), wire[:, k, h, :])
+                        wire[row_of(2*k+h), :] = jnp.where(mine, scaled(x, h), wire[row_of(2*k+h), :])
             return 0
 
         lax.fori_loop(0, 8, late, 0)
         return 0
 
-    lax.fori_loop(1, (ctl[0, 1] + 15) // 16, turn, 0)
+    if limit_copy is not None:
+        limit_copy.wait()
+    lax.fori_loop(1, (ctl[0, 64] + 15) // 16, turn, 0)
 
 
 def scatter_add(bnd, cell_ref, val_ref, acc_ref):
@@ -278,7 +283,7 @@
 
 def from_wire(pos, wire, val, gain=None):
     for k in range(2):
-        x = [wire[:, k, h, :] for h in range(2)]
+        x = [wire[row_of(2*k+h), :] for h in range(2)]
         if gain is not None:
             x = [x[h] * gain[:, h*128:(h+1)*128] for h in range(2)]
         o = permute_lanes(jnp.concatenate(x, axis=1), pos[...])
@@ -286,9 +291,12 @@
         val[k, 128:, :] = o[1].T
 
 
-def gather_kernel(ctl, slot, order, first, place, t, wire, s, keys):
+def first_kernel(col, lev, t, *refs):
+    side, wire, s, keys, limits, sem = refs[:8], refs[8], *refs[9:]
+    sort_side(cell_key(col[0], lev[0]), *side)
+    copy = pltpu.make_async_copy(side[7], limits, sem)
     put_edges(t, wire)
-    lookup(ctl, slot, order, first, place, t, wire, s, keys)
+    lookup(limits, *side[3:7], t, wire, s, keys, limit_copy=copy)
 
 
 def tube_kernel(bnd, coupling, cell, pos, gain, drift, wire, ions, inverse, w_out, smooth_out, last_out, edge_out, val, acc):
@@ -311,7 +319,7 @@
 
 def drag_kernel(last, ctl, drag, slot, order, first_at, place, gain, drift, w, smooth, up, ions, edge, n_out, wire, t, s, keys):
     for r in range(2):
-        wire[:, 2, r, :] = edge[r]
+        wire[row_of(4+r), :] = edge[r]
     first = lax.broadcasted_iota(i32, (128, 128), 0) == 0
     d = drift[...]
     n = [[], []]
@@ -387,7 +395,8 @@
 
 
 def exchange(x):
-    return lax.all_to_all(x, ("gx", "gy"), split_axis=0, concat_axis=0, tiled=True)
+    x = x.reshape(128, 3, 2, 128)
+    return lax.all_to_all(x, ("gx", "gy"), split_axis=0, concat_axis=0, tiled=True).reshape(768, 128)
 
 
 def per_device(
@@ -408,7 +417,7 @@
 ):
     visc = viscosity[None, :]
     sd = jax.ShapeDtypeStruct
-    wire_t = sd((128, 3, 2, 128), f32)
+    wire_t = sd((768, 128), f32)
     tube_t = sd(ion_density.shape, f32)
     vals = pltpu.VMEM((2, 256, 128), f32)
     accs = pltpu.VMEM((2, 256 + W, 256), f32)
@@ -419,9 +428,9 @@
     side_t += (sd((128, 256), i32), sd((128, 128), i32), sd((128, 256), i32), sd((8, 128), i32))
     seek = [pltpu.VMEM((2, 1024, 128), f32), pltpu.VMEM((1024, 128), i32)]
 
-    cA, pA, bA, *gA, ctA = call(
-        tile_sort_kernel, side_t, [], outgoing_column, send_level, smem=0, name="tilesort")
-    wire = call(gather_kernel, wire_t, seek, ctA, *gA, neutral_wind.reshape(flat), name="first")
+    cA, pA, bA, *gA, ctA, wire = call(
+        first_kernel, side_t + (wire_t,), seek + [pltpu.SMEM((8, 128), i32), pltpu.SemaphoreType.DMA],
+        outgoing_column, send_level, neutral_wind.reshape(flat), smem=0, name="first")
     came = exchange(wire)
     wire, tub = tied(wire, recv_tube)
     cB, pB, bB, *gB, ctB, gain, drift = call(

time: 169 us -> 166 us (0.982)
  Pallas kernels: 84.5 us -> 80.7 us
    pallas_call x9 -> x8, Pallas kernels: 84.5 us -> 80.7 us  [call(): pl.pallas_call(kernel, out_shape=outs, in_specs=[SM] * smem + [VM] * (len...]
  transfers between devices with their start and end apart: 3 -> 3, of which waited for: 3 -> 3; matrix products, arithmetic and copies ran while one was open for 0% -> 0% of each run, Pallas kernels for 4% -> 3%
where the time goes in v7:
time: 166 us; the launch traced here: 165 us
  Pallas kernels  80.7 us (49%)
  blocking collectives  55.1 us (33%)
  starting transfers between devices  18.1 us (11%)
  waiting for transfers between devices  8.65 us (5%)
  local copies, waits for them, and re-layouts  1.92 us (1%)
    pallas_call x8, Pallas kernels, call(): pl.pallas_call(kernel, out_shape=outs, in_specs=[SM] * smem + [VM] * (len...  80.7 us
    all_to_all x3, blocking collectives, exchange(): lax.all_to_all(x, ('gx', 'gy'), split_axis=0, concat_axis=0, tiled=True)  55.1 us
    all_to_all x1, starting transfers between devices, exchange(): lax.all_to_all(x, ('gx', 'gy'), split_axis=0, concat_axis=0, tiled=True)  11.5 us
    all_to_all x1, waiting for transfers between devices, exchange(): lax.all_to_all(x, ('gx', 'gy'), split_axis=0, concat_axis=0, tiled=True)  6.76 us
    ppermute x2, starting transfers between devices, tubes(): up = lax.ppermute(out_last, 'gy', up_route)  6.62 us
  transfers between devices with their start and end apart: 3, of which 3 were waited for; matrix products, arithmetic and copies ran while one was open for 0% of the time, Pallas kernels for 3%

profile of v7, /device:TPU:1, one launch (start us, length us, event | category | flops | bytes accessed | tf_op | source)
XLA Modules:
  0.0 165.2 jit_solution(3236942237801363138)
XLA Ops:
  0.6 10.6 %first.1 = (s32[256,128]{1,0:T(8,128)}, s32[128,256]{1,0:T(8,128)}, s32[32,128]{1,0:T(8,128)}, s32[1024,128]{1,0:T(8,128)}, s32[128,256]{1,0:T(8,128)}, /*index=...) custom-call(s32[1,128,256]{2,1,0:T(8,128)} %col.1, s32[1,128,256]{2,1,0:T(8,128)} %lev.1, ...), custom_call_target="tpu_custom_call" | custom-call | tf_op jit(solution)/shard_map/first/pallas_call | solution.py:383
  11.2 11.5 %all-to-all-start = ((f32[128,3,2,128]{3,2,1,0:T(2,128)}), f32[128,3,2,128]{3,2,1,0:T(2,128)S(1)}, u32[]{:S(2)}, u32[]{:S(2)}) async-start(f32[128,3,2,128]{3,2,1,0:T(2,128)} %bitcast.18), calls=%async_computation | async-start | bytes 786432 | tf_op jit(solution)/shard_map/all_to_all | solution.py:399
  22.7 5.2 %tubesort.1 = (s32[256,128]{1,0:T(8,128)}, s32[128,256]{1,0:T(8,128)}, s32[32,128]{1,0:T(8,128)}, s32[1024,128]{1,0:T(8,128)}, s32[128,256]{1,0:T(8,128)}, /*ind...) custom-call(s32[1,128,256]{2,1,0:T(8,128)} %tub, ...), custom_call_target="tpu_custom_call" | custom-call | tf_op jit(solution)/shard_map/tubesort/pallas_call | solution.py:383
  27.9 6.8 %all-to-all-done = f32[128,3,2,128]{3,2,1,0:T(2,128)S(1)} async-done(((f32[128,3,2,128]{3,2,1,0:T(2,128)}), f32[128,3,2,128]{3,2,1,0:T(2,128)S(1)}, u32[]{:S(2)}, u32[]{:S(2)}) %all-to-all-start) | async-done | bytes 393248 | tf_op jit(solution)/shard_map/all_to_all | solution.py:399
  34.6 0.0 copy-start
  34.6 0.8 copy-done
  35.4 11.0 %tube.2 = (f32[2,128,512]{2,1,0:T(8,128)}, f32[2,128,512]{2,1,0:T(8,128)}, f32[2,1,512]{2,1,0:T(1,128)}, f32[2,128,128]{2,1,0:T(8,128)}) custom-call(s32[32,128]{1,0:T(8,128)} %get-tuple-element.48.bnd, f32[2,2]{1,0:T(2,128)} %coupling.3, s32[256,128]{1,0:T(8,128)} %get-tuple-element.49.cell, s32[128,256]{1,0:T(8,128)} %get-tuple-element.50.pos, ...), custom_call_target="tpu_custom_call" | custom-call | tf_op jit(solution)/shard_map/tube/pallas_call | solution.py:383
  46.4 3.3 %collective-permute-start = (f32[2,1,512]{2,1,0:T(1,128)}, f32[2,1,512]{2,1,0:T(1,128)S(1)}, u32[]{:S(2)}, u32[]{:S(2)}) collective-permute-start(f32[2,1,512]{2,1,0:T(1,128)} %get-tuple-element.58), channel_id=1, source_target_pairs={{0,1},{1,2},{2,3},{3,4},{4,5},{5,6},{6,7},{7,8},{8,9},{9,10},{10,1... | collective-permute-start | bytes 12296 | tf_op jit(solution)/shard_map/ppermute | solution.py:444
  49.7 0.9 collective-permute-done.a_10_
  50.7 0.0 copy-start.2
  50.7 0.6 copy-done.2
  51.2 8.0 %drag.2 = (f32[2,128,512]{2,1,0:T(8,128)}, f32[768,128]{1,0:T(8,128)}) custom-call(s32[8,128]{1,0:T(8,128)} %get-tuple-element.41.a_0_, f32[2]{0:T(128)} %a_1_.3, s32[1024,128]{1,0:T(8,128)} %get-tuple-element.42.a_2_, s32[128,256]{1,0:T(8,128)} %get-tuple-element.43.a_3_, s32[128,128]{1,0:T(8,128)} %get-tuple-element.44.a_4_, ...), custom_call_target="tpu_custom_call" | custom-call | tf_op jit(solution)/shard_map/drag/pallas_call | solution.py:383
  59.3 18.8 %all_to_all.20 = f32[128,3,2,128]{3,2,1,0:T(2,128)} all-to-all(f32[128,3,2,128]{3,2,1,0:T(2,128)} %bitcast.21), channel_id=1, replica_groups=mesh['gx'=8,'gy'=16] {'gx','gy'}, dimensions={0} | all-to-all | bytes 786432 | tf_op jit(solution)/shard_map/all_to_all | solution.py:399
  78.0 16.2 %mid.1 = (f32[2,512,128]{2,1,0:T(8,128)}, f32[768,128]{1,0:T(8,128)}) custom-call(s32[32,128]{1,0:T(8,128)} %get-tuple-element.36.bnd, s32[8,128]{1,0:T(8,128)} %get-tuple-element.51.ctl, s32[256,128]{1,0:T(8,128)} %get-tuple-element.37.cell, s32[128,256]{1,0:T(8,128)} %get-tuple-element.38.pos, s32[1024,128]{1,0:T(8,128)} %get-tuple-element.52.slot, ...), custom_call_target="tpu_custom_call" | custom-call | tf_op jit(solution)/shard_map/mid/pallas_call | solution.py:383
  94.2 17.6 %all_to_all.21 = f32[128,3,2,128]{3,2,1,0:T(2,128)} all-to-all(f32[128,3,2,128]{3,2,1,0:T(2,128)} %bitcast.20), channel_id=1, replica_groups=mesh['gx'=8,'gy'=16] {'gx','gy'}, dimensions={0} | all-to-all | bytes 786432 | tf_op jit(solution)/shard_map/all_to_all | solution.py:399
  111.8 11.0 %tube.3 = (f32[2,128,512]{2,1,0:T(8,128)}, f32[2,128,512]{2,1,0:T(8,128)}, f32[2,1,512]{2,1,0:T(1,128)}, f32[2,128,128]{2,1,0:T(8,128)}) custom-call(s32[32,128]{1,0:T(8,128)} %get-tuple-element.48.bnd, f32[2,2]{1,0:T(2,128)} %coupling.3, s32[256,128]{1,0:T(8,128)} %get-tuple-element.49.cell, s32[128,256]{1,0:T(8,128)} %get-tuple-element.50.pos, ...), custom_call_target="tpu_custom_call" | custom-call | tf_op jit(solution)/shard_map/tube/pallas_call | solution.py:383
  122.8 3.3 %collective-permute-start.1 = (f32[2,1,512]{2,1,0:T(1,128)}, f32[2,1,512]{2,1,0:T(1,128)S(1)}, u32[]{:S(2)}, u32[]{:S(2)}) collective-permute-start(f32[2,1,512]{2,1,0:T(1,128)} %get-tuple-element.65), channel_id=1, source_target_pairs={{0,1},{1,2},{2,3},{3,4},{4,5},{5,6},{6,7},{7,8},{8,9},{9,10},{10,1... | collective-permute-start | bytes 12296 | tf_op jit(solution)/shard_map/ppermute | solution.py:444
  126.2 0.9 collective-permute-done.1.a_10_
  127.1 0.0 copy-start.1
  127.1 0.6 copy-done.1
  127.7 7.8 %drag.3 = (f32[2,128,512]{2,1,0:T(8,128)}, f32[768,128]{1,0:T(8,128)}) custom-call(s32[8,128]{1,0:T(8,128)} %get-tuple-element.41.a_0_, f32[2]{0:T(128)} %a_1_.3, s32[1024,128]{1,0:T(8,128)} %get-tuple-element.42.a_2_, s32[128,256]{1,0:T(8,128)} %get-tuple-element.43.a_3_, s32[128,128]{1,0:T(8,128)} %get-tuple-element.44.a_4_, ...), custom_call_target="tpu_custom_call" | custom-call | tf_op jit(solution)/shard_map/drag/pallas_call | solution.py:383
  135.5 18.8 %all_to_all.22 = f32[128,3,2,128]{3,2,1,0:T(2,128)} all-to-all(f32[128,3,2,128]{3,2,1,0:T(2,128)} %bitcast.19), channel_id=1, replica_groups=mesh['gx'=8,'gy'=16] {'gx','gy'}, dimensions={0} | all-to-all | bytes 786432 | tf_op jit(solution)/shard_map/all_to_all | solution.py:399
  154.3 10.9 %end.1 = f32[2,16,32,128]{3,2,1,0:T(8,128)} custom-call(s32[32,128]{1,0:T(8,128)} %get-tuple-element.36.bnd, s32[256,128]{1,0:T(8,128)} %get-tuple-element.37.cell, s32[128,256]{1,0:T(8,128)} %get-tuple-element.38.pos, f32[768,128]{1,0:T(8,128)} %bitcast.13, f32[2,16,32,128]{3,2,1,0:T(8,128)} %start.1, f32[2,16,32,128]{3,2,1,0:T(8,128)} %bitcast.17, ...), custom_call_target="tpu_custom_call" | custom-call | tf_op jit(solution)/shard_map/end/pallas_call | solution.py:383
Async XLA Ops:
  11.2 23.4 %all-to-all-start = ((f32[128,3,2,128]{3,2,1,0:T(2,128)}), f32[128,3,2,128]{3,2,1,0:T(2,128)S(1)}, u32[]{:S(2)}, u32[]{:S(2)}) async-start(f32[128,3,2,128]{3,2,1,0:T(2,128)} %bitcast.18), calls=%async_computation | async-start | bytes 786432 | tf_op jit(solution)/shard_map/all_to_all | solution.py:399
  34.6 0.8 copy-start
  46.4 4.3 %collective-permute-start = (f32[2,1,512]{2,1,0:T(1,128)}, f32[2,1,512]{2,1,0:T(1,128)S(1)}, u32[]{:S(2)}, u32[]{:S(2)}) collective-permute-start(f32[2,1,512]{2,1,0:T(1,128)} %get-tuple-element.58), channel_id=1, source_target_pairs={{0,1},{1,2},{2,3},{3,4},{4,5},{5,6},{6,7},{7,8},{8,9},{9,10},{10,1... | collective-permute-start | bytes 12296 | tf_op jit(solution)/shard_map/ppermute | solution.py:444
  50.7 0.6 copy-start.2
  122.8 4.3 %collective-permute-start.1 = (f32[2,1,512]{2,1,0:T(1,128)}, f32[2,1,512]{2,1,0:T(1,128)S(1)}, u32[]{:S(2)}, u32[]{:S(2)}) collective-permute-start(f32[2,1,512]{2,1,0:T(1,128)} %get-tuple-element.65), channel_id=1, source_target_pairs={{0,1},{1,2},{2,3},{3,4},{4,5},{5,6},{6,7},{7,8},{8,9},{9,10},{10,1... | collective-permute-start | bytes 12296 | tf_op jit(solution)/shard_map/ppermute | solution.py:444
  127.1 0.6 copy-start.1

commit v8 on v7

--- a/solution.py
+++ b/solution.py
@@ -164,8 +164,10 @@
     return [take2(x, idx[:, :128]), take2(x, idx[:, 128:])]
 
 
-def lookup(ctl, slot, order, first, place, t_ref, wire, s_ref, key_ref, gain=None, limit_copy=None):
+def lookup(ctl, slot, order, first, place, t_ref, wire, s_ref, key_ref, gain=None, limit_copy=None, hook=None):
     half = t_ref.shape[1] // 2
+
+    slot = slot() if callable(slot) else slot
 
     def group(g, keys):
         for b in range(8):
@@ -195,6 +197,10 @@
     lax.fori_loop(0, 8, each, 0)
     if limit_copy is not None:
         limit_copy.start()
+    if hook is not None:
+        hook()
+    place, order, first = [x() if callable(x) else x for x in (place, order, first)]
+    gain = gain() if callable(gain) else gain
     parts = [[s_ref[k, j*128:(j+1)*128, :].T for j in range(8)] for k in range(2)]
     for h in range(2):
         at = place[:, h*128:(h+1)*128]
@@ -293,33 +299,45 @@
 
 def first_kernel(col, lev, t, *refs):
     side, wire, s, keys, limits, sem = refs[:8], refs[8], *refs[9:]
-    sort_side(cell_key(col[0], lev[0]), *side)
-    copy = pltpu.make_async_copy(side[7], limits, sem)
+    cell, pos, bnd, slot, order, first, place, ctl = side
+    view = [x.ref for x in (cell, pos)] + [bnd] + [x.ref for x in (slot, order, first, place)] + [ctl]
+    sort_side(cell_key(col[0], lev[0]), *view)
+    t = t()
     put_edges(t, wire)
-    lookup(limits, *side[3:7], t, wire, s, keys, limit_copy=copy)
+
+    def hook():
+        for x in (slot, cell, pos, order, place, first):
+            x.send()
+
+    lookup(limits, *view[3:7], t, wire, s, keys, limit_copy=pltpu.make_async_copy(ctl, limits, sem), hook=hook)
 
 
 def tube_kernel(bnd, coupling, cell, pos, gain, drift, wire, ions, inverse, w_out, smooth_out, last_out, edge_out, val, acc):
-    pass_edges(wire, edge_out)
-    from_wire(pos, wire, val, gain)
-    scatter_add(bnd, cell, val, acc)
-    w = []
+    wire = wire()
+    pass_edges(wire, edge_out.ref)
+    from_wire(pos(), wire, val, gain())
+    scatter_add(bnd, cell(), val, acc)
+    edge_out.send()
+    w = w_out.ref
     for k in range(2):
         for j in range(4):
-            w_out[k, :, j*128:(j+1)*128] = acc[k, (j%2)*128:(j%2+1)*128, (j//2)*128:(j//2+1)*128]
+            w[k, :, j*128:(j+1)*128] = acc[k, (j % 2)*128:(j % 2+1)*128, (j//2)*128:(j//2+1)*128]
+    ions, drift, inverse = ions(), drift(), inverse()
     for k in range(2):
         n = ions[k]
-        growth = coupling[k, 0] * w_out[0] + coupling[k, 1] * w_out[1]
+        growth = coupling[k, 0] * w[0] + coupling[k, 1] * w[1]
         rhs = n + ion_factor * n * growth
         mix = lax.dot_general(rhs.astype(bf16), inverse[0, k], (((1,), (0,)), ((), ())), preferred_element_type=f32)
         sm = rhs + mix
         smooth_out[k] = sm
         last_out[k] = drift[127:128, :1] * sm[127:128, :]
+        if k == 0:
+            w_out.send()
 
 
 def drag_kernel(last, ctl, drag, slot, order, first_at, place, gain, drift, w, smooth, up, ions, edge, n_out, wire, t, s, keys):
-    for r in range(2):
-        wire[row_of(4+r), :] = edge[r]
+    w, smooth, drift = w(), smooth(), drift()
+    ions = ions() if last else None
     first = lax.broadcasted_iota(i32, (128, 128), 0) == 0
     d = drift[...]
     n = [[], []]
@@ -331,12 +349,19 @@
             inflow = jnp.where(first, jnp.broadcast_to(up[k, :, sl], (128, 128)), pltpu.roll(out, 1, 0))
             x = sm - out + inflow
             n[k].append(x)
-            n_out[k, :, sl] = 0.5 * (ions[k, :, sl] + x) if last else x
+            n_out.ref[k, :, sl] = 0.5 * (ions[k, :, sl] + x) if last else x
     for j in range(4):
         f = -(drag[0] * n[0][j] + drag[1] * n[1][j])
         for k in range(2):
             t[k, j*128:(j+1)*128, :] = f * w[k, :, j*128:(j+1)*128]
-    lookup(ctl, slot, order, first_at, place, t, wire, s, keys, gain)
+
+    def hook():
+        n_out.send()
+        move = edge()
+        for r in range(2):
+            wire[row_of(4+r), :] = move[r]
+
+    lookup(ctl, slot, order, first_at, place, t, wire, s, keys, gain, hook=hook)
 
 
 def tend_all(wind, forcing, visc, wire, acc, emit):
@@ -357,8 +382,11 @@
 
 
 def mid_kernel(bnd, ctl, cell, pos, slot, order, first, place, wire, wind, forcing, visc, mid, wire_out, val, acc, s, keys):
-    from_wire(pos, wire, val)
-    scatter_add(bnd, cell, val, acc)
+    wire = wire()
+    from_wire(pos(), wire, val)
+    scatter_add(bnd, cell(), val, acc)
+    wind, forcing, out = wind(), forcing(), mid
+    mid = out.ref
     CY = wind.shape[2]
 
     def emit(k, i, u, f):
@@ -366,12 +394,14 @@
 
     tend_all(wind, forcing, visc, wire, acc, emit)
     put_edges(mid, wire_out)
-    lookup(ctl, slot, order, first, place, mid, wire_out, s, keys)
+    lookup(ctl, slot, order, first, place, mid, wire_out, s, keys, hook=out.send)
 
 
 def end_kernel(bnd, cell, pos, wire, start, wind, forcing, visc, out, val, acc):
-    from_wire(pos, wire, val)
-    scatter_add(bnd, cell, val, acc)
+    wire = wire()
+    from_wire(pos(), wire, val)
+    scatter_add(bnd, cell(), val, acc)
+    wind, forcing, start = wind(), forcing(), start()
 
     def emit(k, i, u, f):
         out[k, i] = 0.5 * (start[k, i] + u) + (0.5 * neutral_step) * f
@@ -379,15 +409,62 @@
     tend_all(wind, forcing, visc, wire, acc, emit)
 
 
-def call(kernel, outs, scratch, *args, smem=1, name=None):
-    return pl.pallas_call(
-        kernel,
+class Incoming:
+    def __init__(self, src, dst, sem):
+        self.ref, self.copy, self.due = dst, pltpu.make_async_copy(src, dst, sem), True
+        self.copy.start()
+
+    def __call__(self):
+        if self.due:
+            self.due = False
+            self.copy.wait()
+        return self.ref
+
+
+class Outgoing:
+    def __init__(self, dst, src, sem):
+        self.ref, self.copy, self.sent = src, pltpu.make_async_copy(src, dst, sem), False
+
+    def send(self):
+        self.sent = True
+        self.copy.start()
+
+
+def call(kernel, outs, scratch, *args, smem=1, early=(), late=(), name=None):
+    single = not isinstance(outs, tuple)
+    outs = (outs,) if single else outs
+    early, late = list(early), list(late)
+    anywhere = pl.BlockSpec(memory_space=pl.ANY)
+    moved = [pltpu.VMEM(args[i].shape, args[i].dtype) for i in early]
+    moved += [pltpu.VMEM(outs[i].shape, outs[i].dtype) for i in late]
+    count = len(moved)
+
+    def body(*refs):
+        ins = list(refs[:len(args)])
+        made = list(refs[len(args):len(args)+len(outs)])
+        rest = refs[len(args)+len(outs):]
+        own, bufs = rest[:len(scratch)], rest[len(scratch):]
+        for n, i in enumerate(early):
+            ins[i] = Incoming(ins[i], bufs[n], bufs[count].at[n])
+        for n, i in enumerate(late, len(early)):
+            made[i] = Outgoing(made[i], bufs[n], bufs[count].at[n])
+        kernel(*ins, *made, *own)
+        for i in early:
+            ins[i]()
+        for i in late:
+            if not made[i].sent:
+                made[i].send()
+            made[i].copy.wait()
+
+    result = pl.pallas_call(
+        body,
         out_shape=outs,
-        in_specs=[SM] * smem + [VM] * (len(args) - smem),
-        out_specs=jax.tree.map(lambda _: VM, outs),
-        scratch_shapes=scratch,
+        in_specs=[SM if i < smem else anywhere if i in early else VM for i in range(len(args))],
+        out_specs=tuple(anywhere if i in late else VM for i in range(len(outs))),
+        scratch_shapes=list(scratch) + moved + ([pltpu.SemaphoreType.DMA((count,))] if count else []),
         name=name,
     )(*args)
+    return result[0] if single else result
 
 
 def tied(*arrays):
@@ -430,7 +507,7 @@
 
     cA, pA, bA, *gA, ctA, wire = call(
         first_kernel, side_t + (wire_t,), seek + [pltpu.SMEM((8, 128), i32), pltpu.SemaphoreType.DMA],
-        outgoing_column, send_level, neutral_wind.reshape(flat), smem=0, name="first")
+        outgoing_column, send_level, neutral_wind.reshape(flat), smem=0, early=(2,), late=(0, 1, 3, 4, 5, 6), name="first")
     came = exchange(wire)
     wire, tub = tied(wire, recv_tube)
     cB, pB, bB, *gB, ctB, gain, drift = call(
@@ -440,20 +517,22 @@
     def tubes(came, ions, last):
         w, smooth, out_last, edge = call(
             tube_kernel, (tube_t, tube_t, sd((2, 1, 512), f32), sd((2, 128, 128), f32)), [vals, accs],
-            bB, coupling, cB, pB, gain, drift, came, ions, inverse, smem=2, name="tube")
+            bB, coupling, cB, pB, gain, drift, came, ions, inverse, smem=2, early=(6, 3, 4, 2, 7, 8, 5), late=(0, 3), name="tube")
         up = lax.ppermute(out_last, "gy", up_route)
         return call(
             lambda *a: drag_kernel(last, *a), (tube_t, wire_t), [tabs] + seek,
-            ctB, drag_rate, *gB, gain, drift, w, smooth, up, ion_density, edge, smem=2, name="drag")
+            ctB, drag_rate, *gB, gain, drift, w, smooth, up, ion_density if last else up, edge, smem=2,
+            early=(9, 8) + ((11,) if last else ()) + (7, 2, 12, 5, 6, 3, 4), late=(0,), name="drag")
 
     n1, wire = tubes(came, ion_density, False)
     mid, wire = call(
         mid_kernel, (sd(flat, f32), wire_t), [vals, accs] + seek,
-        bA, ctA, cA, pA, *gA, exchange(wire), neutral_wind, forcing, visc, smem=2, name="mid")
+        bA, ctA, cA, pA, *gA, exchange(wire), neutral_wind, forcing, visc, smem=2,
+        early=(8, 3, 2, 9, 10, 4, 7, 5, 6), late=(0,), name="mid")
     ion_out, wire = tubes(exchange(wire), n1, True)
     wind_out = call(
         end_kernel, sd(neutral_wind.shape, f32), [vals, accs],
-        bA, cA, pA, exchange(wire), neutral_wind, mid.reshape(neutral_wind.shape), forcing, visc, name="end")
+        bA, cA, pA, exchange(wire), neutral_wind, mid.reshape(neutral_wind.shape), forcing, visc, early=(3, 2, 1, 5, 6, 4), name="end")
     return (wind_out, ion_out)
 
 

time: 166 us -> 169 us (1.018)
  Pallas kernels: 80.7 us -> 83.3 us
    pallas_call x8, Pallas kernels: 80.7 us -> 83.3 us  [call(): pl.pallas_call(body, out_shape=outs, in_specs=[SM if i < smem else anywhe...]
where the time goes in v8:
time: 169 us; the launch traced here: 168 us
  Pallas kernels  83.3 us (49%)
  blocking collectives  55.2 us (33%)
  starting transfers between devices  18.1 us (11%)
  waiting for transfers between devices  8.65 us (5%)
  local copies, waits for them, and re-layouts  1.92 us (1%)
    pallas_call x8, Pallas kernels, call(): pl.pallas_call(body, out_shape=outs, in_specs=[SM if i < smem else anywhe...  83.3 us
    all_to_all x3, blocking collectives, exchange(): lax.all_to_all(x, ('gx', 'gy'), split_axis=0, concat_axis=0, tiled=True)  55.2 us
    all_to_all x1, starting transfers between devices, exchange(): lax.all_to_all(x, ('gx', 'gy'), split_axis=0, concat_axis=0, tiled=True)  11.5 us
    all_to_all x1, waiting for transfers between devices, exchange(): lax.all_to_all(x, ('gx', 'gy'), split_axis=0, concat_axis=0, tiled=True)  6.76 us
    ppermute x2, starting transfers between devices, tubes(): up = lax.ppermute(out_last, 'gy', up_route)  6.64 us
  transfers between devices with their start and end apart: 3, of which 3 were waited for; matrix products, arithmetic and copies ran while one was open for 0% of the time, Pallas kernels for 3%

profile of v8, /device:TPU:1, one launch (start us, length us, event | category | flops | bytes accessed | tf_op | source)
XLA Modules:
  0.0 168.1 jit_solution(9010275409361870008)
XLA Ops:
  0.6 10.1 %first.1 = (s32[256,128]{1,0:T(8,128)}, s32[128,256]{1,0:T(8,128)}, s32[32,128]{1,0:T(8,128)}, s32[1024,128]{1,0:T(8,128)}, s32[128,256]{1,0:T(8,128)}, /*index=...) custom-call(s32[1,128,256]{2,1,0:T(8,128)} %refs_0_.1, s32[1,128,256]{2,1,0:T(8,128)} %refs_1_.6, ...), custom_call_target="tpu_custom_call" | custom-call | tf_op jit(solution)/shard_map/first/pallas_call | solution.py:459
  10.7 11.5 %all-to-all-start = ((f32[128,3,2,128]{3,2,1,0:T(2,128)}), f32[128,3,2,128]{3,2,1,0:T(2,128)S(1)}, u32[]{:S(2)}, u32[]{:S(2)}) async-start(f32[128,3,2,128]{3,2,1,0:T(2,128)} %bitcast.18), calls=%async_computation | async-start | bytes 786432 | tf_op jit(solution)/shard_map/all_to_all | solution.py:476
  22.2 5.2 %tubesort.1 = (s32[256,128]{1,0:T(8,128)}, s32[128,256]{1,0:T(8,128)}, s32[32,128]{1,0:T(8,128)}, s32[1024,128]{1,0:T(8,128)}, s32[128,256]{1,0:T(8,128)}, /*ind...) custom-call(s32[1,128,256]{2,1,0:T(8,128)} %refs_0_.2, ...), custom_call_target="tpu_custom_call" | custom-call | tf_op jit(solution)/shard_map/tubesort/pallas_call | solution.py:459
  27.4 6.8 %all-to-all-done = f32[128,3,2,128]{3,2,1,0:T(2,128)S(1)} async-done(((f32[128,3,2,128]{3,2,1,0:T(2,128)}), f32[128,3,2,128]{3,2,1,0:T(2,128)S(1)}, u32[]{:S(2)}, u32[]{:S(2)}) %all-to-all-start) | async-done | bytes 393248 | tf_op jit(solution)/shard_map/all_to_all | solution.py:476
  34.1 0.0 copy-start
  34.1 0.8 copy-done
  34.9 12.0 %tube.2 = (f32[2,128,512]{2,1,0:T(8,128)}, f32[2,128,512]{2,1,0:T(8,128)}, f32[2,1,512]{2,1,0:T(1,128)}, f32[2,128,128]{2,1,0:T(8,128)}) custom-call(s32[32,128]{1,0:T(8,128)} %get-tuple-element.48.refs_0_, f32[2,2]{1,0:T(2,128)} %refs_1_.10, s32[256,128]{1,0:T(8,128)} %get-tuple-element.49.refs_2_, s32[128,256]{1,0:T(8,128)} %get-tuple-element.50.refs_3_, ...), custom_call_target="tpu_custom_call" | custom-call | tf_op jit(solution)/shard_map/tube/pallas_call | solution.py:459
  46.9 3.3 %collective-permute-start = (f32[2,1,512]{2,1,0:T(1,128)}, f32[2,1,512]{2,1,0:T(1,128)S(1)}, u32[]{:S(2)}, u32[]{:S(2)}) collective-permute-start(f32[2,1,512]{2,1,0:T(1,128)} %get-tuple-element.58), channel_id=1, source_target_pairs={{0,1},{1,2},{2,3},{3,4},{4,5},{5,6},{6,7},{7,8},{8,9},{9,10},{10,1... | collective-permute-start | bytes 12296 | tf_op jit(solution)/shard_map/ppermute | solution.py:521
  50.2 0.9 collective-permute-done.refs_10_.refs_11_
  51.2 0.0 copy-start.1
  51.2 0.6 copy-done.1
  51.8 8.1 %drag.2 = (f32[2,128,512]{2,1,0:T(8,128)}, f32[768,128]{1,0:T(8,128)}) custom-call(s32[8,128]{1,0:T(8,128)} %get-tuple-element.41.refs_0_, f32[2]{0:T(128)} %refs_1_.11, s32[1024,128]{1,0:T(8,128)} %get-tuple-element.42.refs_2_, s32[128,256]{1,0:T(8,128)} %get-tuple-element.43.refs_3_, s32[128,128]{1,0:T(8,128)} %get-tuple-element.44.refs_4_, ...), custom_call_target="tpu_custom_call" | custom-call | tf_op jit(solution)/shard_map/drag/pallas_call | solution.py:459
  59.9 18.8 %all_to_all.20 = f32[128,3,2,128]{3,2,1,0:T(2,128)} all-to-all(f32[128,3,2,128]{3,2,1,0:T(2,128)} %bitcast.21), channel_id=1, replica_groups=mesh['gx'=8,'gy'=16] {'gx','gy'}, dimensions={0} | all-to-all | bytes 786432 | tf_op jit(solution)/shard_map/all_to_all | solution.py:476
  78.6 16.4 %mid.1 = (f32[2,512,128]{2,1,0:T(8,128)}, f32[768,128]{1,0:T(8,128)}) custom-call(s32[32,128]{1,0:T(8,128)} %get-tuple-element.36.refs_0_, s32[8,128]{1,0:T(8,128)} %get-tuple-element.51.refs_1_, s32[256,128]{1,0:T(8,128)} %get-tuple-element.37.refs_2_.refs_1_, s32[128,256]{1,0:T(8,128)} %get-tuple-element.38.refs_3_.refs_2_, ...), custom_call_target="tpu_custom_call" | custom-call | tf_op jit(solution)/shard_map/mid/pallas_call | solution.py:459
  95.1 17.7 %all_to_all.21 = f32[128,3,2,128]{3,2,1,0:T(2,128)} all-to-all(f32[128,3,2,128]{3,2,1,0:T(2,128)} %bitcast.20), channel_id=1, replica_groups=mesh['gx'=8,'gy'=16] {'gx','gy'}, dimensions={0} | all-to-all | bytes 786432 | tf_op jit(solution)/shard_map/all_to_all | solution.py:476
  112.7 12.0 %tube.3 = (f32[2,128,512]{2,1,0:T(8,128)}, f32[2,128,512]{2,1,0:T(8,128)}, f32[2,1,512]{2,1,0:T(1,128)}, f32[2,128,128]{2,1,0:T(8,128)}) custom-call(s32[32,128]{1,0:T(8,128)} %get-tuple-element.48.refs_0_, f32[2,2]{1,0:T(2,128)} %refs_1_.10, s32[256,128]{1,0:T(8,128)} %get-tuple-element.49.refs_2_, s32[128,256]{1,0:T(8,128)} %get-tuple-element.50.refs_3_, ...), custom_call_target="tpu_custom_call" | custom-call | tf_op jit(solution)/shard_map/tube/pallas_call | solution.py:459
  124.7 3.3 %collective-permute-start.1 = (f32[2,1,512]{2,1,0:T(1,128)}, f32[2,1,512]{2,1,0:T(1,128)S(1)}, u32[]{:S(2)}, u32[]{:S(2)}) collective-permute-start(f32[2,1,512]{2,1,0:T(1,128)} %get-tuple-element.65), channel_id=1, source_target_pairs={{0,1},{1,2},{2,3},{3,4},{4,5},{5,6},{6,7},{7,8},{8,9},{9,10},{10,1... | collective-permute-start | bytes 12296 | tf_op jit(solution)/shard_map/ppermute | solution.py:521
  128.1 0.9 collective-permute-done.1.refs_10_
  129.0 0.0 copy-start.2
  129.0 0.6 copy-done.2
  129.6 8.1 %drag.3 = (f32[2,128,512]{2,1,0:T(8,128)}, f32[768,128]{1,0:T(8,128)}) custom-call(s32[8,128]{1,0:T(8,128)} %get-tuple-element.41.refs_0_, f32[2]{0:T(128)} %refs_1_.11, s32[1024,128]{1,0:T(8,128)} %get-tuple-element.42.refs_2_, s32[128,256]{1,0:T(8,128)} %get-tuple-element.43.refs_3_, s32[128,128]{1,0:T(8,128)} %get-tuple-element.44.refs_4_, ...), custom_call_target="tpu_custom_call" | custom-call | tf_op jit(solution)/shard_map/drag/pallas_call | solution.py:459
  137.7 18.8 %all_to_all.22 = f32[128,3,2,128]{3,2,1,0:T(2,128)} all-to-all(f32[128,3,2,128]{3,2,1,0:T(2,128)} %bitcast.19), channel_id=1, replica_groups=mesh['gx'=8,'gy'=16] {'gx','gy'}, dimensions={0} | all-to-all | bytes 786432 | tf_op jit(solution)/shard_map/all_to_all | solution.py:476
  156.5 11.5 %end.1 = f32[2,16,32,128]{3,2,1,0:T(8,128)} custom-call(s32[32,128]{1,0:T(8,128)} %get-tuple-element.36.refs_0_, s32[256,128]{1,0:T(8,128)} %get-tuple-element.37.refs_2_.refs_1_, s32[128,256]{1,0:T(8,128)} %get-tuple-element.38.refs_3_.refs_2_, f32[768,128]{1,0:T(8,128)} %bitcast.13, f32[2,16,32,128]{3,2,1,0:T(8,128)} %refs_4_.1, ...), custom_call_target="tpu_custom_call" | custom-call | tf_op jit(solution)/shard_map/end/pallas_call | solution.py:459
Async XLA Ops:
  10.7 23.4 %all-to-all-start = ((f32[128,3,2,128]{3,2,1,0:T(2,128)}), f32[128,3,2,128]{3,2,1,0:T(2,128)S(1)}, u32[]{:S(2)}, u32[]{:S(2)}) async-start(f32[128,3,2,128]{3,2,1,0:T(2,128)} %bitcast.18), calls=%async_computation | async-start | bytes 786432 | tf_op jit(solution)/shard_map/all_to_all | solution.py:476
  34.1 0.8 copy-start
  46.9 4.3 %collective-permute-start = (f32[2,1,512]{2,1,0:T(1,128)}, f32[2,1,512]{2,1,0:T(1,128)S(1)}, u32[]{:S(2)}, u32[]{:S(2)}) collective-permute-start(f32[2,1,512]{2,1,0:T(1,128)} %get-tuple-element.58), channel_id=1, source_target_pairs={{0,1},{1,2},{2,3},{3,4},{4,5},{5,6},{6,7},{7,8},{8,9},{9,10},{10,1... | collective-permute-start | bytes 12296 | tf_op jit(solution)/shard_map/ppermute | solution.py:521
  51.2 0.6 copy-start.1
  124.7 4.3 %collective-permute-start.1 = (f32[2,1,512]{2,1,0:T(1,128)}, f32[2,1,512]{2,1,0:T(1,128)S(1)}, u32[]{:S(2)}, u32[]{:S(2)}) collective-permute-start(f32[2,1,512]{2,1,0:T(1,128)} %get-tuple-element.65), channel_id=1, source_target_pairs={{0,1},{1,2},{2,3},{3,4},{4,5},{5,6},{6,7},{7,8},{8,9},{9,10},{10,1... | collective-permute-start | bytes 12296 | tf_op jit(solution)/shard_map/ppermute | solution.py:521
  129.0 0.6 copy-start.2

commit v9 on v7

--- a/solution.py
+++ b/solution.py
@@ -8,7 +8,7 @@
 i32, f32, bf16 = jnp.int32, jnp.float32, jnp.bfloat16
 VM = pl.BlockSpec(memory_space=pltpu.VMEM)
 SM = pl.BlockSpec(memory_space=pltpu.SMEM)
-W, NB, UN = 80, 16, 2
+W, NB, UN, GB, LIMIT = 80, 16, 2, 16, 24
 neutral_step = 0.4
 ion_factor = 0.5
 
@@ -167,14 +167,14 @@
 def lookup(ctl, slot, order, first, place, t_ref, wire, s_ref, key_ref, gain=None, limit_copy=None):
     half = t_ref.shape[1] // 2
 
-    def group(g, keys):
-        for b in range(8):
+    def group(at_bucket, count, keys):
+        for b in range(count):
             rows = []
             for j in range(8):
-                at = g*32 + 4*b + j//2 + (j % 2)*half
+                at = at_bucket*4 + 4*b + j//2 + (j % 2)*half
                 rows.append([jnp.broadcast_to(t_ref[k, pl.ds(at, 1), :], (8, 128)) for k in range(2)])
             for i in range(2):
-                sl = pl.ds(pl.multiple_of(g*128 + b*16 + i*8, 8), 8)
+                sl = pl.ds(pl.multiple_of(at_bucket*16 + b*16 + i*8, 8), 8)
                 key = keys[sl, :]
                 sub, lev = key >> 7, key & 127
                 acc = [take(rows[0][k], lev) for k in range(2)]
@@ -186,13 +186,13 @@
                     s_ref[k, sl, :] = acc[k]
 
     def each(g, _):
-        group(g, slot)
+        group(g*GB, GB, slot)
         return 0
 
     def scaled(x, h):
         return x if gain is None else x * gain[:, h*128:(h+1)*128]
 
-    lax.fori_loop(0, 8, each, 0)
+    lax.fori_loop(0, 64//GB, each, 0)
     if limit_copy is not None:
         limit_copy.start()
     parts = [[s_ref[k, j*128:(j+1)*128, :].T for j in range(8)] for k in range(2)]
@@ -214,7 +214,7 @@
             @pl.when(most > 16*t)
             def _():
                 slot_tile(order[...], first, t, g, key_ref)
-                group(g, key_ref)
+                group(g*8, 8, key_ref)
                 tile = pl.ds(pl.multiple_of(g*128, 128), 128)
                 for h in range(2):
                     at = place[:, h*128:(h+1)*128]
@@ -386,6 +386,7 @@
         in_specs=[SM] * smem + [VM] * (len(args) - smem),
         out_specs=jax.tree.map(lambda _: VM, outs),
         scratch_shapes=scratch,
+        compiler_params=pltpu.CompilerParams(vmem_limit_bytes=LIMIT << 20),
         name=name,
     )(*args)
 

time: 166 us -> 161 us (0.970)
  Pallas kernels: 80.7 us -> 66.8 us
  local copies, waits for them, and re-layouts: 1.92 us -> 14.3 us
  waiting for transfers between devices: 8.65 us -> 4.4 us
    pallas_call x8, Pallas kernels: 80.7 us -> 66.8 us  [call(): pl.pallas_call(kernel, out_shape=outs, in_specs=[SM] * smem + [VM] * (len...]
    unnamed x6 -> x60, local copies, waits for them, and re-layouts: 1.92 us -> 14.3 us
    all_to_all x1, waiting for transfers between devices: 6.76 us -> 3.11 us  [exchange(): lax.all_to_all(x, ('gx', 'gy'), split_axis=0, concat_axis=0, tiled=True)]
  transfers between devices with their start and end apart: 3 -> 3, of which waited for: 3 -> 3; matrix products, arithmetic and copies ran while one was open for 0% -> 0% of each run, Pallas kernels for 3% -> 2%
where the time goes in v9:
time: 161 us; the launch traced here: 160 us
  Pallas kernels  66.8 us (41%)
  blocking collectives  55.3 us (34%)
  starting transfers between devices  18.3 us (11%)
  local copies, waits for them, and re-layouts  14.3 us (9%)
  waiting for transfers between devices  4.4 us (3%)
    pallas_call x8, Pallas kernels, call(): pl.pallas_call(kernel, out_shape=outs, in_specs=[SM] * smem + [VM] * (len...  66.8 us
    all_to_all x3, blocking collectives, exchange(): lax.all_to_all(x, ('gx', 'gy'), split_axis=0, concat_axis=0, tiled=True)  55.3 us
    unnamed x60, local copies, waits for them, and re-layouts  14.3 us
    all_to_all x1, starting transfers between devices, exchange(): lax.all_to_all(x, ('gx', 'gy'), split_axis=0, concat_axis=0, tiled=True)  11.5 us
    ppermute x2, starting transfers between devices, tubes(): up = lax.ppermute(out_last, 'gy', up_route)  6.82 us
  transfers between devices with their start and end apart: 3, of which 3 were waited for; matrix products, arithmetic and copies ran while one was open for 0% of the time, Pallas kernels for 2%

profile of v9, /device:TPU:1, one launch (start us, length us, event | category | flops | bytes accessed | tf_op | source)
XLA Modules:
  0.0 159.9 jit_solution(10202245327455745970)
XLA Ops:
  0.6 0.0 copy-start
  0.6 1.0 copy-done
  1.7 0.9 copy-done.11
  2.6 0.9 copy-done.12
  3.5 8.7 %first.1 = (s32[256,128]{1,0:T(8,128)S(1)}, s32[128,256]{1,0:T(8,128)S(1)}, s32[32,128]{1,0:T(8,128)S(1)}, s32[1024,128]{1,0:T(8,128)S(1)}, s32[128,256]{1,0:T(8...) custom-call(s32[1,128,256]{2,1,0:T(8,128)S(1)} %copy-done.11, ...), custom_call_target="tpu_custom_call" | custom-call | tf_op jit(solution)/shard_map/first/pallas_call | solution.py:383
  12.2 0.0 copy-start.5
  12.2 0.8 copy-done.5
  13.0 0.7 copy-done.7
  13.6 0.7 copy-done.9
  14.3 0.6 copy-done.19
  14.9 0.6 copy-done.24
  15.5 11.5 %all-to-all-start = ((f32[128,3,2,128]{3,2,1,0:T(2,128)}), f32[128,3,2,128]{3,2,1,0:T(2,128)S(1)}, u32[]{:S(2)}, u32[]{:S(2)}) async-start(f32[128,3,2,128]{3,2,1,0:T(2,128)} %bitcast.2), calls=%async_computation | async-start | bytes 786432 | tf_op jit(solution)/shard_map/all_to_all | solution.py:400
  27.0 0.0 copy-start.29
  27.0 0.6 copy-done.29
  27.7 0.9 copy-done.13
  28.6 0.9 copy-done.14
  29.5 0.9 copy-done.15
  30.4 0.8 copy-done.21
  31.2 3.4 %tubesort.1 = (s32[256,128]{1,0:T(8,128)S(1)}, s32[128,256]{1,0:T(8,128)S(1)}, s32[32,128]{1,0:T(8,128)S(1)}, s32[1024,128]{1,0:T(8,128)S(1)}, s32[128,256]{1,0:...) custom-call(s32[1,128,256]{2,1,0:T(8,128)S(1)} %copy-done.13, ...), custom_call_target="tpu_custom_call" | custom-call | tf_op jit(solution)/shard_map/tubesort/pallas_call | solution.py:383
  34.6 0.0 copy-start.16
  34.6 0.6 copy-done.16
  35.2 0.6 copy-done.22
  35.8 3.1 %all-to-all-done = f32[128,3,2,128]{3,2,1,0:T(2,128)S(1)} async-done(((f32[128,3,2,128]{3,2,1,0:T(2,128)}), f32[128,3,2,128]{3,2,1,0:T(2,128)S(1)}, u32[]{:S(2)}, u32[]{:S(2)}) %all-to-all-start) | async-done | bytes 393248 | tf_op jit(solution)/shard_map/all_to_all | solution.py:400
  38.9 0.0 copy-done.3
  38.9 0.0 copy-done.2
  38.9 0.7 copy-done.26
  39.6 0.7 copy-done.17
  40.3 9.3 %tube.2 = (f32[2,128,512]{2,1,0:T(8,128)S(1)}, f32[2,128,512]{2,1,0:T(8,128)S(1)}, f32[2,1,512]{2,1,0:T(1,128)S(1)}, f32[2,128,128]{2,1,0:T(8,128)S(1)}) custom-call(s32[32,128]{1,0:T(8,128)S(1)} %copy-done.17, f32[2,2]{1,0:T(2,128)S(1)} %copy-done.26, s32[256,128]{1,0:T(8,128)S(1)} %get-tuple-element.49.cell, s32[128,256]{1,0:T(8,128)S(1)} %get-tuple-element.50.pos, ...), custom_call_target="tpu_custom_call" | custom-call | tf_op jit(solution)/shard_map/tube/pallas_call | solution.py:383
  49.7 3.5 %collective-permute-start = (f32[2,1,512]{2,1,0:T(1,128)S(1)}, f32[2,1,512]{2,1,0:T(1,128)S(1)}, u32[]{:S(2)}, u32[]{:S(2)}) collective-permute-start(f32[2,1,512]{2,1,0:T(1,128)S(1)} %get-tuple-element.58), channel_id=1, source_target_pairs={{0,1},{1,2},{2,3},{3,4},{4,5},{5,6},{6,7},{7,8},{8,9},{9,10},{10,1... | collective-permute-start | bytes 12296 | tf_op jit(solution)/shard_map/ppermute | solution.py:445
  53.2 0.6 collective-permute-done.a_10_
  53.7 0.7 copy-done.23
  54.4 0.0 copy-done.27
  54.4 5.4 %drag.2 = (f32[2,128,512]{2,1,0:T(8,128)S(1)}, f32[768,128]{1,0:T(8,128)S(1)}) custom-call(s32[8,128]{1,0:T(8,128)S(1)} %copy-done.23, f32[2]{0:T(128)S(1)} %copy-done.27, s32[1024,128]{1,0:T(8,128)S(1)} %get-tuple-element.42.a_2_, s32[128,256]{1,0:T(8,128)S(1)} %get-tuple-element.43.a_3_, s32[128,128]{1,0:T(8,128)S(1)} %get-tuple-element.44.a_4_, ...), custom_call_target="tpu_custom_call" | custom-call | tf_op jit(solution)/shard_map/drag/pallas_call | solution.py:383
  59.9 0.0 copy-start.1
  59.9 0.0 copy-start.8
  59.9 0.0 copy-start.10
  59.9 20.1 %all_to_all.20 = f32[128,3,2,128]{3,2,1,0:T(2,128)S(1)} all-to-all(f32[128,3,2,128]{3,2,1,0:T(2,128)S(1)} %bitcast.20), channel_id=1, replica_groups=mesh['gx'=8,'gy'=16] {'gx','gy'}, dimensions={0} | all-to-all | bytes 786432 | tf_op jit(solution)/shard_map/all_to_all | solution.py:400
  80.0 0.0 copy-done.4
  80.0 0.0 copy-done.6
  80.1 0.6 copy-done.25
  80.7 14.1 %mid.1 = (f32[2,512,128]{2,1,0:T(8,128)S(1)}, f32[768,128]{1,0:T(8,128)S(1)}) custom-call(s32[32,128]{1,0:T(8,128)S(1)} %get-tuple-element.36.bnd, s32[8,128]{1,0:T(8,128)S(1)} %copy-done.25, s32[256,128]{1,0:T(8,128)S(1)} %get-tuple-element.37.cell, s32[128,256]{1,0:T(8,128)S(1)} %get-tuple-element.38.pos, s32[1024,128]{1,0:T(8,128)S(1)} %copy-done.6, ...), custom_call_target="tpu_custom_call" | custom-call | tf_op jit(solution)/shard_map/mid/pallas_call | solution.py:383
  94.8 16.7 %all_to_all.21 = f32[128,3,2,128]{3,2,1,0:T(2,128)S(1)} all-to-all(f32[128,3,2,128]{3,2,1,0:T(2,128)S(1)} %bitcast.19), channel_id=1, replica_groups=mesh['gx'=8,'gy'=16] {'gx','gy'}, dimensions={0} | all-to-all | bytes 786432 | tf_op jit(solution)/shard_map/all_to_all | solution.py:400
  111.6 9.3 %tube.3 = (f32[2,128,512]{2,1,0:T(8,128)S(1)}, f32[2,128,512]{2,1,0:T(8,128)S(1)}, f32[2,1,512]{2,1,0:T(1,128)S(1)}, f32[2,128,128]{2,1,0:T(8,128)S(1)}) custom-call(s32[32,128]{1,0:T(8,128)S(1)} %copy-done.18, f32[2,2]{1,0:T(2,128)S(1)} %copy-done.26, s32[256,128]{1,0:T(8,128)S(1)} %get-tuple-element.49.cell, s32[128,256]{1,0:T(8,128)S(1)} %get-tuple-element.50.pos, ...), custom_call_target="tpu_custom_call" | custom-call | tf_op jit(solution)/shard_map/tube/pallas_call | solution.py:383
  120.9 3.3 %collective-permute-start.1 = (f32[2,1,512]{2,1,0:T(1,128)S(1)}, f32[2,1,512]{2,1,0:T(1,128)S(1)}, u32[]{:S(2)}, u32[]{:S(2)}) collective-permute-start(f32[2,1,512]{2,1,0:T(1,128)S(1)} %get-tuple-element.65), channel_id=1, source_target_pairs={{0,1},{1,2},{2,3},{3,4},{4,5},{5,6},{6,7},{7,8},{8,9},{9,10},{10,1... | collective-permute-start | bytes 12296 | tf_op jit(solution)/shard_map/ppermute | solution.py:445
  124.2 0.7 collective-permute-done.1.a_10_
  125.0 6.3 %drag.3 = (f32[2,128,512]{2,1,0:T(8,128)}, f32[768,128]{1,0:T(8,128)S(1)}) custom-call(s32[8,128]{1,0:T(8,128)S(1)} %copy-done.23, f32[2]{0:T(128)S(1)} %copy-done.27, s32[1024,128]{1,0:T(8,128)S(1)} %get-tuple-element.42.a_2_, s32[128,256]{1,0:T(8,128)S(1)} %get-tuple-element.43.a_3_, s32[128,128]{1,0:T(8,128)S(1)} %get-tuple-element.44.a_4_, ...), custom_call_target="tpu_custom_call" | custom-call | tf_op jit(solution)/shard_map/drag/pallas_call | solution.py:383
  131.2 18.4 %all_to_all.22 = f32[128,3,2,128]{3,2,1,0:T(2,128)S(1)} all-to-all(f32[128,3,2,128]{3,2,1,0:T(2,128)S(1)} %bitcast.18), channel_id=1, replica_groups=mesh['gx'=8,'gy'=16] {'gx','gy'}, dimensions={0} | all-to-all | bytes 786432 | tf_op jit(solution)/shard_map/all_to_all | solution.py:400
  149.7 10.3 %end.1 = f32[2,16,32,128]{3,2,1,0:T(8,128)} custom-call(s32[32,128]{1,0:T(8,128)S(1)} %get-tuple-element.36.bnd, s32[256,128]{1,0:T(8,128)S(1)} %get-tuple-element.37.cell, s32[128,256]{1,0:T(8,128)S(1)} %get-tuple-element.38.pos, f32[768,128]{1,0:T(8,128)S(1)} %bitcast.13, f32[2,16,32,128]{3,2,1,0:T(8,128)S(1)} %copy-done.1, ...), custom_call_target="tpu_custom_call" | custom-call | tf_op jit(solution)/shard_map/end/pallas_call | solution.py:383
  (29 shorter events, 0.0 us)
Async XLA Ops:
  0.6 1.0 copy-start
  1.7 0.9 copy-start.11
  2.6 0.9 copy-start.12
  3.5 35.5 %copy-start.3 = (bf16[1,2,512,512]{3,2,1,0:T(8,128)(2,1)S(1)}, bf16[1,2,512,512]{3,2,1,0:T(8,128)(2,1)}, u32[]{:S(2)}) copy-start(bf16[1,2,512,512]{3,2,1,0:T(8,128)(2,1)} %inverse.3) | copy-start | bytes 3145732
  12.2 0.8 copy-start.5
  13.0 0.7 copy-start.7
  13.6 0.7 copy-start.9
  14.3 0.6 copy-start.19
  14.9 0.6 copy-start.24
  15.5 23.4 %copy-start.2 = (f32[2,128,512]{2,1,0:T(8,128)S(1)}, f32[2,128,512]{2,1,0:T(8,128)}, u32[]{:S(2)}) copy-start(f32[2,128,512]{2,1,0:T(8,128)} %a_11_.3) | copy-start | bytes 1572868
  15.5 23.4 %all-to-all-start = ((f32[128,3,2,128]{3,2,1,0:T(2,128)}), f32[128,3,2,128]{3,2,1,0:T(2,128)S(1)}, u32[]{:S(2)}, u32[]{:S(2)}) async-start(f32[128,3,2,128]{3,2,1,0:T(2,128)} %bitcast.2), calls=%async_computation | async-start | bytes 786432 | tf_op jit(solution)/shard_map/all_to_all | solution.py:400
  27.0 0.7 copy-start.29
  27.7 0.9 copy-start.13
  28.6 0.9 copy-start.14
  29.5 0.9 copy-start.15
  30.4 0.8 copy-start.21
  34.6 0.6 copy-start.16
  35.2 0.6 copy-start.22
  38.9 0.7 copy-start.26
  39.6 0.7 copy-start.17
  49.7 4.1 %collective-permute-start = (f32[2,1,512]{2,1,0:T(1,128)S(1)}, f32[2,1,512]{2,1,0:T(1,128)S(1)}, u32[]{:S(2)}, u32[]{:S(2)}) collective-permute-start(f32[2,1,512]{2,1,0:T(1,128)S(1)} %get-tuple-element.58), channel_id=1, source_target_pairs={{0,1},{1,2},{2,3},{3,4},{4,5},{5,6},{6,7},{7,8},{8,9},{9,10},{10,1... | collective-permute-start | bytes 12296 | tf_op jit(solution)/shard_map/ppermute | solution.py:445
  53.7 0.7 copy-start.23
  53.7 0.7 copy-start.27
  54.4 25.6 %copy-start.4 = (f32[2,16,32,128]{3,2,1,0:T(8,128)S(1)}, f32[2,16,32,128]{3,2,1,0:T(8,128)}, u32[]{:S(2)}) copy-start(f32[2,16,32,128]{3,2,1,0:T(8,128)} %forcing.3) | copy-start | bytes 1572868
  54.4 25.6 %copy-start.6 = (s32[1024,128]{1,0:T(8,128)S(1)}, s32[1024,128]{1,0:T(8,128)}, u32[]{:S(2)}) copy-start(s32[1024,128]{1,0:T(8,128)} %copy-done.5) | copy-start | bytes 1572868
  54.4 25.6 %copy-start.20 = (s32[128,128]{1,0:T(8,128)S(1)}, s32[128,128]{1,0:T(8,128)}, u32[]{:S(2)}) copy-start(s32[128,128]{1,0:T(8,128)} %copy-done.19) | copy-start | bytes 196612
  59.9 20.2 %copy-start.1 = (f32[2,16,32,128]{3,2,1,0:T(8,128)S(1)}, f32[2,16,32,128]{3,2,1,0:T(8,128)}, u32[]{:S(2)}) copy-start(f32[2,16,32,128]{3,2,1,0:T(8,128)} %start.1) | copy-start | bytes 1572868
  59.9 20.2 %copy-start.8 = (s32[128,256]{1,0:T(8,128)S(1)}, s32[128,256]{1,0:T(8,128)}, u32[]{:S(2)}) copy-start(s32[128,256]{1,0:T(8,128)} %copy-done.7) | copy-start | bytes 393220
  59.9 20.2 %copy-start.10 = (s32[128,256]{1,0:T(8,128)S(1)}, s32[128,256]{1,0:T(8,128)}, u32[]{:S(2)}) copy-start(s32[128,256]{1,0:T(8,128)} %copy-done.9) | copy-start | bytes 393220
  80.0 0.7 copy-start.25
  80.0 0.7 copy-start.28
  94.8 16.7 %copy-start.18 = (s32[32,128]{1,0:T(8,128)S(1)}, s32[32,128]{1,0:T(8,128)}, u32[]{:S(2)}) copy-start(s32[32,128]{1,0:T(8,128)} %copy-done.16) | copy-start | bytes 49156
  120.9 4.1 %collective-permute-start.1 = (f32[2,1,512]{2,1,0:T(1,128)S(1)}, f32[2,1,512]{2,1,0:T(1,128)S(1)}, u32[]{:S(2)}, u32[]{:S(2)}) collective-permute-start(f32[2,1,512]{2,1,0:T(1,128)S(1)} %get-tuple-element.65), channel_id=1, source_target_pairs={{0,1},{1,2},{2,3},{3,4},{4,5},{5,6},{6,7},{7,8},{8,9},{9,10},{10,1... | collective-permute-start | bytes 12296 | tf_op jit(solution)/shard_map/ppermute | solution.py:445

commit v10 on v9

--- a/solution.py
+++ b/solution.py
@@ -8,7 +8,8 @@
 i32, f32, bf16 = jnp.int32, jnp.float32, jnp.bfloat16
 VM = pl.BlockSpec(memory_space=pltpu.VMEM)
 SM = pl.BlockSpec(memory_space=pltpu.SMEM)
-W, NB, UN, GB, LIMIT = 80, 16, 2, 16, 24
+W, NB, UN, GB = 80, 16, 2, 16
+LIMITS = {"first": None, "tubesort": 24, "tube0": 24, "drag0": 24, "mid": 24, "tube1": 24, "drag1": 24, "end": 24}
 neutral_step = 0.4
 ion_factor = 0.5
 
@@ -229,10 +230,13 @@
 
     if limit_copy is not None:
         limit_copy.wait()
+    else:
+        ctl = ctl()
     lax.fori_loop(1, (ctl[0, 64] + 15) // 16, turn, 0)
 
 
 def scatter_add(bnd, cell_ref, val_ref, acc_ref):
+    bnd = bnd()
     acc_ref[...] = jnp.zeros_like(acc_ref)
     iota = lax.broadcasted_iota(i32, (256, 128), 0).astype(f32).astype(bf16)
     one, zero = jnp.ones((256, 128), bf16), jnp.zeros((256, 128), bf16)
@@ -307,6 +311,7 @@
     for k in range(2):
         for j in range(4):
             w_out[k, :, j*128:(j+1)*128] = acc[k, (j%2)*128:(j%2+1)*128, (j//2)*128:(j//2+1)*128]
+    coupling = coupling()
     for k in range(2):
         n = ions[k]
         growth = coupling[k, 0] * w_out[0] + coupling[k, 1] * w_out[1]
@@ -332,6 +337,7 @@
             x = sm - out + inflow
             n[k].append(x)
             n_out[k, :, sl] = 0.5 * (ions[k, :, sl] + x) if last else x
+    drag = drag()
     for j in range(4):
         f = -(drag[0] * n[0][j] + drag[1] * n[1][j])
         for k in range(2):
@@ -344,7 +350,7 @@
     xlo, xhi, ylo, yhi = beside_tile(wire)
     sub = lax.broadcasted_iota(i32, (CY, 128), 0)
     lane = lax.broadcasted_iota(i32, (CY, 128), 1)
-    v = jnp.broadcast_to(visc[...], (CY, 128))
+    v = jnp.broadcast_to(visc()[...], (CY, 128))
     for k in range(2):
         for i in range(CX):
             u = wind[k, i]
@@ -379,14 +385,41 @@
     tend_all(wind, forcing, visc, wire, acc, emit)
 
 
-def call(kernel, outs, scratch, *args, smem=1, name=None):
+class Incoming:
+    def __init__(self, src, dst, sem):
+        self.ref, self.copy, self.due = dst, pltpu.make_async_copy(src, dst, sem), True
+        self.copy.start()
+
+    def __call__(self):
+        if self.due:
+            self.due = False
+            self.copy.wait()
+        return self.ref
+
+
+def call(kernel, outs, scratch, *args, smem=(), vmem=(), limit=None, name=None):
+    small = list(smem) + list(vmem)
+    boxes = [pltpu.SMEM(args[i].shape, args[i].dtype) for i in smem]
+    boxes += [pltpu.VMEM(args[i].shape, args[i].dtype) for i in vmem]
+    boxes += [pltpu.SemaphoreType.DMA((len(small),))] if small else []
+
+    def body(*refs):
+        refs = list(refs)
+        own = refs[len(refs) - len(boxes):]
+        refs = refs[:len(refs) - len(boxes)]
+        for n, i in enumerate(small):
+            refs[i] = Incoming(refs[i], own[n], own[-1].at[n])
+        kernel(*refs)
+        for i in small:
+            refs[i]()
+
     return pl.pallas_call(
-        kernel,
+        body,
         out_shape=outs,
-        in_specs=[SM] * smem + [VM] * (len(args) - smem),
+        in_specs=[pl.BlockSpec(memory_space=pltpu.HBM) if i in small else VM for i in range(len(args))],
         out_specs=jax.tree.map(lambda _: VM, outs),
-        scratch_shapes=scratch,
-        compiler_params=pltpu.CompilerParams(vmem_limit_bytes=LIMIT << 20),
+        scratch_shapes=list(scratch) + boxes,
+        compiler_params=pltpu.CompilerParams(vmem_limit_bytes=limit and limit << 20),
         name=name,
     )(*args)
 
@@ -431,30 +464,30 @@
 
     cA, pA, bA, *gA, ctA, wire = call(
         first_kernel, side_t + (wire_t,), seek + [pltpu.SMEM((8, 128), i32), pltpu.SemaphoreType.DMA],
-        outgoing_column, send_level, neutral_wind.reshape(flat), smem=0, name="first")
+        outgoing_column, send_level, neutral_wind.reshape(flat), limit=LIMITS["first"], name="first")
     came = exchange(wire)
     wire, tub = tied(wire, recv_tube)
     cB, pB, bB, *gB, ctB, gain, drift = call(
         tube_sort_kernel, side_t + (sd((128, 256), f32), sd((128, 128), f32)), [],
-        tub, recv_point, recv_weight, pair_count, drift_fraction[None, :], smem=0, name="tubesort")
+        tub, recv_point, recv_weight, pair_count, drift_fraction[None, :], limit=LIMITS["tubesort"], name="tubesort")
 
     def tubes(came, ions, last):
         w, smooth, out_last, edge = call(
             tube_kernel, (tube_t, tube_t, sd((2, 1, 512), f32), sd((2, 128, 128), f32)), [vals, accs],
-            bB, coupling, cB, pB, gain, drift, came, ions, inverse, smem=2, name="tube")
+            bB, coupling, cB, pB, gain, drift, came, ions, inverse, smem=(0, 1), limit=LIMITS["tube1" if last else "tube0"], name="tube")
         up = lax.ppermute(out_last, "gy", up_route)
         return call(
             lambda *a: drag_kernel(last, *a), (tube_t, wire_t), [tabs] + seek,
-            ctB, drag_rate, *gB, gain, drift, w, smooth, up, ion_density, edge, smem=2, name="drag")
+            ctB, drag_rate, *gB, gain, drift, w, smooth, up, ion_density if last else up, edge, smem=(0, 1), limit=LIMITS["drag1" if last else "drag0"], name="drag")
 
     n1, wire = tubes(came, ion_density, False)
     mid, wire = call(
         mid_kernel, (sd(flat, f32), wire_t), [vals, accs] + seek,
-        bA, ctA, cA, pA, *gA, exchange(wire), neutral_wind, forcing, visc, smem=2, name="mid")
+        bA, ctA, cA, pA, *gA, exchange(wire), neutral_wind, forcing, visc, smem=(0, 1), vmem=(11,), limit=LIMITS["mid"], name="mid")
     ion_out, wire = tubes(exchange(wire), n1, True)
     wind_out = call(
         end_kernel, sd(neutral_wind.shape, f32), [vals, accs],
-        bA, cA, pA, exchange(wire), neutral_wind, mid.reshape(neutral_wind.shape), forcing, visc, name="end")
+        bA, cA, pA, exchange(wire), neutral_wind, mid.reshape(neutral_wind.shape), forcing, visc, smem=(0,), vmem=(7,), limit=LIMITS["end"], name="end")
     return (wind_out, ion_out)
 
 

time: 161 us -> 153 us (0.950)
  local copies, waits for them, and re-layouts: 14.3 us -> 5.03 us
  waiting for transfers between devices: 4.4 us -> 6.8 us
    unnamed x60 -> x44, local copies, waits for them, and re-layouts: 14.3 us -> 5.03 us
    all_to_all x1, waiting for transfers between devices: 3.11 us -> 5.51 us  [exchange(): lax.all_to_all(x, ('gx', 'gy'), split_axis=0, concat_axis=0, tiled=True)]
where the time goes in v10:
time: 153 us; the launch traced here: 152 us
  Pallas kernels  67.3 us (44%)
  blocking collectives  53.9 us (35%)
  starting transfers between devices  18.3 us (12%)
  waiting for transfers between devices  6.8 us (4%)
  local copies, waits for them, and re-layouts  5.03 us (3%)
    pallas_call x8, Pallas kernels, call(): pl.pallas_call(body, out_shape=outs, in_specs=[pl.BlockSpec(memory_space=...  67.3 us
    all_to_all x3, blocking collectives, exchange(): lax.all_to_all(x, ('gx', 'gy'), split_axis=0, concat_axis=0, tiled=True)  53.9 us
    all_to_all x1, starting transfers between devices, exchange(): lax.all_to_all(x, ('gx', 'gy'), split_axis=0, concat_axis=0, tiled=True)  11.5 us
    ppermute x2, starting transfers between devices, tubes(): up = lax.ppermute(out_last, 'gy', up_route)  6.83 us
    all_to_all x1, waiting for transfers between devices, exchange(): lax.all_to_all(x, ('gx', 'gy'), split_axis=0, concat_axis=0, tiled=True)  5.51 us
    unnamed x44, local copies, waits for them, and re-layouts  5.03 us
  transfers between devices with their start and end apart: 3, of which 3 were waited for; matrix products, arithmetic and copies ran while one was open for 0% of the time, Pallas kernels for 2%

profile of v10, /device:TPU:1, one launch (start us, length us, event | category | flops | bytes accessed | tf_op | source)
XLA Modules:
  0.0 152.4 jit_solution(6535318264966646963)
XLA Ops:
  0.6 0.0 copy-start.1
  0.6 0.0 copy-start.9
  0.7 0.0 copy-start.10
  0.7 10.4 %first.1 = (s32[256,128]{1,0:T(8,128)}, s32[128,256]{1,0:T(8,128)}, s32[32,128]{1,0:T(8,128)}, s32[1024,128]{1,0:T(8,128)}, s32[128,256]{1,0:T(8,128)}, /*index=...) custom-call(s32[1,128,256]{2,1,0:T(8,128)} %refs_0_.1, s32[1,128,256]{2,1,0:T(8,128)} %refs_1_.6, ...), custom_call_target="tpu_custom_call" | custom-call | tf_op jit(solution)/shard_map/first/pallas_call | solution.py:416
  11.0 0.0 copy-start.2
  11.0 11.5 %all-to-all-start = ((f32[128,3,2,128]{3,2,1,0:T(2,128)}), f32[128,3,2,128]{3,2,1,0:T(2,128)S(1)}, u32[]{:S(2)}, u32[]{:S(2)}) async-start(f32[128,3,2,128]{3,2,1,0:T(2,128)} %bitcast.24), calls=%async_computation | async-start | bytes 786432 | tf_op jit(solution)/shard_map/all_to_all | solution.py:433
  22.5 0.0 copy-done.9
  22.5 0.0 copy-done.10
  22.6 0.0 copy-start.11
  22.6 0.9 copy-done.11
  23.5 0.8 copy-done.14
  24.3 0.7 copy-done.21
  25.0 3.4 %tubesort.1 = (s32[256,128]{1,0:T(8,128)S(1)}, s32[128,256]{1,0:T(8,128)S(1)}, s32[32,128]{1,0:T(8,128)S(1)}, s32[1024,128]{1,0:T(8,128)S(1)}, s32[128,256]{1,0:...) custom-call(s32[1,128,256]{2,1,0:T(8,128)S(1)} %copy-done.9, ...), custom_call_target="tpu_custom_call" | custom-call | tf_op jit(solution)/shard_map/tubesort/pallas_call | solution.py:416
  28.4 0.0 copy-start.15
  28.4 0.6 copy-done.15
  29.0 5.5 %all-to-all-done = f32[128,3,2,128]{3,2,1,0:T(2,128)S(1)} async-done(((f32[128,3,2,128]{3,2,1,0:T(2,128)}), f32[128,3,2,128]{3,2,1,0:T(2,128)S(1)}, u32[]{:S(2)}, u32[]{:S(2)}) %all-to-all-start) | async-done | bytes 393248 | tf_op jit(solution)/shard_map/all_to_all | solution.py:433
  34.5 0.0 copy-done.1
  34.5 0.0 copy-done.2
  34.5 0.7 copy-done.18
  35.2 9.3 %tube.2 = (f32[2,128,512]{2,1,0:T(8,128)S(1)}, f32[2,128,512]{2,1,0:T(8,128)S(1)}, f32[2,1,512]{2,1,0:T(1,128)S(1)}, f32[2,128,128]{2,1,0:T(8,128)S(1)}) custom-call(s32[32,128]{1,0:T(8,128)S(1)} %get-tuple-element.48.refs_0_, f32[2,2]{1,0:T(2,128)S(1)} %copy-done.18, s32[256,128]{1,0:T(8,128)S(1)} %get-tuple-element.49.refs_2_, ...), custom_call_target="tpu_custom_call" | custom-call | tf_op jit(solution)/shard_map/tube/pallas_call | solution.py:416
  44.5 3.5 %collective-permute-start = (f32[2,1,512]{2,1,0:T(1,128)S(1)}, f32[2,1,512]{2,1,0:T(1,128)S(1)}, u32[]{:S(2)}, u32[]{:S(2)}) collective-permute-start(f32[2,1,512]{2,1,0:T(1,128)S(1)} %get-tuple-element.58), channel_id=1, source_target_pairs={{0,1},{1,2},{2,3},{3,4},{4,5},{5,6},{6,7},{7,8},{8,9},{9,10},{10,1... | collective-permute-start | bytes 12296 | tf_op jit(solution)/shard_map/ppermute | solution.py:478
  48.0 0.6 collective-permute-done.refs_10_.refs_11_
  48.5 0.7 copy-done.16
  49.2 0.0 copy-done.19
  49.2 0.0 copy-start.8
  49.2 0.0 copy-start.13
  49.2 5.4 %drag.2 = (f32[2,128,512]{2,1,0:T(8,128)S(1)}, f32[768,128]{1,0:T(8,128)S(1)}) custom-call(s32[8,128]{1,0:T(8,128)S(1)} %copy-done.16, f32[2]{0:T(128)S(1)} %copy-done.19, s32[1024,128]{1,0:T(8,128)S(1)} %get-tuple-element.42.refs_2_, s32[128,256]{1,0:T(8,128)S(1)} %get-tuple-element.43.refs_3_, s32[128,128]{1,0:T(8,128)S(1)} %get-tuple-element.44.refs_4_, ...), custom_call_target="tpu_custom_call" | custom-call | tf_op jit(solution)/shard_map/drag/pallas_call | solution.py:416
  54.6 0.0 copy-start
  54.6 0.0 copy-start.4
  54.6 0.0 copy-start.5
  54.6 0.0 copy-start.17
  54.7 18.6 %all_to_all.20 = f32[128,3,2,128]{3,2,1,0:T(2,128)S(1)} all-to-all(f32[128,3,2,128]{3,2,1,0:T(2,128)S(1)} %bitcast.20), channel_id=1, replica_groups=mesh['gx'=8,'gy'=16] {'gx','gy'}, dimensions={0} | all-to-all | bytes 786432 | tf_op jit(solution)/shard_map/all_to_all | solution.py:433
  73.2 0.0 copy-done.3
  73.2 0.0 copy-done.6
  73.2 0.0 copy-done.7
  73.3 0.0 copy-done.8
  73.3 0.0 copy-done.13
  73.3 0.0 copy-done
  73.3 0.6 copy-done.12
  74.0 0.0 copy-done.20
  74.0 13.7 %mid.1 = (f32[2,512,128]{2,1,0:T(8,128)S(1)}, f32[768,128]{1,0:T(8,128)S(1)}) custom-call(s32[32,128]{1,0:T(8,128)S(1)} %copy-done.12, s32[8,128]{1,0:T(8,128)S(1)} %copy-done.17, s32[256,128]{1,0:T(8,128)S(1)} %copy-done.4, s32[128,256]{1,0:T(8,128)S(1)} %copy-done.5, s32[1024,128]{1,0:T(8,128)S(1)} %copy-done.6, s32[128,256]{1,0:T(8,128)S(1)} %copy-done.7, ...), custom_call_target="tpu_custom_call" | custom-call | tf_op jit(solution)/shard_map/mid/pallas_call | solution.py:416
  87.6 16.7 %all_to_all.21 = f32[128,3,2,128]{3,2,1,0:T(2,128)S(1)} all-to-all(f32[128,3,2,128]{3,2,1,0:T(2,128)S(1)} %bitcast.19), channel_id=1, replica_groups=mesh['gx'=8,'gy'=16] {'gx','gy'}, dimensions={0} | all-to-all | bytes 786432 | tf_op jit(solution)/shard_map/all_to_all | solution.py:433
  104.3 9.3 %tube.3 = (f32[2,128,512]{2,1,0:T(8,128)S(1)}, f32[2,128,512]{2,1,0:T(8,128)S(1)}, f32[2,1,512]{2,1,0:T(1,128)S(1)}, f32[2,128,128]{2,1,0:T(8,128)S(1)}) custom-call(s32[32,128]{1,0:T(8,128)S(1)} %get-tuple-element.48.refs_0_, f32[2,2]{1,0:T(2,128)S(1)} %copy-done.18, s32[256,128]{1,0:T(8,128)S(1)} %get-tuple-element.49.refs_2_, ...), custom_call_target="tpu_custom_call" | custom-call | tf_op jit(solution)/shard_map/tube/pallas_call | solution.py:416
  113.6 3.3 %collective-permute-start.1 = (f32[2,1,512]{2,1,0:T(1,128)S(1)}, f32[2,1,512]{2,1,0:T(1,128)S(1)}, u32[]{:S(2)}, u32[]{:S(2)}) collective-permute-start(f32[2,1,512]{2,1,0:T(1,128)S(1)} %get-tuple-element.65), channel_id=1, source_target_pairs={{0,1},{1,2},{2,3},{3,4},{4,5},{5,6},{6,7},{7,8},{8,9},{9,10},{10,1... | collective-permute-start | bytes 12296 | tf_op jit(solution)/shard_map/ppermute | solution.py:478
  116.9 0.7 collective-permute-done.1.refs_10_
  117.7 6.2 %drag.3 = (f32[2,128,512]{2,1,0:T(8,128)}, f32[768,128]{1,0:T(8,128)S(1)}) custom-call(s32[8,128]{1,0:T(8,128)S(1)} %copy-done.16, f32[2]{0:T(128)S(1)} %copy-done.19, s32[1024,128]{1,0:T(8,128)S(1)} %get-tuple-element.42.refs_2_, s32[128,256]{1,0:T(8,128)S(1)} %get-tuple-element.43.refs_3_, s32[128,128]{1,0:T(8,128)S(1)} %get-tuple-element.44.refs_4_, ...), custom_call_target="tpu_custom_call" | custom-call | tf_op jit(solution)/shard_map/drag/pallas_call | solution.py:416
  123.8 18.6 %all_to_all.22 = f32[128,3,2,128]{3,2,1,0:T(2,128)S(1)} all-to-all(f32[128,3,2,128]{3,2,1,0:T(2,128)S(1)} %bitcast.18), channel_id=1, replica_groups=mesh['gx'=8,'gy'=16] {'gx','gy'}, dimensions={0} | all-to-all | bytes 786432 | tf_op jit(solution)/shard_map/all_to_all | solution.py:433
  142.4 9.8 %end.1 = f32[2,16,32,128]{3,2,1,0:T(8,128)} custom-call(s32[32,128]{1,0:T(8,128)S(1)} %copy-done.12, s32[256,128]{1,0:T(8,128)S(1)} %copy-done.4, s32[128,256]{1,0:T(8,128)S(1)} %copy-done.5, f32[768,128]{1,0:T(8,128)S(1)} %bitcast.13, f32[2,16,32,128]{3,2,1,0:T(8,128)S(1)} %copy-done, f32[2,16,32,128]{3,2,1,0:T(8,128)S(1)} %bitcast.17, ...), custom_call_target="tpu_custom_call" | custom-call | tf_op jit(solution)/shard_map/end/pallas_call | solution.py:416
  (13 shorter events, 0.0 us)
Async XLA Ops:
  0.6 33.8 %copy-start.1 = (bf16[1,2,512,512]{3,2,1,0:T(8,128)(2,1)S(1)}, bf16[1,2,512,512]{3,2,1,0:T(8,128)(2,1)}, u32[]{:S(2)}) copy-start(bf16[1,2,512,512]{3,2,1,0:T(8,128)(2,1)} %refs_8_.3) | copy-start | bytes 3145732
  0.6 21.9 %copy-start.9 = (s32[1,128,256]{2,1,0:T(8,128)S(1)}, s32[1,128,256]{2,1,0:T(8,128)}, u32[]{:S(2)}) copy-start(s32[1,128,256]{2,1,0:T(8,128)} %refs_0_.2) | copy-start | bytes 393220
  0.7 21.9 %copy-start.10 = (s32[1,128,256]{2,1,0:T(8,128)S(1)}, s32[1,128,256]{2,1,0:T(8,128)}, u32[]{:S(2)}) copy-start(s32[1,128,256]{2,1,0:T(8,128)} %refs_1_.7) | copy-start | bytes 393220
  11.0 23.5 %copy-start.2 = (f32[2,128,512]{2,1,0:T(8,128)S(1)}, f32[2,128,512]{2,1,0:T(8,128)}, u32[]{:S(2)}) copy-start(f32[2,128,512]{2,1,0:T(8,128)} %refs_11_.1) | copy-start | bytes 1572868
  11.0 23.4 %all-to-all-start = ((f32[128,3,2,128]{3,2,1,0:T(2,128)}), f32[128,3,2,128]{3,2,1,0:T(2,128)S(1)}, u32[]{:S(2)}, u32[]{:S(2)}) async-start(f32[128,3,2,128]{3,2,1,0:T(2,128)} %bitcast.24), calls=%async_computation | async-start | bytes 786432 | tf_op jit(solution)/shard_map/all_to_all | solution.py:433
  22.6 0.9 copy-start.11
  23.5 0.8 copy-start.14
  24.3 0.7 copy-start.21
  28.4 0.6 copy-start.15
  34.5 0.7 copy-start.18
  44.5 4.1 %collective-permute-start = (f32[2,1,512]{2,1,0:T(1,128)S(1)}, f32[2,1,512]{2,1,0:T(1,128)S(1)}, u32[]{:S(2)}, u32[]{:S(2)}) collective-permute-start(f32[2,1,512]{2,1,0:T(1,128)S(1)} %get-tuple-element.58), channel_id=1, source_target_pairs={{0,1},{1,2},{2,3},{3,4},{4,5},{5,6},{6,7},{7,8},{8,9},{9,10},{10,1... | collective-permute-start | bytes 12296 | tf_op jit(solution)/shard_map/ppermute | solution.py:478
  48.5 0.7 copy-start.16
  48.5 0.7 copy-start.19
  49.2 24.0 %copy-start.3 = (f32[2,16,32,128]{3,2,1,0:T(8,128)S(1)}, f32[2,16,32,128]{3,2,1,0:T(8,128)}, u32[]{:S(2)}) copy-start(f32[2,16,32,128]{3,2,1,0:T(8,128)} %refs_6_.1) | copy-start | bytes 1572868
  49.2 24.0 %copy-start.6 = (s32[1024,128]{1,0:T(8,128)S(1)}, s32[1024,128]{1,0:T(8,128)}, u32[]{:S(2)}) copy-start(s32[1024,128]{1,0:T(8,128)} %get-tuple-element.52.refs_4_) | copy-start | bytes 1572868
  49.2 24.0 %copy-start.7 = (s32[128,256]{1,0:T(8,128)S(1)}, s32[128,256]{1,0:T(8,128)}, u32[]{:S(2)}) copy-start(s32[128,256]{1,0:T(8,128)} %get-tuple-element.53.refs_5_) | copy-start | bytes 393220
  49.2 24.0 %copy-start.8 = (s32[128,256]{1,0:T(8,128)S(1)}, s32[128,256]{1,0:T(8,128)}, u32[]{:S(2)}) copy-start(s32[128,256]{1,0:T(8,128)} %get-tuple-element.55.refs_7_) | copy-start | bytes 393220
  49.2 24.0 %copy-start.13 = (s32[128,128]{1,0:T(8,128)S(1)}, s32[128,128]{1,0:T(8,128)}, u32[]{:S(2)}) copy-start(s32[128,128]{1,0:T(8,128)} %get-tuple-element.54.refs_6_) | copy-start | bytes 196612
  54.6 18.7 %copy-start = (f32[2,16,32,128]{3,2,1,0:T(8,128)S(1)}, f32[2,16,32,128]{3,2,1,0:T(8,128)}, u32[]{:S(2)}) copy-start(f32[2,16,32,128]{3,2,1,0:T(8,128)} %refs_4_.1) | copy-start | bytes 1572868
  54.6 18.7 %copy-start.4 = (s32[256,128]{1,0:T(8,128)S(1)}, s32[256,128]{1,0:T(8,128)}, u32[]{:S(2)}) copy-start(s32[256,128]{1,0:T(8,128)} %get-tuple-element.37.refs_2_.refs_1_) | copy-start | bytes 393220
  54.6 18.7 %copy-start.5 = (s32[128,256]{1,0:T(8,128)S(1)}, s32[128,256]{1,0:T(8,128)}, u32[]{:S(2)}) copy-start(s32[128,256]{1,0:T(8,128)} %get-tuple-element.38.refs_3_.refs_2_) | copy-start | bytes 393220
  54.6 18.7 %copy-start.17 = (s32[8,128]{1,0:T(8,128)S(1)}, s32[8,128]{1,0:T(8,128)}, u32[]{:S(2)}) copy-start(s32[8,128]{1,0:T(8,128)} %get-tuple-element.51.refs_1_) | copy-start | bytes 12292
  73.2 0.7 copy-start.12
  73.2 0.7 copy-start.20
  113.6 4.1 %collective-permute-start.1 = (f32[2,1,512]{2,1,0:T(1,128)S(1)}, f32[2,1,512]{2,1,0:T(1,128)S(1)}, u32[]{:S(2)}, u32[]{:S(2)}) collective-permute-start(f32[2,1,512]{2,1,0:T(1,128)S(1)} %get-tuple-element.65), channel_id=1, source_target_pairs={{0,1},{1,2},{2,3},{3,4},{4,5},{5,6},{6,7},{7,8},{8,9},{9,10},{10,1... | collective-permute-start | bytes 12296 | tf_op jit(solution)/shard_map/ppermute | solution.py:478

commit v11 on v10

--- a/solution.py
+++ b/solution.py
@@ -8,7 +8,7 @@
 i32, f32, bf16 = jnp.int32, jnp.float32, jnp.bfloat16
 VM = pl.BlockSpec(memory_space=pltpu.VMEM)
 SM = pl.BlockSpec(memory_space=pltpu.SMEM)
-W, NB, UN, GB = 80, 16, 2, 16
+W, NB, UN, GB = 72, 16, 4, 16
 LIMITS = {"first": None, "tubesort": 24, "tube0": 24, "drag0": 24, "mid": 24, "tube1": 24, "drag1": 24, "end": 24}
 neutral_step = 0.4
 ion_factor = 0.5

time: 153 us -> 147 us (0.961)
  Pallas kernels: 67.3 us -> 61.8 us
    pallas_call x8, Pallas kernels: 67.3 us -> 61.8 us  [call(): pl.pallas_call(body, out_shape=outs, in_specs=[pl.BlockSpec(memory_space=...]
where the time goes in v11:
time: 147 us
  Pallas kernels  61.8 us (42%)
  blocking collectives  53.6 us (36%)
  starting transfers between devices  18.5 us (13%)
  waiting for transfers between devices  6.58 us (4%)
  local copies, waits for them, and re-layouts  5.03 us (3%)
    pallas_call x8, Pallas kernels, call(): pl.pallas_call(body, out_shape=outs, in_specs=[pl.BlockSpec(memory_space=...  61.8 us
    all_to_all x3, blocking collectives, exchange(): lax.all_to_all(x, ('gx', 'gy'), split_axis=0, concat_axis=0, tiled=True)  53.6 us
    all_to_all x1, starting transfers between devices, exchange(): lax.all_to_all(x, ('gx', 'gy'), split_axis=0, concat_axis=0, tiled=True)  11.5 us
    ppermute x2, starting transfers between devices, tubes(): up = lax.ppermute(out_last, 'gy', up_route)  7.05 us
    all_to_all x1, waiting for transfers between devices, exchange(): lax.all_to_all(x, ('gx', 'gy'), split_axis=0, concat_axis=0, tiled=True)  5.51 us
    unnamed x44, local copies, waits for them, and re-layouts  5.03 us
  transfers between devices with their start and end apart: 3, of which 3 were waited for; matrix products, arithmetic and copies ran while one was open for 0% of the time, Pallas kernels for 2%

profile of v11, /device:TPU:1, one launch (start us, length us, event | category | flops | bytes accessed | tf_op | source)
XLA Modules:
  0.0 146.6 jit_solution(13586491906015871653)
XLA Ops:
  0.6 0.0 copy-start.1
  0.6 0.0 copy-start.9
  0.7 0.0 copy-start.10
  0.7 10.4 %first.1 = (s32[256,128]{1,0:T(8,128)}, s32[128,256]{1,0:T(8,128)}, s32[32,128]{1,0:T(8,128)}, s32[1024,128]{1,0:T(8,128)}, s32[128,256]{1,0:T(8,128)}, /*index=...) custom-call(s32[1,128,256]{2,1,0:T(8,128)} %refs_0_.1, s32[1,128,256]{2,1,0:T(8,128)} %refs_1_.6, ...), custom_call_target="tpu_custom_call" | custom-call | tf_op jit(solution)/shard_map/first/pallas_call | solution.py:416
  11.0 0.0 copy-start.2
  11.0 11.5 %all-to-all-start = ((f32[128,3,2,128]{3,2,1,0:T(2,128)}), f32[128,3,2,128]{3,2,1,0:T(2,128)S(1)}, u32[]{:S(2)}, u32[]{:S(2)}) async-start(f32[128,3,2,128]{3,2,1,0:T(2,128)} %bitcast.24), calls=%async_computation | async-start | bytes 786432 | tf_op jit(solution)/shard_map/all_to_all | solution.py:433
  22.5 0.0 copy-done.9
  22.5 0.0 copy-done.10
  22.6 0.0 copy-start.11
  22.6 0.9 copy-done.11
  23.5 0.8 copy-done.14
  24.3 0.7 copy-done.21
  25.0 3.4 %tubesort.1 = (s32[256,128]{1,0:T(8,128)S(1)}, s32[128,256]{1,0:T(8,128)S(1)}, s32[32,128]{1,0:T(8,128)S(1)}, s32[1024,128]{1,0:T(8,128)S(1)}, s32[128,256]{1,0:...) custom-call(s32[1,128,256]{2,1,0:T(8,128)S(1)} %copy-done.9, ...), custom_call_target="tpu_custom_call" | custom-call | tf_op jit(solution)/shard_map/tubesort/pallas_call | solution.py:416
  28.4 0.0 copy-start.15
  28.4 0.6 copy-done.15
  29.0 5.5 %all-to-all-done = f32[128,3,2,128]{3,2,1,0:T(2,128)S(1)} async-done(((f32[128,3,2,128]{3,2,1,0:T(2,128)}), f32[128,3,2,128]{3,2,1,0:T(2,128)S(1)}, u32[]{:S(2)}, u32[]{:S(2)}) %all-to-all-start) | async-done | bytes 393248 | tf_op jit(solution)/shard_map/all_to_all | solution.py:433
  34.5 0.0 copy-done.1
  34.5 0.0 copy-done.2
  34.5 0.7 copy-done.18
  35.2 7.9 %tube.2 = (f32[2,128,512]{2,1,0:T(8,128)S(1)}, f32[2,128,512]{2,1,0:T(8,128)S(1)}, f32[2,1,512]{2,1,0:T(1,128)S(1)}, f32[2,128,128]{2,1,0:T(8,128)S(1)}) custom-call(s32[32,128]{1,0:T(8,128)S(1)} %get-tuple-element.48.refs_0_, f32[2,2]{1,0:T(2,128)S(1)} %copy-done.18, s32[256,128]{1,0:T(8,128)S(1)} %get-tuple-element.49.refs_2_, ...), custom_call_target="tpu_custom_call" | custom-call | tf_op jit(solution)/shard_map/tube/pallas_call | solution.py:416
  43.1 3.5 %collective-permute-start = (f32[2,1,512]{2,1,0:T(1,128)S(1)}, f32[2,1,512]{2,1,0:T(1,128)S(1)}, u32[]{:S(2)}, u32[]{:S(2)}) collective-permute-start(f32[2,1,512]{2,1,0:T(1,128)S(1)} %get-tuple-element.58), channel_id=1, source_target_pairs={{0,1},{1,2},{2,3},{3,4},{4,5},{5,6},{6,7},{7,8},{8,9},{9,10},{10,1... | collective-permute-start | bytes 12296 | tf_op jit(solution)/shard_map/ppermute | solution.py:478
  46.6 0.6 collective-permute-done.refs_10_.refs_11_
  47.1 0.7 copy-done.16
  47.8 0.0 copy-done.19
  47.8 0.0 copy-start.8
  47.9 5.4 %drag.2 = (f32[2,128,512]{2,1,0:T(8,128)S(1)}, f32[768,128]{1,0:T(8,128)S(1)}) custom-call(s32[8,128]{1,0:T(8,128)S(1)} %copy-done.16, f32[2]{0:T(128)S(1)} %copy-done.19, s32[1024,128]{1,0:T(8,128)S(1)} %get-tuple-element.42.refs_2_, s32[128,256]{1,0:T(8,128)S(1)} %get-tuple-element.43.refs_3_, s32[128,128]{1,0:T(8,128)S(1)} %get-tuple-element.44.refs_4_, ...), custom_call_target="tpu_custom_call" | custom-call | tf_op jit(solution)/shard_map/drag/pallas_call | solution.py:416
  53.2 0.0 copy-start
  53.2 0.0 copy-start.4
  53.3 0.0 copy-start.5
  53.3 0.0 copy-start.17
  53.3 18.4 %all_to_all.20 = f32[128,3,2,128]{3,2,1,0:T(2,128)S(1)} all-to-all(f32[128,3,2,128]{3,2,1,0:T(2,128)S(1)} %bitcast.20), channel_id=1, replica_groups=mesh['gx'=8,'gy'=16] {'gx','gy'}, dimensions={0} | all-to-all | bytes 786432 | tf_op jit(solution)/shard_map/all_to_all | solution.py:433
  71.7 0.0 copy-done.3
  71.7 0.0 copy-done.7
  71.7 0.0 copy-done.8
  71.7 0.0 copy-done.13
  71.8 0.0 copy-done
  71.8 0.0 copy-done.4
  71.8 0.0 copy-done.5
  71.8 0.0 copy-done.17
  71.8 0.6 copy-done.12
  72.4 12.3 %mid.1 = (f32[2,512,128]{2,1,0:T(8,128)S(1)}, f32[768,128]{1,0:T(8,128)S(1)}) custom-call(s32[32,128]{1,0:T(8,128)S(1)} %copy-done.12, s32[8,128]{1,0:T(8,128)S(1)} %copy-done.17, s32[256,128]{1,0:T(8,128)S(1)} %copy-done.4, s32[128,256]{1,0:T(8,128)S(1)} %copy-done.5, s32[1024,128]{1,0:T(8,128)S(1)} %copy-done.6, s32[128,256]{1,0:T(8,128)S(1)} %copy-done.7, ...), custom_call_target="tpu_custom_call" | custom-call | tf_op jit(solution)/shard_map/mid/pallas_call | solution.py:416
  84.7 16.7 %all_to_all.21 = f32[128,3,2,128]{3,2,1,0:T(2,128)S(1)} all-to-all(f32[128,3,2,128]{3,2,1,0:T(2,128)S(1)} %bitcast.19), channel_id=1, replica_groups=mesh['gx'=8,'gy'=16] {'gx','gy'}, dimensions={0} | all-to-all | bytes 786432 | tf_op jit(solution)/shard_map/all_to_all | solution.py:433
  101.4 7.9 %tube.3 = (f32[2,128,512]{2,1,0:T(8,128)S(1)}, f32[2,128,512]{2,1,0:T(8,128)S(1)}, f32[2,1,512]{2,1,0:T(1,128)S(1)}, f32[2,128,128]{2,1,0:T(8,128)S(1)}) custom-call(s32[32,128]{1,0:T(8,128)S(1)} %get-tuple-element.48.refs_0_, f32[2,2]{1,0:T(2,128)S(1)} %copy-done.18, s32[256,128]{1,0:T(8,128)S(1)} %get-tuple-element.49.refs_2_, ...), custom_call_target="tpu_custom_call" | custom-call | tf_op jit(solution)/shard_map/tube/pallas_call | solution.py:416
  109.3 3.5 %collective-permute-start.1 = (f32[2,1,512]{2,1,0:T(1,128)S(1)}, f32[2,1,512]{2,1,0:T(1,128)S(1)}, u32[]{:S(2)}, u32[]{:S(2)}) collective-permute-start(f32[2,1,512]{2,1,0:T(1,128)S(1)} %get-tuple-element.65), channel_id=1, source_target_pairs={{0,1},{1,2},{2,3},{3,4},{4,5},{5,6},{6,7},{7,8},{8,9},{9,10},{10,1... | collective-permute-start | bytes 12296 | tf_op jit(solution)/shard_map/ppermute | solution.py:478
  112.9 0.5 collective-permute-done.1.refs_10_
  113.4 6.2 %drag.3 = (f32[2,128,512]{2,1,0:T(8,128)}, f32[768,128]{1,0:T(8,128)S(1)}) custom-call(s32[8,128]{1,0:T(8,128)S(1)} %copy-done.16, f32[2]{0:T(128)S(1)} %copy-done.19, s32[1024,128]{1,0:T(8,128)S(1)} %get-tuple-element.42.refs_2_, s32[128,256]{1,0:T(8,128)S(1)} %get-tuple-element.43.refs_3_, s32[128,128]{1,0:T(8,128)S(1)} %get-tuple-element.44.refs_4_, ...), custom_call_target="tpu_custom_call" | custom-call | tf_op jit(solution)/shard_map/drag/pallas_call | solution.py:416
  119.6 18.5 %all_to_all.22 = f32[128,3,2,128]{3,2,1,0:T(2,128)S(1)} all-to-all(f32[128,3,2,128]{3,2,1,0:T(2,128)S(1)} %bitcast.18), channel_id=1, replica_groups=mesh['gx'=8,'gy'=16] {'gx','gy'}, dimensions={0} | all-to-all | bytes 786432 | tf_op jit(solution)/shard_map/all_to_all | solution.py:433
  138.0 8.4 %end.1 = f32[2,16,32,128]{3,2,1,0:T(8,128)} custom-call(s32[32,128]{1,0:T(8,128)S(1)} %copy-done.12, s32[256,128]{1,0:T(8,128)S(1)} %copy-done.4, s32[128,256]{1,0:T(8,128)S(1)} %copy-done.5, f32[768,128]{1,0:T(8,128)S(1)} %bitcast.13, f32[2,16,32,128]{3,2,1,0:T(8,128)S(1)} %copy-done, f32[2,16,32,128]{3,2,1,0:T(8,128)S(1)} %bitcast.17, ...), custom_call_target="tpu_custom_call" | custom-call | tf_op jit(solution)/shard_map/end/pallas_call | solution.py:416
  (13 shorter events, 0.0 us)
Async XLA Ops:
  0.6 33.8 %copy-start.1 = (bf16[1,2,512,512]{3,2,1,0:T(8,128)(2,1)S(1)}, bf16[1,2,512,512]{3,2,1,0:T(8,128)(2,1)}, u32[]{:S(2)}) copy-start(bf16[1,2,512,512]{3,2,1,0:T(8,128)(2,1)} %refs_8_.3) | copy-start | bytes 3145732
  0.6 21.9 %copy-start.9 = (s32[1,128,256]{2,1,0:T(8,128)S(1)}, s32[1,128,256]{2,1,0:T(8,128)}, u32[]{:S(2)}) copy-start(s32[1,128,256]{2,1,0:T(8,128)} %refs_0_.2) | copy-start | bytes 393220
  0.7 21.9 %copy-start.10 = (s32[1,128,256]{2,1,0:T(8,128)S(1)}, s32[1,128,256]{2,1,0:T(8,128)}, u32[]{:S(2)}) copy-start(s32[1,128,256]{2,1,0:T(8,128)} %refs_1_.7) | copy-start | bytes 393220
  11.0 23.5 %copy-start.2 = (f32[2,128,512]{2,1,0:T(8,128)S(1)}, f32[2,128,512]{2,1,0:T(8,128)}, u32[]{:S(2)}) copy-start(f32[2,128,512]{2,1,0:T(8,128)} %refs_11_.1) | copy-start | bytes 1572868
  11.0 23.4 %all-to-all-start = ((f32[128,3,2,128]{3,2,1,0:T(2,128)}), f32[128,3,2,128]{3,2,1,0:T(2,128)S(1)}, u32[]{:S(2)}, u32[]{:S(2)}) async-start(f32[128,3,2,128]{3,2,1,0:T(2,128)} %bitcast.24), calls=%async_computation | async-start | bytes 786432 | tf_op jit(solution)/shard_map/all_to_all | solution.py:433
  22.6 0.9 copy-start.11
  23.5 0.8 copy-start.14
  24.3 0.7 copy-start.21
  28.4 0.6 copy-start.15
  34.5 0.7 copy-start.18
  43.1 4.1 %collective-permute-start = (f32[2,1,512]{2,1,0:T(1,128)S(1)}, f32[2,1,512]{2,1,0:T(1,128)S(1)}, u32[]{:S(2)}, u32[]{:S(2)}) collective-permute-start(f32[2,1,512]{2,1,0:T(1,128)S(1)} %get-tuple-element.58), channel_id=1, source_target_pairs={{0,1},{1,2},{2,3},{3,4},{4,5},{5,6},{6,7},{7,8},{8,9},{9,10},{10,1... | collective-permute-start | bytes 12296 | tf_op jit(solution)/shard_map/ppermute | solution.py:478
  47.1 0.7 copy-start.16
  47.1 0.7 copy-start.19
  47.8 23.9 %copy-start.3 = (f32[2,16,32,128]{3,2,1,0:T(8,128)S(1)}, f32[2,16,32,128]{3,2,1,0:T(8,128)}, u32[]{:S(2)}) copy-start(f32[2,16,32,128]{3,2,1,0:T(8,128)} %refs_6_.1) | copy-start | bytes 1572868
  47.8 23.9 %copy-start.6 = (s32[1024,128]{1,0:T(8,128)S(1)}, s32[1024,128]{1,0:T(8,128)}, u32[]{:S(2)}) copy-start(s32[1024,128]{1,0:T(8,128)} %get-tuple-element.52.refs_4_) | copy-start | bytes 1572868
  47.8 23.9 %copy-start.7 = (s32[128,256]{1,0:T(8,128)S(1)}, s32[128,256]{1,0:T(8,128)}, u32[]{:S(2)}) copy-start(s32[128,256]{1,0:T(8,128)} %get-tuple-element.53.refs_5_) | copy-start | bytes 393220
  47.8 23.9 %copy-start.8 = (s32[128,256]{1,0:T(8,128)S(1)}, s32[128,256]{1,0:T(8,128)}, u32[]{:S(2)}) copy-start(s32[128,256]{1,0:T(8,128)} %get-tuple-element.55.refs_7_) | copy-start | bytes 393220
  47.8 23.9 %copy-start.13 = (s32[128,128]{1,0:T(8,128)S(1)}, s32[128,128]{1,0:T(8,128)}, u32[]{:S(2)}) copy-start(s32[128,128]{1,0:T(8,128)} %get-tuple-element.54.refs_6_) | copy-start | bytes 196612
  53.2 18.5 %copy-start = (f32[2,16,32,128]{3,2,1,0:T(8,128)S(1)}, f32[2,16,32,128]{3,2,1,0:T(8,128)}, u32[]{:S(2)}) copy-start(f32[2,16,32,128]{3,2,1,0:T(8,128)} %refs_4_.1) | copy-start | bytes 1572868
  53.2 18.5 %copy-start.4 = (s32[256,128]{1,0:T(8,128)S(1)}, s32[256,128]{1,0:T(8,128)}, u32[]{:S(2)}) copy-start(s32[256,128]{1,0:T(8,128)} %get-tuple-element.37.refs_2_.refs_1_) | copy-start | bytes 393220
  53.3 18.5 %copy-start.5 = (s32[128,256]{1,0:T(8,128)S(1)}, s32[128,256]{1,0:T(8,128)}, u32[]{:S(2)}) copy-start(s32[128,256]{1,0:T(8,128)} %get-tuple-element.38.refs_3_.refs_2_) | copy-start | bytes 393220
  53.3 18.5 %copy-start.17 = (s32[8,128]{1,0:T(8,128)S(1)}, s32[8,128]{1,0:T(8,128)}, u32[]{:S(2)}) copy-start(s32[8,128]{1,0:T(8,128)} %get-tuple-element.51.refs_1_) | copy-start | bytes 12292
  71.7 0.7 copy-start.12
  71.7 0.7 copy-start.20
  109.3 4.1 %collective-permute-start.1 = (f32[2,1,512]{2,1,0:T(1,128)S(1)}, f32[2,1,512]{2,1,0:T(1,128)S(1)}, u32[]{:S(2)}, u32[]{:S(2)}) collective-permute-start(f32[2,1,512]{2,1,0:T(1,128)S(1)} %get-tuple-element.65), channel_id=1, source_target_pairs={{0,1},{1,2},{2,3},{3,4},{4,5},{5,6},{6,7},{7,8},{8,9},{9,10},{10,1... | collective-permute-start | bytes 12296 | tf_op jit(solution)/shard_map/ppermute | solution.py:478

commit v12 on v11

--- a/solution.py
+++ b/solution.py
@@ -8,7 +8,7 @@
 i32, f32, bf16 = jnp.int32, jnp.float32, jnp.bfloat16
 VM = pl.BlockSpec(memory_space=pltpu.VMEM)
 SM = pl.BlockSpec(memory_space=pltpu.SMEM)
-W, NB, UN, GB = 72, 16, 4, 16
+W, NB, UN, GB = 72, 16, 8, 16
 LIMITS = {"first": None, "tubesort": 24, "tube0": 24, "drag0": 24, "mid": 24, "tube1": 24, "drag1": 24, "end": 24}
 neutral_step = 0.4
 ion_factor = 0.5

time: 147 us -> 146 us (level)
  Pallas kernels: 61.8 us -> 60.3 us
where the time goes in v12:
time: 146 us; the launch traced here: 145 us
  Pallas kernels  60.3 us (41%)
  blocking collectives  53.6 us (37%)
  starting transfers between devices  18.1 us (12%)
  waiting for transfers between devices  6.97 us (5%)
  local copies, waits for them, and re-layouts  5.03 us (3%)
    pallas_call x8, Pallas kernels, call(): pl.pallas_call(body, out_shape=outs, in_specs=[pl.BlockSpec(memory_space=...  60.3 us
    all_to_all x3, blocking collectives, exchange(): lax.all_to_all(x, ('gx', 'gy'), split_axis=0, concat_axis=0, tiled=True)  53.6 us
    all_to_all x1, starting transfers between devices, exchange(): lax.all_to_all(x, ('gx', 'gy'), split_axis=0, concat_axis=0, tiled=True)  11.5 us
    ppermute x2, starting transfers between devices, tubes(): up = lax.ppermute(out_last, 'gy', up_route)  6.65 us
    all_to_all x1, waiting for transfers between devices, exchange(): lax.all_to_all(x, ('gx', 'gy'), split_axis=0, concat_axis=0, tiled=True)  5.5 us
    unnamed x44, local copies, waits for them, and re-layouts  5.03 us
  transfers between devices with their start and end apart: 3, of which 3 were waited for; matrix products, arithmetic and copies ran while one was open for 0% of the time, Pallas kernels for 2%

profile of v12, /device:TPU:1, one launch (start us, length us, event | category | flops | bytes accessed | tf_op | source)
XLA Modules:
  0.0 145.2 jit_solution(12693315608586475468)
XLA Ops:
  0.6 0.0 copy-start.1
  0.6 0.0 copy-start.9
  0.7 0.0 copy-start.10
  0.7 10.4 %first.1 = (s32[256,128]{1,0:T(8,128)}, s32[128,256]{1,0:T(8,128)}, s32[32,128]{1,0:T(8,128)}, s32[1024,128]{1,0:T(8,128)}, s32[128,256]{1,0:T(8,128)}, /*index=...) custom-call(s32[1,128,256]{2,1,0:T(8,128)} %refs_0_.1, s32[1,128,256]{2,1,0:T(8,128)} %refs_1_.6, ...), custom_call_target="tpu_custom_call" | custom-call | tf_op jit(solution)/shard_map/first/pallas_call | solution.py:416
  11.0 0.0 copy-start.2
  11.0 11.5 %all-to-all-start = ((f32[128,3,2,128]{3,2,1,0:T(2,128)}), f32[128,3,2,128]{3,2,1,0:T(2,128)S(1)}, u32[]{:S(2)}, u32[]{:S(2)}) async-start(f32[128,3,2,128]{3,2,1,0:T(2,128)} %bitcast.24), calls=%async_computation | async-start | bytes 786432 | tf_op jit(solution)/shard_map/all_to_all | solution.py:433
  22.5 0.0 copy-done.9
  22.6 0.0 copy-done.10
  22.6 0.0 copy-start.11
  22.6 0.9 copy-done.11
  23.5 0.8 copy-done.14
  24.3 0.7 copy-done.21
  25.0 3.4 %tubesort.1 = (s32[256,128]{1,0:T(8,128)S(1)}, s32[128,256]{1,0:T(8,128)S(1)}, s32[32,128]{1,0:T(8,128)S(1)}, s32[1024,128]{1,0:T(8,128)S(1)}, s32[128,256]{1,0:...) custom-call(s32[1,128,256]{2,1,0:T(8,128)S(1)} %copy-done.9, ...), custom_call_target="tpu_custom_call" | custom-call | tf_op jit(solution)/shard_map/tubesort/pallas_call | solution.py:416
  28.4 0.0 copy-start.15
  28.4 0.6 copy-done.15
  29.0 5.5 %all-to-all-done = f32[128,3,2,128]{3,2,1,0:T(2,128)S(1)} async-done(((f32[128,3,2,128]{3,2,1,0:T(2,128)}), f32[128,3,2,128]{3,2,1,0:T(2,128)S(1)}, u32[]{:S(2)}, u32[]{:S(2)}) %all-to-all-start) | async-done | bytes 393248 | tf_op jit(solution)/shard_map/all_to_all | solution.py:433
  34.5 0.0 copy-done.1
  34.5 0.0 copy-done.2
  34.5 0.7 copy-done.18
  35.2 7.5 %tube.2 = (f32[2,128,512]{2,1,0:T(8,128)S(1)}, f32[2,128,512]{2,1,0:T(8,128)S(1)}, f32[2,1,512]{2,1,0:T(1,128)S(1)}, f32[2,128,128]{2,1,0:T(8,128)S(1)}) custom-call(s32[32,128]{1,0:T(8,128)S(1)} %get-tuple-element.48.refs_0_, f32[2,2]{1,0:T(2,128)S(1)} %copy-done.18, s32[256,128]{1,0:T(8,128)S(1)} %get-tuple-element.49.refs_2_, ...), custom_call_target="tpu_custom_call" | custom-call | tf_op jit(solution)/shard_map/tube/pallas_call | solution.py:416
  42.7 3.3 %collective-permute-start = (f32[2,1,512]{2,1,0:T(1,128)S(1)}, f32[2,1,512]{2,1,0:T(1,128)S(1)}, u32[]{:S(2)}, u32[]{:S(2)}) collective-permute-start(f32[2,1,512]{2,1,0:T(1,128)S(1)} %get-tuple-element.58), channel_id=1, source_target_pairs={{0,1},{1,2},{2,3},{3,4},{4,5},{5,6},{6,7},{7,8},{8,9},{9,10},{10,1... | collective-permute-start | bytes 12296 | tf_op jit(solution)/shard_map/ppermute | solution.py:478
  46.0 0.7 collective-permute-done.refs_10_.refs_11_
  46.7 0.7 copy-done.16
  47.4 0.0 copy-done.19
  47.4 0.0 copy-start.8
  47.4 0.0 copy-start.13
  47.4 5.4 %drag.2 = (f32[2,128,512]{2,1,0:T(8,128)S(1)}, f32[768,128]{1,0:T(8,128)S(1)}) custom-call(s32[8,128]{1,0:T(8,128)S(1)} %copy-done.16, f32[2]{0:T(128)S(1)} %copy-done.19, s32[1024,128]{1,0:T(8,128)S(1)} %get-tuple-element.42.refs_2_, s32[128,256]{1,0:T(8,128)S(1)} %get-tuple-element.43.refs_3_, s32[128,128]{1,0:T(8,128)S(1)} %get-tuple-element.44.refs_4_, ...), custom_call_target="tpu_custom_call" | custom-call | tf_op jit(solution)/shard_map/drag/pallas_call | solution.py:416
  52.8 0.0 copy-start
  52.8 0.0 copy-start.4
  52.8 0.0 copy-start.5
  52.8 0.0 copy-start.17
  52.9 18.4 %all_to_all.20 = f32[128,3,2,128]{3,2,1,0:T(2,128)S(1)} all-to-all(f32[128,3,2,128]{3,2,1,0:T(2,128)S(1)} %bitcast.20), channel_id=1, replica_groups=mesh['gx'=8,'gy'=16] {'gx','gy'}, dimensions={0} | all-to-all | bytes 786432 | tf_op jit(solution)/shard_map/all_to_all | solution.py:433
  71.3 0.0 copy-done.3
  71.3 0.0 copy-done.6
  71.3 0.0 copy-done.7
  71.3 0.0 copy-done.8
  71.3 0.0 copy-done.13
  71.3 0.0 copy-done
  71.4 0.6 copy-done.12
  72.0 0.0 copy-done.20
  72.0 11.8 %mid.1 = (f32[2,512,128]{2,1,0:T(8,128)S(1)}, f32[768,128]{1,0:T(8,128)S(1)}) custom-call(s32[32,128]{1,0:T(8,128)S(1)} %copy-done.12, s32[8,128]{1,0:T(8,128)S(1)} %copy-done.17, s32[256,128]{1,0:T(8,128)S(1)} %copy-done.4, s32[128,256]{1,0:T(8,128)S(1)} %copy-done.5, s32[1024,128]{1,0:T(8,128)S(1)} %copy-done.6, s32[128,256]{1,0:T(8,128)S(1)} %copy-done.7, ...), custom_call_target="tpu_custom_call" | custom-call | tf_op jit(solution)/shard_map/mid/pallas_call | solution.py:416
  83.9 16.7 %all_to_all.21 = f32[128,3,2,128]{3,2,1,0:T(2,128)S(1)} all-to-all(f32[128,3,2,128]{3,2,1,0:T(2,128)S(1)} %bitcast.19), channel_id=1, replica_groups=mesh['gx'=8,'gy'=16] {'gx','gy'}, dimensions={0} | all-to-all | bytes 786432 | tf_op jit(solution)/shard_map/all_to_all | solution.py:433
  100.6 7.5 %tube.3 = (f32[2,128,512]{2,1,0:T(8,128)S(1)}, f32[2,128,512]{2,1,0:T(8,128)S(1)}, f32[2,1,512]{2,1,0:T(1,128)S(1)}, f32[2,128,128]{2,1,0:T(8,128)S(1)}) custom-call(s32[32,128]{1,0:T(8,128)S(1)} %get-tuple-element.48.refs_0_, f32[2,2]{1,0:T(2,128)S(1)} %copy-done.18, s32[256,128]{1,0:T(8,128)S(1)} %get-tuple-element.49.refs_2_, ...), custom_call_target="tpu_custom_call" | custom-call | tf_op jit(solution)/shard_map/tube/pallas_call | solution.py:416
  108.1 3.3 %collective-permute-start.1 = (f32[2,1,512]{2,1,0:T(1,128)S(1)}, f32[2,1,512]{2,1,0:T(1,128)S(1)}, u32[]{:S(2)}, u32[]{:S(2)}) collective-permute-start(f32[2,1,512]{2,1,0:T(1,128)S(1)} %get-tuple-element.65), channel_id=1, source_target_pairs={{0,1},{1,2},{2,3},{3,4},{4,5},{5,6},{6,7},{7,8},{8,9},{9,10},{10,1... | collective-permute-start | bytes 12296 | tf_op jit(solution)/shard_map/ppermute | solution.py:478
  111.4 0.7 collective-permute-done.1.refs_10_
  112.1 6.4 %drag.3 = (f32[2,128,512]{2,1,0:T(8,128)}, f32[768,128]{1,0:T(8,128)S(1)}) custom-call(s32[8,128]{1,0:T(8,128)S(1)} %copy-done.16, f32[2]{0:T(128)S(1)} %copy-done.19, s32[1024,128]{1,0:T(8,128)S(1)} %get-tuple-element.42.refs_2_, s32[128,256]{1,0:T(8,128)S(1)} %get-tuple-element.43.refs_3_, s32[128,128]{1,0:T(8,128)S(1)} %get-tuple-element.44.refs_4_, ...), custom_call_target="tpu_custom_call" | custom-call | tf_op jit(solution)/shard_map/drag/pallas_call | solution.py:416
  118.6 18.4 %all_to_all.22 = f32[128,3,2,128]{3,2,1,0:T(2,128)S(1)} all-to-all(f32[128,3,2,128]{3,2,1,0:T(2,128)S(1)} %bitcast.18), channel_id=1, replica_groups=mesh['gx'=8,'gy'=16] {'gx','gy'}, dimensions={0} | all-to-all | bytes 786432 | tf_op jit(solution)/shard_map/all_to_all | solution.py:433
  137.0 8.0 %end.1 = f32[2,16,32,128]{3,2,1,0:T(8,128)} custom-call(s32[32,128]{1,0:T(8,128)S(1)} %copy-done.12, s32[256,128]{1,0:T(8,128)S(1)} %copy-done.4, s32[128,256]{1,0:T(8,128)S(1)} %copy-done.5, f32[768,128]{1,0:T(8,128)S(1)} %bitcast.13, f32[2,16,32,128]{3,2,1,0:T(8,128)S(1)} %copy-done, f32[2,16,32,128]{3,2,1,0:T(8,128)S(1)} %bitcast.17, ...), custom_call_target="tpu_custom_call" | custom-call | tf_op jit(solution)/shard_map/end/pallas_call | solution.py:416
  (13 shorter events, 0.0 us)
Async XLA Ops:
  0.6 33.8 %copy-start.1 = (bf16[1,2,512,512]{3,2,1,0:T(8,128)(2,1)S(1)}, bf16[1,2,512,512]{3,2,1,0:T(8,128)(2,1)}, u32[]{:S(2)}) copy-start(bf16[1,2,512,512]{3,2,1,0:T(8,128)(2,1)} %refs_8_.3) | copy-start | bytes 3145732
  0.6 21.9 %copy-start.9 = (s32[1,128,256]{2,1,0:T(8,128)S(1)}, s32[1,128,256]{2,1,0:T(8,128)}, u32[]{:S(2)}) copy-start(s32[1,128,256]{2,1,0:T(8,128)} %refs_0_.2) | copy-start | bytes 393220
  0.7 21.9 %copy-start.10 = (s32[1,128,256]{2,1,0:T(8,128)S(1)}, s32[1,128,256]{2,1,0:T(8,128)}, u32[]{:S(2)}) copy-start(s32[1,128,256]{2,1,0:T(8,128)} %refs_1_.7) | copy-start | bytes 393220
  11.0 23.5 %copy-start.2 = (f32[2,128,512]{2,1,0:T(8,128)S(1)}, f32[2,128,512]{2,1,0:T(8,128)}, u32[]{:S(2)}) copy-start(f32[2,128,512]{2,1,0:T(8,128)} %refs_11_.1) | copy-start | bytes 1572868
  11.0 23.4 %all-to-all-start = ((f32[128,3,2,128]{3,2,1,0:T(2,128)}), f32[128,3,2,128]{3,2,1,0:T(2,128)S(1)}, u32[]{:S(2)}, u32[]{:S(2)}) async-start(f32[128,3,2,128]{3,2,1,0:T(2,128)} %bitcast.24), calls=%async_computation | async-start | bytes 786432 | tf_op jit(solution)/shard_map/all_to_all | solution.py:433
  22.6 0.9 copy-start.11
  23.5 0.8 copy-start.14
  24.3 0.7 copy-start.21
  28.4 0.6 copy-start.15
  34.5 0.7 copy-start.18
  42.7 4.1 %collective-permute-start = (f32[2,1,512]{2,1,0:T(1,128)S(1)}, f32[2,1,512]{2,1,0:T(1,128)S(1)}, u32[]{:S(2)}, u32[]{:S(2)}) collective-permute-start(f32[2,1,512]{2,1,0:T(1,128)S(1)} %get-tuple-element.58), channel_id=1, source_target_pairs={{0,1},{1,2},{2,3},{3,4},{4,5},{5,6},{6,7},{7,8},{8,9},{9,10},{10,1... | collective-permute-start | bytes 12296 | tf_op jit(solution)/shard_map/ppermute | solution.py:478
  46.7 0.7 copy-start.16
  46.7 0.7 copy-start.19
  47.4 23.9 %copy-start.3 = (f32[2,16,32,128]{3,2,1,0:T(8,128)S(1)}, f32[2,16,32,128]{3,2,1,0:T(8,128)}, u32[]{:S(2)}) copy-start(f32[2,16,32,128]{3,2,1,0:T(8,128)} %refs_6_.1) | copy-start | bytes 1572868
  47.4 23.9 %copy-start.6 = (s32[1024,128]{1,0:T(8,128)S(1)}, s32[1024,128]{1,0:T(8,128)}, u32[]{:S(2)}) copy-start(s32[1024,128]{1,0:T(8,128)} %get-tuple-element.52.refs_4_) | copy-start | bytes 1572868
  47.4 23.9 %copy-start.7 = (s32[128,256]{1,0:T(8,128)S(1)}, s32[128,256]{1,0:T(8,128)}, u32[]{:S(2)}) copy-start(s32[128,256]{1,0:T(8,128)} %get-tuple-element.53.refs_5_) | copy-start | bytes 393220
  47.4 23.9 %copy-start.8 = (s32[128,256]{1,0:T(8,128)S(1)}, s32[128,256]{1,0:T(8,128)}, u32[]{:S(2)}) copy-start(s32[128,256]{1,0:T(8,128)} %get-tuple-element.55.refs_7_) | copy-start | bytes 393220
  47.4 23.9 %copy-start.13 = (s32[128,128]{1,0:T(8,128)S(1)}, s32[128,128]{1,0:T(8,128)}, u32[]{:S(2)}) copy-start(s32[128,128]{1,0:T(8,128)} %get-tuple-element.54.refs_6_) | copy-start | bytes 196612
  52.8 18.5 %copy-start = (f32[2,16,32,128]{3,2,1,0:T(8,128)S(1)}, f32[2,16,32,128]{3,2,1,0:T(8,128)}, u32[]{:S(2)}) copy-start(f32[2,16,32,128]{3,2,1,0:T(8,128)} %refs_4_.1) | copy-start | bytes 1572868
  52.8 18.5 %copy-start.4 = (s32[256,128]{1,0:T(8,128)S(1)}, s32[256,128]{1,0:T(8,128)}, u32[]{:S(2)}) copy-start(s32[256,128]{1,0:T(8,128)} %get-tuple-element.37.refs_2_.refs_1_) | copy-start | bytes 393220
  52.8 18.5 %copy-start.5 = (s32[128,256]{1,0:T(8,128)S(1)}, s32[128,256]{1,0:T(8,128)}, u32[]{:S(2)}) copy-start(s32[128,256]{1,0:T(8,128)} %get-tuple-element.38.refs_3_.refs_2_) | copy-start | bytes 393220
  52.8 18.5 %copy-start.17 = (s32[8,128]{1,0:T(8,128)S(1)}, s32[8,128]{1,0:T(8,128)}, u32[]{:S(2)}) copy-start(s32[8,128]{1,0:T(8,128)} %get-tuple-element.51.refs_1_) | copy-start | bytes 12292
  71.3 0.7 copy-start.12
  71.3 0.7 copy-start.20
  108.1 4.1 %collective-permute-start.1 = (f32[2,1,512]{2,1,0:T(1,128)S(1)}, f32[2,1,512]{2,1,0:T(1,128)S(1)}, u32[]{:S(2)}, u32[]{:S(2)}) collective-permute-start(f32[2,1,512]{2,1,0:T(1,128)S(1)} %get-tuple-element.65), channel_id=1, source_target_pairs={{0,1},{1,2},{2,3},{3,4},{4,5},{5,6},{6,7},{7,8},{8,9},{9,10},{10,1... | collective-permute-start | bytes 12296 | tf_op jit(solution)/shard_map/ppermute | solution.py:478
